TPU v7x, 32 devices: a whole 2x2x4 slice. The times are simulated.
32 devices in a mesh: dp: 8 (over z, y), tensor: 4 (over x, core).
Axes of the slice: x: 2, y: 2, z: 4, core: 2. Of those that a mesh axis runs over, the one named last changes fastest.
Arguments:
- tokens: bfloat16 [3, 4096, 1536], P(None, ('dp', 'tensor')), may hold values from -6 to 6
- lengths: int32 [3, 32, 6], P(None, ('dp', 'tensor')), may hold values from 1 to 64, 128 in all within a row
- first_gain: bfloat16 [1536], P(('dp', 'tensor')), may hold values from 0.099609375 to 1.8984375
- query_weight: bfloat16 [1536, 1536], P(('dp', 'tensor')), may hold values from -0.15625 to 0.15625
- key_weight: bfloat16 [1536, 768], P(('dp', 'tensor')), may hold values from -0.15625 to 0.15625
- value_weight: bfloat16 [1536, 768], P(('dp', 'tensor')), may hold values from -0.15625 to 0.15625
- output_weight: bfloat16 [1536, 1536], P(('dp', 'tensor')), may hold values from -0.4375 to 0.4375
- second_gain: bfloat16 [1536], P(('dp', 'tensor')), may hold values from 0.099609375 to 1.8984375
- gate_weight: bfloat16 [1536, 4096], P('dp', 'tensor'), may hold values from -0.15625 to 0.15625
- up_weight: bfloat16 [1536, 4096], P('dp', 'tensor'), may hold values from -0.15625 to 0.15625
- down_weight: bfloat16 [4096, 1536], P('tensor', 'dp'), may hold values from -0.09375 to 0.09375
- cotangent: bfloat16 [3, 4096, 1536], P(None, ('dp', 'tensor')), may hold values from -6 to 6
Outputs:
- layer_out: bfloat16 [3, 4096, 1536], P(None, ('dp', 'tensor'))
- input_grad: float32 [3, 4096, 1536], P(None, ('dp', 'tensor'))
- first_gain_grad: float32 [1536], P(('dp', 'tensor'))
- query_grad: float32 [1536, 1536], P(('dp', 'tensor'))
- key_grad: float32 [1536, 768], P(('dp', 'tensor'))
- value_grad: float32 [1536, 768], P(('dp', 'tensor'))
- output_grad: float32 [1536, 1536], P(('dp', 'tensor'))
- second_gain_grad: float32 [1536], P(('dp', 'tensor'))
- gate_grad: float32 [1536, 4096], P('dp', 'tensor')
- up_grad: float32 [1536, 4096], P('dp', 'tensor')
- down_grad: float32 [4096, 1536], P('tensor', 'dp')
Inputs may be any that keep to these rules, and one draw needn't show every extreme that they name: Row lengths[m, p] splits the 128 rows of pack p of micro-batch m into 6 runs in order, summing to 128; the first 5 runs are sequences, the last is padding; no run is longer than 64 rows.
All inputs are finite; a program needn't handle non-finite values.
Results may differ from a plain program's by a relative error of at most 0.013.
Values may be sent and summed in bfloat16 or wider, within the bound.
No kernel may reach another device: no remote copies, remote signals or barrier semaphores. Data moves between devices by JAX's collectives and lax.ppermute only.
A program may use at most 192 MiB of HBM per device.

v0:
```python
import math

import jax
import jax.numpy as jnp
from jax import lax
from jax.sharding import PartitionSpec as P

HEADS = 16
KV_HEADS = 8
HEAD = 96
SLOTS = 6


EPSILON = 1e-05
ROPE_BASE = 100000.0
NEG_LARGE = -1e30


def pack_layout(seq_lengths, row_count):
    seq_ends = jnp.cumsum(seq_lengths)
    seq_starts = seq_ends - seq_lengths
    row_index = jnp.arange(row_count, dtype=jnp.int32)
    segment = jnp.sum((row_index[:, None] >= seq_ends[None, :]).astype(jnp.int32), axis=1)
    owner_hot = segment[:, None] == jnp.arange(seq_lengths.shape[0], dtype=jnp.int32)[None, :]
    position = row_index - jnp.sum(jnp.where(owner_hot, seq_starts[None, :], 0), axis=1)
    return (segment, position)


def rotary_tables(position, head_size):
    half_size = head_size // 2
    freq_index = jnp.arange(half_size, dtype=jnp.float32)
    inverse = jnp.exp(freq_index * (-2.0 / head_size) * math.log(ROPE_BASE))
    angles = position.astype(jnp.float32)[:, None] * inverse[None, :]
    return (jnp.cos(angles), jnp.sin(angles))


def rotate(vectors, cosine, sine_part):
    half_size = vectors.shape[-1] // 2
    lower_half = vectors[..., :half_size]
    upper_half = vectors[..., half_size:]
    cosine = cosine[:, None, :]
    sine_part = sine_part[:, None, :]
    return jnp.concatenate(
        [
            lower_half * cosine - upper_half * sine_part,
            upper_half * cosine + lower_half * sine_part,
        ],
        axis=-1,
    )


def unrotate(vectors, cosine, sine_part):
    half_size = vectors.shape[-1] // 2
    lower_half = vectors[..., :half_size]
    upper_half = vectors[..., half_size:]
    cosine = cosine[:, None, :]
    sine_part = sine_part[:, None, :]
    return jnp.concatenate(
        [
            lower_half * cosine + upper_half * sine_part,
            upper_half * cosine - lower_half * sine_part,
        ],
        axis=-1,
    )


def visible(segment, row_valid):
    row_index = jnp.arange(segment.shape[0], dtype=jnp.int32)
    same_seq = segment[:, None] == segment[None, :]
    return same_seq & (row_index[None, :] <= row_index[:, None]) & row_valid[:, None]


def product(left_side, right_side):
    return jnp.dot(left_side, right_side, preferred_element_type=jnp.float32)


def across(left_side, right_side):
    return lax.dot_general(
        left_side, right_side, (((0,), (0,)), ((), ())), preferred_element_type=jnp.float32
    )


def against(left_side, right_side):
    return lax.dot_general(
        left_side, right_side, (((1,), (1,)), ((), ())), preferred_element_type=jnp.float32
    )


def norm_back(upstream, signal, inverse, gain_vec):
    weighted = upstream * gain_vec
    gain_part = jnp.sum(upstream * signal * inverse, axis=0)
    signal_part = inverse * weighted - signal * (inverse * inverse * inverse) * jnp.mean(
        weighted * signal, axis=1, keepdims=True
    )
    return (signal_part, gain_part)


def fetch_attention(first_gain, query_weight, key_weight, value_weight, output_weight, second_gain):
    return (
        lax.all_gather(first_gain, ("dp", "tensor"), axis=0, tiled=True),
        lax.all_gather(query_weight, ("dp", "tensor"), axis=0, tiled=True),
        lax.all_gather(key_weight, ("dp", "tensor"), axis=0, tiled=True),
        lax.all_gather(value_weight, ("dp", "tensor"), axis=0, tiled=True),
        lax.all_gather(output_weight, ("dp", "tensor"), axis=0, tiled=True),
        lax.all_gather(second_gain, ("dp", "tensor"), axis=0, tiled=True),
    )


def fetch_mlp(gate_weight, up_weight, down_weight):
    return (
        lax.all_gather(gate_weight, "dp", axis=0, tiled=True),
        lax.all_gather(up_weight, "dp", axis=0, tiled=True),
        lax.all_gather(down_weight, "dp", axis=1, tiled=True),
    )


def reduce_attention(new_parts):
    return (
        lax.psum_scatter(new_parts[0], ("dp", "tensor"), scatter_dimension=0, tiled=True),
        lax.psum_scatter(new_parts[1], ("dp", "tensor"), scatter_dimension=0, tiled=True),
        lax.psum_scatter(new_parts[2], ("dp", "tensor"), scatter_dimension=0, tiled=True),
        lax.psum_scatter(new_parts[3], ("dp", "tensor"), scatter_dimension=0, tiled=True),
        lax.psum_scatter(new_parts[4], ("dp", "tensor"), scatter_dimension=0, tiled=True),
        lax.psum_scatter(new_parts[5], ("dp", "tensor"), scatter_dimension=0, tiled=True),
    )


def reduce_mlp(new_parts):
    return (
        lax.psum_scatter(new_parts[0], "dp", scatter_dimension=0, tiled=True),
        lax.psum_scatter(new_parts[1], "dp", scatter_dimension=0, tiled=True),
        lax.psum_scatter(new_parts[2], "dp", scatter_dimension=1, tiled=True),
    )


def accumulate(running, new_parts):
    if running is None:
        return tuple(new_parts)
    return tuple((earlier + latest for earlier, latest in zip(running, new_parts)))


def forward_block(inputs, seq_lengths, attn_full, mlp_full):
    first_gain, query_weight, key_weight, value_weight, output_weight, second_gain = attn_full
    gate_weight, up_weight, down_weight = mlp_full
    row_count = inputs.shape[0]
    group_size = HEADS // KV_HEADS
    factor = 1.0 / math.sqrt(HEAD)
    segment, position = pack_layout(seq_lengths, row_count)
    allowed = visible(segment, segment < SLOTS - 1)
    cosine, sine_part = rotary_tables(position, HEAD)
    first_scale = lax.rsqrt(jnp.mean(inputs * inputs, axis=1, keepdims=True) + EPSILON)
    normed_first = (inputs * first_scale * first_gain.astype(jnp.float32)).astype(jnp.bfloat16)
    queries = rotate(
        product(normed_first, query_weight).reshape(row_count, HEADS, HEAD), cosine, sine_part
    )
    queries = queries.astype(jnp.bfloat16).reshape(row_count, KV_HEADS, group_size, HEAD)
    key_vecs = rotate(
        product(normed_first, key_weight).reshape(row_count, KV_HEADS, HEAD), cosine, sine_part
    ).astype(jnp.bfloat16)
    values = (
        product(normed_first, value_weight).astype(jnp.bfloat16).reshape(row_count, KV_HEADS, HEAD)
    )
    scores = (
        jnp.einsum("qhgd,khd->hgqk", queries, key_vecs, preferred_element_type=jnp.float32) * factor
    )
    row_peak = jnp.max(jnp.where(allowed, scores, NEG_LARGE), axis=-1, keepdims=True)
    raised = jnp.where(allowed, jnp.exp(jnp.where(allowed, scores - row_peak, 0.0)), 0.0)
    totals = jnp.sum(raised, axis=-1, keepdims=True)
    safe_totals = jnp.where(totals > 0, totals, 1.0)
    log_total = row_peak + jnp.log(safe_totals)
    attn_probs = (raised / safe_totals).astype(jnp.bfloat16)
    blended = jnp.einsum("hgqk,khd->qhgd", attn_probs, values, preferred_element_type=jnp.float32)
    attended = blended.reshape(row_count, HEADS * HEAD).astype(jnp.bfloat16)
    middle = inputs + product(attended, output_weight)
    second_scale = lax.rsqrt(jnp.mean(middle * middle, axis=1, keepdims=True) + EPSILON)
    normed_second = (middle * second_scale * second_gain.astype(jnp.float32)).astype(jnp.bfloat16)
    gathered = lax.all_gather(normed_second, "tensor", axis=0, tiled=True)
    gate_pre = product(gathered, gate_weight)
    up_pre = product(gathered, up_weight)
    hidden = (jax.nn.silu(gate_pre) * up_pre).astype(jnp.bfloat16)
    layer_sum = middle + lax.psum_scatter(
        product(hidden, down_weight).astype(jnp.bfloat16), "tensor", scatter_dimension=0, tiled=True
    ).astype(jnp.float32)
    saved_state = (
        inputs,
        first_scale,
        normed_first,
        allowed,
        cosine,
        sine_part,
        queries,
        key_vecs,
        values,
        log_total,
        attended,
        middle,
        second_scale,
        gathered,
        gate_pre,
        up_pre,
        hidden,
    )
    return (layer_sum, saved_state)


def backward_block(upstream_low, saved_state, attn_full, mlp_full):
    (
        inputs,
        first_scale,
        normed_first,
        allowed,
        cosine,
        sine_part,
        queries,
        key_vecs,
        values,
        log_total,
        attended,
        middle,
        second_scale,
        gathered,
        gate_pre,
        up_pre,
        hidden,
    ) = saved_state
    first_gain, query_weight, key_weight, value_weight, output_weight, second_gain = attn_full
    gate_weight, up_weight, down_weight = mlp_full
    row_count = inputs.shape[0]
    group_size = HEADS // KV_HEADS
    factor = 1.0 / math.sqrt(HEAD)
    upstream = upstream_low.astype(jnp.float32)
    grad_gathered = lax.all_gather(upstream_low, "tensor", axis=0, tiled=True)
    hidden_grad = against(grad_gathered, down_weight)
    sig_gate = jax.nn.sigmoid(gate_pre)
    gate_grad = (hidden_grad * up_pre * sig_gate * (1.0 + gate_pre * (1.0 - sig_gate))).astype(
        jnp.bfloat16
    )
    up_grad = (hidden_grad * gate_pre * sig_gate).astype(jnp.bfloat16)
    mlp_parts = (
        across(gathered, gate_grad),
        across(gathered, up_grad),
        across(hidden, grad_gathered),
    )
    second_grad = lax.psum_scatter(
        against(gate_grad, gate_weight) + against(up_grad, up_weight),
        "tensor",
        scatter_dimension=0,
        tiled=True,
    )
    middle_part, second_gain_grad = norm_back(
        second_grad, middle, second_scale, second_gain.astype(jnp.float32)
    )
    middle_grad = upstream + middle_part
    middle_low = middle_grad.astype(jnp.bfloat16)
    output_part = across(attended, middle_low)
    attended_grad = (
        against(middle_low, output_weight)
        .astype(jnp.bfloat16)
        .reshape(row_count, KV_HEADS, group_size, HEAD)
    )
    scores = (
        jnp.einsum("qhgd,khd->hgqk", queries, key_vecs, preferred_element_type=jnp.float32) * factor
    )
    attn_probs = jnp.where(allowed, jnp.exp(jnp.where(allowed, scores - log_total, 0.0)), 0.0)
    prob_grad = jnp.einsum(
        "qhgd,khd->hgqk", attended_grad, values, preferred_element_type=jnp.float32
    )
    delta_sum = jnp.sum(attn_probs * prob_grad, axis=-1, keepdims=True)
    score_grad = (attn_probs * (prob_grad - delta_sum)).astype(jnp.bfloat16)
    value_grad = jnp.einsum(
        "hgqk,qhgd->khd",
        attn_probs.astype(jnp.bfloat16),
        attended_grad,
        preferred_element_type=jnp.float32,
    )
    value_grad = value_grad.astype(jnp.bfloat16).reshape(row_count, KV_HEADS * HEAD)
    query_rot_grad = (
        jnp.einsum("hgqk,khd->qhgd", score_grad, key_vecs, preferred_element_type=jnp.float32)
        * factor
    )
    key_rot_grad = (
        jnp.einsum("hgqk,qhgd->khd", score_grad, queries, preferred_element_type=jnp.float32)
        * factor
    )
    query_grad = (
        unrotate(query_rot_grad.reshape(row_count, HEADS, HEAD), cosine, sine_part)
        .astype(jnp.bfloat16)
        .reshape(row_count, HEADS * HEAD)
    )
    key_grad = (
        unrotate(key_rot_grad, cosine, sine_part)
        .astype(jnp.bfloat16)
        .reshape(row_count, KV_HEADS * HEAD)
    )
    first_grad = (
        against(query_grad, query_weight)
        + against(key_grad, key_weight)
        + against(value_grad, value_weight)
    )
    input_part, first_gain_grad = norm_back(
        first_grad, inputs, first_scale, first_gain.astype(jnp.float32)
    )
    input_grad = middle_grad + input_part
    attn_parts = (
        first_gain_grad,
        across(normed_first, query_grad),
        across(normed_first, key_grad),
        across(normed_first, value_grad),
        output_part,
        second_gain_grad,
    )
    return (input_grad, attn_parts, mlp_parts)


def per_device(
    tokens,
    lengths,
    first_gain,
    query_weight,
    key_weight,
    value_weight,
    output_weight,
    second_gain,
    gate_weight,
    up_weight,
    down_weight,
    cotangent,
):
    micro_count = tokens.shape[0]
    outputs = []
    input_grads = []
    attn_total = None
    mlp_total = None
    for step_index in range(micro_count):
        attn_full = fetch_attention(
            first_gain, query_weight, key_weight, value_weight, output_weight, second_gain
        )
        mlp_full = fetch_mlp(gate_weight, up_weight, down_weight)
        layer_sum, saved_state = forward_block(
            tokens[step_index].astype(jnp.float32), lengths[step_index, 0], attn_full, mlp_full
        )
        outputs.append(layer_sum.astype(jnp.bfloat16))
        input_grad, attn_parts, mlp_parts = backward_block(
            cotangent[step_index], saved_state, attn_full, mlp_full
        )
        input_grads.append(input_grad)
        attn_parts = reduce_attention(attn_parts)
        mlp_parts = reduce_mlp(mlp_parts)
        attn_total = accumulate(attn_total, attn_parts)
        mlp_total = accumulate(mlp_total, mlp_parts)
    return (
        jnp.stack(outputs),
        jnp.stack(input_grads),
        attn_total[0],
        attn_total[1],
        attn_total[2],
        attn_total[3],
        attn_total[4],
        attn_total[5],
        mlp_total[0],
        mlp_total[1],
        mlp_total[2],
    )


def solution(mesh):
    placed = (
        P(None, ("dp", "tensor"), None),
        P(None, ("dp", "tensor"), None),
        P(("dp", "tensor")),
        P(("dp", "tensor"), None),
        P(("dp", "tensor"), None),
        P(("dp", "tensor"), None),
        P(("dp", "tensor"), None),
        P(("dp", "tensor")),
        P("dp", "tensor"),
        P("dp", "tensor"),
        P("tensor", "dp"),
        P(None, ("dp", "tensor"), None),
    )
    return jax.shard_map(
        per_device,
        mesh=mesh,
        in_specs=placed,
        out_specs=(
            P(None, ("dp", "tensor"), None),
            P(None, ("dp", "tensor"), None),
            P(("dp", "tensor")),
            P(("dp", "tensor"), None),
            P(("dp", "tensor"), None),
            P(("dp", "tensor"), None),
            P(("dp", "tensor"), None),
            P(("dp", "tensor")),
            P("dp", "tensor"),
            P("dp", "tensor"),
            P("tensor", "dp"),
        ),
        check_vma=False,
    )
```

profile of v0, /device:TPU:0, one launch (start us, length us, event | category | flops | bytes accessed | tf_op | source)
XLA Modules:
  0.0 1699.0 jit_solution(15163263010389915065)
XLA Ops:
  14.5 42.2 %all-reduce.5 = (bf16[1536]{0:T(1024)(128)(2,1)S(1)}, bf16[1536]{0:T(1024)(128)(2,1)S(1)}) all-reduce(bf16[1536]{0:T(1024)(128)(2,1)S(1)} %dynamic-update-slice, bf16[1536]{0:T(1024)(128)(2,1)S(1)} %dynamic-update-slice.1), channel_id=1, replica_groups=mesh['dp'=8,'tensor'=4] {'dp','tensor'}, use_global_device_ids=true, to_apply=%add | all-reduce | flops 3072 | bytes 12288
  61.2 9.6 all-gather.17.cloned.1.call-done
  74.0 55.8 %all-gather.19.cloned.1.call-done = bf16[1536,768]{1,0:T(8,128)(2,1)} async-done(((bf16[48,768]{1,0:T(8,128)(2,1)}), bf16[1536,768]{1,0:T(8,128)(2,1)}) %all-gather.19.cloned.1.call-update) | async-done | bytes 2359312 | tf_op jit(solution)/shard_map/all_gather | solution.py:102
  135.1 60.2 %all-gather.21.cloned.1.call-done = bf16[1536,1536]{1,0:T(8,128)(2,1)} async-done(((bf16[48,1536]{1,0:T(8,128)(2,1)}), bf16[1536,1536]{1,0:T(8,128)(2,1)}) %all-gather.21.cloned.1.call-update) | async-done | bytes 4718608 | tf_op jit(solution)/shard_map/all_gather | solution.py:101
  207.8 52.7 %all-gather.23.cloned.1.call-done = bf16[1536,1536]{1,0:T(8,128)(2,1)} async-done(((bf16[48,1536]{1,0:T(8,128)(2,1)}), bf16[1536,1536]{1,0:T(8,128)(2,1)}) %all-gather.23.cloned.1.call-update) | async-done | bytes 4718608 | tf_op jit(solution)/shard_map/all_gather | solution.py:104
  268.4 53.5 %all-gather.29.cloned.1.call-done = bf16[1536,1024]{1,0:T(8,128)(2,1)} async-done(((bf16[192,1024]{1,0:T(8,128)(2,1)}), bf16[1536,1024]{1,0:T(8,128)(2,1)}) %all-gather.29.cloned.1.call-update) | async-done | bytes 3145744 | tf_op jit(solution)/shard_map/all_gather | solution.py:112
  321.9 20.3 %all-gather.25.cloned.1.call-done = bf16[512,1536]{1,0:T(8,128)(2,1)} async-done(((bf16[128,1536]{1,0:T(8,128)(2,1)}), bf16[512,1536]{1,0:T(8,128)(2,1)}) %all-gather.25.cloned.1.call-update) | async-done | bytes 1572880 | tf_op jit(solution)/shard_map/all_gather | solution.py:177
  347.7 57.1 %all-gather.27.cloned.1.call-done = bf16[1536,1024]{1,0:T(8,128)(2,1)} async-done(((bf16[192,1024]{1,0:T(8,128)(2,1)}), bf16[1536,1024]{1,0:T(8,128)(2,1)}) %all-gather.27.cloned.1.call-update) | async-done | bytes 3145744 | tf_op jit(solution)/shard_map/all_gather | solution.py:111
  409.9 15.4 all-gather.37.cloned.1.call-done
  425.3 62.7 %all-gather.31.cloned.1.call-done = bf16[1024,1536]{0,1:T(8,128)(2,1)} async-done(((bf16[1024,192]{0,1:T(8,128)(2,1)}), bf16[1024,1536]{0,1:T(8,128)(2,1)}) %all-gather.31.cloned.1.call-update) | async-done | bytes 3145744 | tf_op jit(solution)/shard_map/all_gather | solution.py:113
  531.1 35.7 %reduce-scatter.20.cloned.1.call-done = f32[128,1536]{1,0:T(8,128)} async-done(((f32[512,1536]{1,0:T(8,128)}), f32[128,1536]{1,0:T(8,128)}) %reduce-scatter.20.cloned.1.call-update) | async-done | bytes 786448 | tf_op jit(solution)/shard_map/reduce_scatter | solution.py:244
  572.2 17.7 %all-gather.35.cloned.1.call-done = bf16[512,1536]{1,0:T(8,128)(2,1)} async-done(((bf16[128,1536]{1,0:T(8,128)(2,1)}), bf16[512,1536]{1,0:T(8,128)(2,1)}) %all-gather.35.cloned.1.call-update) | async-done | bytes 1572880 | tf_op jit(solution)/shard_map/all_gather | solution.py:177
  598.6 13.0 all-gather.41.cloned.1.call-done
  641.6 12.3 all-gather.39.cloned.1.call-done
  684.4 31.3 %reduce-scatter.16.cloned.1.call-done = bf16[128,1536]{1,0:T(8,128)(2,1)} async-done(((bf16[512,1536]{1,0:T(8,128)(2,1)}), bf16[128,1536]{1,0:T(8,128)(2,1)}) %reduce-scatter.16.cloned.1.call-update) | async-done | bytes 393232 | tf_op jit(solution)/shard_map/reduce_scatter | solution.py:181
  715.7 40.4 %reduce-scatter.22.cloned.1.call-done = f32[128,1536]{1,0:T(8,128)} async-done(((f32[512,1536]{1,0:T(8,128)}), f32[128,1536]{1,0:T(8,128)}) %reduce-scatter.22.cloned.1.call-update) | async-done | bytes 786448 | tf_op jit(solution)/shard_map/reduce_scatter | solution.py:244
  756.1 40.7 %reduce-scatter.24.cloned.1.call-done = f32[128,1536]{1,0:T(8,128)} async-done(((f32[512,1536]{1,0:T(8,128)}), f32[128,1536]{1,0:T(8,128)}) %reduce-scatter.24.cloned.1.call-update) | async-done | bytes 786448 | tf_op jit(solution)/shard_map/reduce_scatter | solution.py:244
  909.6 39.9 %all-reduce.4 = (f32[1536]{0:T(1024)}, f32[1536]{0:T(1024)}) all-reduce(f32[1536]{0:T(1024)} %add_add_fusion.6, f32[1536]{0:T(1024)S(1)} %copy-done.131), channel_id=29, replica_groups=mesh['dp'=8,'tensor'=4] {'dp','tensor'}, use_global_device_ids=true, to_apply=%region_37.38.clone | all-reduce | flops 3072 | bytes 24576
  960.3 85.1 %reduce-scatter.28.cloned.1.call-done = f32[48,768]{1,0:T(8,128)} async-done(((f32[1536,768]{1,0:T(8,128)}), f32[48,768]{1,0:T(8,128)}) %reduce-scatter.28.cloned.1.call-update) | async-done | bytes 147472 | tf_op jit(solution)/shard_map/reduce_scatter | solution.py:121
  1045.4 121.3 %reduce-scatter.38.cloned.1.call-done = f32[1024,192]{0,1:T(8,128)} async-done(((f32[1024,1536]{0,1:T(8,128)}), f32[1024,192]{0,1:T(8,128)}) %reduce-scatter.38.cloned.1.call-update) | async-done | bytes 786448 | tf_op jit(solution)/shard_map/reduce_scatter | solution.py:132
  1166.7 121.3 %reduce-scatter.36.cloned.1.call-done = f32[192,1024]{1,0:T(8,128)} async-done(((f32[1536,1024]{1,0:T(8,128)}), f32[192,1024]{1,0:T(8,128)}) %reduce-scatter.36.cloned.1.call-update) | async-done | bytes 786448 | tf_op jit(solution)/shard_map/reduce_scatter | solution.py:131
  1288.0 121.1 %reduce-scatter.34.cloned.1.call-done = f32[192,1024]{1,0:T(8,128)} async-done(((f32[1536,1024]{1,0:T(8,128)}), f32[192,1024]{1,0:T(8,128)}) %reduce-scatter.34.cloned.1.call-update) | async-done | bytes 786448 | tf_op jit(solution)/shard_map/reduce_scatter | solution.py:130
  1409.2 141.2 %reduce-scatter.32.cloned.1.call-done = f32[48,1536]{1,0:T(8,128)} async-done(((f32[1536,1536]{1,0:T(8,128)}), f32[48,1536]{1,0:T(8,128)}) %reduce-scatter.32.cloned.1.call-update) | async-done | bytes 294928 | tf_op jit(solution)/shard_map/reduce_scatter | solution.py:123
  1550.3 142.0 %reduce-scatter.26.cloned.1.call-done = f32[48,1536]{1,0:T(8,128)} async-done(((f32[1536,1536]{1,0:T(8,128)}), f32[48,1536]{1,0:T(8,128)}) %reduce-scatter.26.cloned.1.call-update) | async-done | bytes 294928 | tf_op jit(solution)/shard_map/reduce_scatter | solution.py:120
  (615 shorter events, 289.8 us)
Async XLA Ops:
  7.2 63.7 %all-gather.17.cloned.1.call-start = ((), (), s32[]{:S(2)}) async-start(), calls=%async_computation.13 | async-start | bytes 2433024 | tf_op jit(solution)/shard_map/all_gather | solution.py:103
  7.9 121.9 %all-gather.19.cloned.1.call-start = ((), (), s32[]{:S(2)}) async-start(), calls=%async_computation.14 | async-start | bytes 2433024 | tf_op jit(solution)/shard_map/all_gather | solution.py:102
  8.7 186.6 %all-gather.21.cloned.1.call-start = ((), (), s32[]{:S(2)}) async-start(), calls=%async_computation.15 | async-start | bytes 4866048 | tf_op jit(solution)/shard_map/all_gather | solution.py:101
  9.4 251.1 %all-gather.23.cloned.1.call-start = ((), (), s32[]{:S(2)}) async-start(), calls=%async_computation.16 | async-start | bytes 4866048 | tf_op jit(solution)/shard_map/all_gather | solution.py:104
  10.0 311.9 %all-gather.29.cloned.1.call-start = ((), (), s32[]{:S(2)}) async-start(), calls=%async_computation.19 | async-start | bytes 3538944 | tf_op jit(solution)/shard_map/all_gather | solution.py:112
  10.6 331.6 %all-gather.25.cloned.1.call-start = ((), (), s32[]{:S(2)}) async-start(), calls=%async_computation.17 | async-start | bytes 1966080 | tf_op jit(solution)/shard_map/all_gather | solution.py:177
  265.2 139.6 %all-gather.27.cloned.1.call-start = ((), (), s32[]{:S(2)}) async-start(), calls=%async_computation.18 | async-start | bytes 3538944 | tf_op jit(solution)/shard_map/all_gather | solution.py:111
  266.0 159.3 %all-gather.37.cloned.1.call-start = ((), (), s32[]{:S(2)}) async-start(), calls=%async_computation.29 | async-start | bytes 1966080 | tf_op jit(solution)/shard_map/all_gather | solution.py:232
  267.1 220.8 %all-gather.31.cloned.1.call-start = ((), (), s32[]{:S(2)}) async-start(), calls=%async_computation.20 | async-start | bytes 3538944 | tf_op jit(solution)/shard_map/all_gather | solution.py:113
  267.9 263.2 %reduce-scatter.14.cloned.1.call-start = ((), (), s32[]{:S(2)}) async-start(), calls=%async_computation.21 | async-start | bytes 1966080 | tf_op jit(solution)/shard_map/reduce_scatter | solution.py:181
  499.2 67.6 %reduce-scatter.20.cloned.1.call-start = ((), (), s32[]{:S(2)}) async-start(), calls=%async_computation.26 | async-start | bytes 3932160 | tf_op jit(solution)/shard_map/reduce_scatter | solution.py:244
  507.9 81.9 %all-gather.35.cloned.1.call-start = ((), (), s32[]{:S(2)}) async-start(), calls=%async_computation.24 | async-start | bytes 1966080 | tf_op jit(solution)/shard_map/all_gather | solution.py:177
  571.3 82.5 %all-gather.39.cloned.1.call-start = ((), (), s32[]{:S(2)}) async-start(), calls=%async_computation.30 | async-start | bytes 1966080 | tf_op jit(solution)/shard_map/all_gather | solution.py:232
  571.9 112.5 %reduce-scatter.18.cloned.1.call-start = ((), (), s32[]{:S(2)}) async-start(), calls=%async_computation.25 | async-start | bytes 1966080 | tf_op jit(solution)/shard_map/reduce_scatter | solution.py:181
  623.4 92.3 %reduce-scatter.16.cloned.1.call-start = ((), (), s32[]{:S(2)}) async-start(), calls=%async_computation.23 | async-start | bytes 1966080 | tf_op jit(solution)/shard_map/reduce_scatter | solution.py:181
  665.4 90.7 %reduce-scatter.22.cloned.1.call-start = ((), (), s32[]{:S(2)}) async-start(), calls=%async_computation.27 | async-start | bytes 3932160 | tf_op jit(solution)/shard_map/reduce_scatter | solution.py:244
  673.7 123.1 %reduce-scatter.24.cloned.1.call-start = ((), (), s32[]{:S(2)}) async-start(), calls=%async_computation.28 | async-start | bytes 3932160 | tf_op jit(solution)/shard_map/reduce_scatter | solution.py:244
  681.6 278.7 %reduce-scatter.30.cloned.1.call-start = ((), (), s32[]{:S(2)}) async-start(), calls=%async_computation.34 | async-start | bytes 4866048 | tf_op jit(solution)/shard_map/reduce_scatter | solution.py:122
  825.1 220.4 %reduce-scatter.28.cloned.1.call-start = ((), (), s32[]{:S(2)}) async-start(), calls=%async_computation.33 | async-start | bytes 4866048 | tf_op jit(solution)/shard_map/reduce_scatter | solution.py:121
  837.9 328.8 %reduce-scatter.38.cloned.1.call-start = ((), (), s32[]{:S(2)}) async-start(), calls=%async_computation.38 | async-start | bytes 7077888 | tf_op jit(solution)/shard_map/reduce_scatter | solution.py:132
  848.5 439.5 %reduce-scatter.36.cloned.1.call-start = ((), (), s32[]{:S(2)}) async-start(), calls=%async_computation.37 | async-start | bytes 7077888 | tf_op jit(solution)/shard_map/reduce_scatter | solution.py:131
  859.3 549.8 %reduce-scatter.34.cloned.1.call-start = ((), (), s32[]{:S(2)}) async-start(), calls=%async_computation.36 | async-start | bytes 7077888 | tf_op jit(solution)/shard_map/reduce_scatter | solution.py:130
  869.7 680.6 %reduce-scatter.32.cloned.1.call-start = ((), (), s32[]{:S(2)}) async-start(), calls=%async_computation.35 | async-start | bytes 9732096 | tf_op jit(solution)/shard_map/reduce_scatter | solution.py:123
  879.8 812.5 %reduce-scatter.26.cloned.1.call-start = ((), (), s32[]{:S(2)}) async-start(), calls=%async_computation.32 | async-start | bytes 9732096 | tf_op jit(solution)/shard_map/reduce_scatter | solution.py:120
  (196 other events, 1816.7 us)
Sparse Core Ops, SparseCore 0:
  10.9 59.9 all-gather.16
  73.8 56.0 all-gather.18
  132.7 62.5 all-gather.20
  198.1 62.4 all-gather.22
  262.6 59.2 all-gather.28
  344.3 60.4 all-gather.26
  427.5 60.4 all-gather.30
  499.3 26.7 reduce-scatter.13
  528.8 37.9 reduce-scatter.19
  570.1 19.6 all-gather.34
  591.9 19.6 all-gather.40
  613.1 19.6 all-gather.32
  634.2 19.6 all-gather.38
  656.2 28.1 reduce-scatter.17
  687.6 28.1 reduce-scatter.15
  718.1 37.9 reduce-scatter.21
  758.8 37.9 reduce-scatter.23
  825.2 107.0 reduce-scatter.29
  939.2 106.1 reduce-scatter.27
  1049.6 117.0 reduce-scatter.37
  1170.9 117.0 reduce-scatter.35
  1292.0 117.0 reduce-scatter.33
  1415.6 134.6 reduce-scatter.31
  1557.6 134.5 reduce-scatter.25
  (2 shorter events, 36.4 us)
where the time goes:
time: 1710 us; the launch traced here: 1700 us
  waiting for transfers between devices  1330 us (78%)
  matrix products  200 us (12%)
  blocking collectives  82.1 us (5%)
  other arithmetic  37.4 us (2%)
  local copies, waits for them, and re-layouts  32.3 us (2%)
    reduce_scatter x1, waiting for transfers between devices, reduce_attention(): lax.psum_scatter(new_parts[1], ('dp', 'tensor'), scatter_dimension=0, til...  142 us
    reduce_scatter x1, waiting for transfers between devices, reduce_attention(): lax.psum_scatter(new_parts[4], ('dp', 'tensor'), scatter_dimension=0, til...  141 us
    reduce_scatter x1, waiting for transfers between devices, reduce_mlp(): lax.psum_scatter(new_parts[1], 'dp', scatter_dimension=0, tiled=True)  121 us
    reduce_scatter x1, waiting for transfers between devices, reduce_mlp(): lax.psum_scatter(new_parts[2], 'dp', scatter_dimension=1, tiled=True)  121 us
    reduce_scatter x1, waiting for transfers between devices, reduce_mlp(): lax.psum_scatter(new_parts[0], 'dp', scatter_dimension=0, tiled=True)  121 us
    reduce_scatter x3, waiting for transfers between devices, backward_block(): lax.psum_scatter(against(gate_grad, gate_weight) + against(up_grad, up_we...  117 us
    reduce_scatter x1, waiting for transfers between devices, reduce_attention(): lax.psum_scatter(new_parts[2], ('dp', 'tensor'), scatter_dimension=0, til...  85.1 us
    unnamed x2, blocking collectives  82.1 us
  transfers between devices with their start and end apart: 26, of which 24 were waited for; matrix products, arithmetic and copies ran while one was open for 13% of the time, Pallas kernels for 0%

commit v1 on v0

v1 whole, which is shorter than its diff:
```python
import math

import jax
import jax.numpy as jnp
from jax import lax
from jax.sharding import PartitionSpec as P

HEADS = 16
KV_HEADS = 8
HEAD = 96
SLOTS = 6
GROUP = HEADS // KV_HEADS
LANES = 128

EPSILON = 1e-05
ROPE_BASE = 100000.0
NEG_LARGE = -1e30
AXES = ("dp", "tensor")
bf16 = jnp.bfloat16
f32 = jnp.float32


def pack_layout(seq_lengths, row_count):
    seq_ends = jnp.cumsum(seq_lengths)
    seq_starts = seq_ends - seq_lengths
    row_index = jnp.arange(row_count, dtype=jnp.int32)
    segment = jnp.sum((row_index[:, None] >= seq_ends[None, :]).astype(jnp.int32), axis=1)
    owner_hot = segment[:, None] == jnp.arange(seq_lengths.shape[0], dtype=jnp.int32)[None, :]
    position = row_index - jnp.sum(jnp.where(owner_hot, seq_starts[None, :], 0), axis=1)
    return (segment, position)


def rotary_tables(position, head_size):
    half_size = head_size // 2
    freq_index = jnp.arange(half_size, dtype=f32)
    inverse = jnp.exp(freq_index * (-2.0 / head_size) * math.log(ROPE_BASE))
    angles = position.astype(f32)[..., None] * inverse
    return (jnp.cos(angles), jnp.sin(angles))


def rotate(vectors, cosine, sine_part):
    half_size = vectors.shape[-1] // 2
    lower_half = vectors[..., :half_size]
    upper_half = vectors[..., half_size:]
    cosine = cosine[..., None, :]
    sine_part = sine_part[..., None, :]
    return jnp.concatenate(
        [
            lower_half * cosine - upper_half * sine_part,
            upper_half * cosine + lower_half * sine_part,
        ],
        axis=-1,
    )


def product(left_side, right_side):
    return jnp.dot(left_side, right_side, preferred_element_type=f32)


def across(left_side, right_side):
    return lax.dot_general(
        left_side, right_side, (((0,), (0,)), ((), ())), preferred_element_type=f32
    )


def against(left_side, right_side):
    return lax.dot_general(
        left_side, right_side, (((1,), (1,)), ((), ())), preferred_element_type=f32
    )


def bits_of(size):
    return [1 << k for k in range(size.bit_length() - 1)]


def near_first(size):
    masks = bits_of(size)
    return masks[:1] + masks[:0:-1]


def far_first(size):
    return bits_of(size)[::-1]


def rel_source(me, masks, block, count):
    place = jnp.arange(count, dtype=jnp.int32)
    step = place // block
    delta = jnp.zeros_like(step)
    for k, mask in enumerate(masks):
        delta = delta + ((step >> k) & 1) * mask
    return (me ^ delta) * block + place % block


def one_hot(source):
    count = source.shape[0]
    rows = lax.broadcasted_iota(jnp.int32, (count, count), 0)
    return (rows == source[None, :]).astype(bf16)


def join(parts):
    return parts[0] if len(parts) == 1 else jnp.concatenate(parts, axis=0)


def program(sizes):
    dp_n, tp_n = sizes["dp"], sizes["tensor"]
    world = dp_n * tp_n

    def swap(array, mask):
        return lax.ppermute(array, AXES, [(i, i ^ mask) for i in range(world)])

    def gather(own, masks, loose):
        held = [own]
        for k, mask in enumerate(masks):
            got = [swap(part, mask) for part in held]
            held = held + got
            if k < len(masks) - loose:
                held = [join(held)]
        return held

    def per_device(
        tokens,
        lengths,
        first_gain,
        query_weight,
        key_weight,
        value_weight,
        output_weight,
        second_gain,
        gate_weight,
        up_weight,
        down_weight,
        cotangent,
    ):
        micro, per_pack, width = tokens.shape
        rows = micro * per_pack
        qw, kw = query_weight.shape[1], key_weight.shape[1]
        ff = gate_weight.shape[1]
        wide = qw + 2 * kw
        shard = query_weight.shape[0]
        dp_i, t_i = lax.axis_index("dp"), lax.axis_index("tensor")
        me = dp_i * tp_n + t_i

        dp_attn = [m * tp_n for m in near_first(dp_n)]
        t_bits = bits_of(tp_n)[::-1]
        attn_masks = dp_attn + t_bits
        mlp_masks = [m * tp_n for m in far_first(dp_n)]

        x_low = tokens.reshape(rows, width)
        dy_low = cotangent.reshape(rows, width)

        gains = jnp.pad(
            jnp.stack([first_gain, second_gain], axis=1), ((0, 0), (0, LANES - 2))
        )
        own_qkv = jnp.concatenate([query_weight, key_weight, value_weight, gains], axis=1)
        own_gu = jnp.concatenate([gate_weight, up_weight], axis=1)
        own_down = down_weight.T

        def gather_attn(own):
            held = gather(own, dp_attn, 2)
            far = [swap(part, t_bits[0]) for part in held]
            pieces = [join(held), join(far)]
            for mask in t_bits[1:]:
                pieces = pieces + [swap(part, mask) for part in pieces]
            return pieces

        qkv_pieces = gather_attn(own_qkv)
        out_pieces = gather_attn(output_weight)
        gu_full = join(gather(own_gu, mlp_masks, 3))
        down_full = join(gather(own_down, mlp_masks, 3))
        n_pieces = len(qkv_pieces)
        part = width // n_pieces

        pick_attn = one_hot(rel_source(me, attn_masks, shard, width))
        mlp_source = rel_source(dp_i, [m // tp_n for m in mlp_masks], shard * tp_n, width)
        pick_mlp = one_hot(mlp_source)

        def order(array, pick):
            return product(array, pick).astype(bf16)

        def restore(array, pick):
            return against(array, pick)

        gains_rel = jnp.concatenate([piece[:, wide : wide + 2] for piece in qkv_pieces], axis=0)
        g1_rel = gains_rel[:, 0].astype(f32)
        g2 = restore(gains_rel[:, 1][None, :], pick_attn)[0]

        segment, position = jax.vmap(lambda own: pack_layout(own, per_pack))(lengths[:, 0])
        cosine, sine_part = rotary_tables(position, HEAD)
        row_index = jnp.arange(per_pack, dtype=jnp.int32)
        allowed = (
            (segment[:, :, None] == segment[:, None, :])
            & (row_index[None, None, :] <= row_index[None, :, None])
            & (segment < SLOTS - 1)[:, :, None]
        )[:, None, None]
        factor = 1.0 / math.sqrt(HEAD)

        inputs = x_low.astype(f32)
        r1 = lax.rsqrt(jnp.mean(inputs * inputs, axis=1, keepdims=True) + EPSILON)
        x_rel = order(x_low, pick_attn).astype(f32)
        n1_rel = (x_rel * r1 * g1_rel).astype(bf16)
        n1_parts = [n1_rel[:, k * part : (k + 1) * part] for k in range(n_pieces)]
        qkv = sum(product(a, b) for a, b in zip(n1_parts, qkv_pieces))
        shape = (micro, per_pack)
        queries = rotate(qkv[:, :qw].reshape(shape + (HEADS, HEAD)), cosine, sine_part)
        queries = queries.astype(bf16).reshape(shape + (KV_HEADS, GROUP, HEAD))
        keys = rotate(
            qkv[:, qw : qw + kw].reshape(shape + (KV_HEADS, HEAD)), cosine, sine_part
        ).astype(bf16)
        values = qkv[:, qw + kw : wide].astype(bf16).reshape(shape + (KV_HEADS, HEAD))
        scores = (
            jnp.einsum("pqhgd,pkhd->phgqk", queries, keys, preferred_element_type=f32) * factor
        )
        row_peak = jnp.max(jnp.where(allowed, scores, NEG_LARGE), axis=-1, keepdims=True)
        raised = jnp.where(allowed, jnp.exp(jnp.where(allowed, scores - row_peak, 0.0)), 0.0)
        totals = jnp.sum(raised, axis=-1, keepdims=True)
        probs = raised / jnp.where(totals > 0, totals, 1.0)
        probs_low = probs.astype(bf16)
        attended = jnp.einsum("phgqk,pkhd->pqhgd", probs_low, values, preferred_element_type=f32)
        attended = attended.reshape(rows, qw).astype(bf16)
        att_rel = order(attended, pick_attn)
        att_parts = [att_rel[:, k * part : (k + 1) * part] for k in range(n_pieces)]
        middle = inputs + sum(product(a, b) for a, b in zip(att_parts, out_pieces))
        r2 = lax.rsqrt(jnp.mean(middle * middle, axis=1, keepdims=True) + EPSILON)
        n2 = (middle * r2 * g2).astype(bf16)
        n2_rel = order(n2, pick_mlp)
        dy_rel = order(dy_low, pick_mlp)

        def spread(own):
            return join(gather(own, t_bits, tp_n))

        def collect(partial):
            for mask in t_bits[::-1]:
                half = partial.shape[0] // 2
                got = swap(partial[half:].astype(bf16), mask)
                partial = partial[:half].astype(f32) + got.astype(f32)
            return partial

        dy_all = spread(dy_rel)
        n2_all = spread(n2_rel)
        gu = product(n2_all, gu_full)
        gate, up = gu[:, :ff], gu[:, ff:]
        sig = jax.nn.sigmoid(gate)
        hidden = (gate * sig * up).astype(bf16)
        dhid = product(dy_all, down_full)
        dgate = (dhid * up * sig * (1.0 + gate * (1.0 - sig))).astype(bf16)
        dup = (dhid * gate * sig).astype(bf16)
        dgu = jnp.concatenate([dgate, dup], axis=1)
        dn2 = restore(collect(against(dgu, gu_full).astype(bf16)).astype(bf16), pick_mlp)
        down_sum = collect(against(hidden, down_full).astype(bf16)).astype(bf16)
        layer_out = (middle + restore(down_sum, pick_mlp)).astype(bf16)

        def reduce_rows(own_half, sent_half, masks):
            total = own_half() + swap(sent_half().astype(bf16), masks[0]).astype(f32)
            for mask in masks[1:]:
                half = total.shape[0] // 2
                got = swap(total[half:].astype(bf16), mask)
                total = total[:half] + got.astype(f32)
            return total

        half = width // 2

        def mlp_grad(left, right):
            return reduce_rows(
                lambda: across(left[:, :half], right),
                lambda: across(left[:, half:], right),
                mlp_masks[::-1],
            )

        down_grad = mlp_grad(dy_all, hidden).T
        gate_grad = mlp_grad(n2_all, dgate)
        up_grad = mlp_grad(n2_all, dup)

        dy = dy_low.astype(f32)
        weighted = dn2 * g2
        dmid = dy + r2 * weighted - middle * (r2 * r2 * r2) * jnp.mean(
            weighted * middle, axis=1, keepdims=True
        )
        dmb = dmid.astype(bf16)

        def attn_grad(lefts, right):
            held = [across(left, right) for left in lefts]
            for mask in t_bits[1:][::-1]:
                n = len(held) // 2
                got = [swap(piece.astype(bf16), mask) for piece in held[n:]]
                held = [a + b.astype(f32) for a, b in zip(held[:n], got)]
            return reduce_rows(
                lambda: held[0], lambda: held[1], [t_bits[0]] + dp_attn[::-1]
            )

        output_grad = attn_grad(att_parts, dmb)
        datt_rel = jnp.concatenate([against(dmb, piece) for piece in out_pieces], axis=1)
        datt = restore(datt_rel.astype(bf16), pick_attn).astype(bf16)
        datt = datt.reshape(shape + (KV_HEADS, GROUP, HEAD))
        dprob = jnp.einsum("pqhgd,pkhd->phgqk", datt, values, preferred_element_type=f32)
        delta = jnp.sum(probs * dprob, axis=-1, keepdims=True)
        dscore = (probs * (dprob - delta)).astype(bf16)
        dvalue = jnp.einsum("phgqk,pqhgd->pkhd", probs_low, datt, preferred_element_type=f32)
        dqr = jnp.einsum("phgqk,pkhd->pqhgd", dscore, keys, preferred_element_type=f32) * factor
        dkr = jnp.einsum("phgqk,pqhgd->pkhd", dscore, queries, preferred_element_type=f32) * factor
        dq = rotate(dqr.reshape(shape + (HEADS, HEAD)), cosine, -sine_part)
        dk = rotate(dkr, cosine, -sine_part)
        dqkv = jnp.concatenate(
            [
                dq.astype(bf16).reshape(rows, qw),
                dk.astype(bf16).reshape(rows, kw),
                dvalue.astype(bf16).reshape(rows, kw),
            ],
            axis=1,
        )
        qkv_grad = attn_grad(n1_parts, dqkv)
        dn1_rel = jnp.concatenate(
            [against(dqkv, piece[:, :wide]) for piece in qkv_pieces], axis=1
        )
        weighted = dn1_rel * g1_rel
        part_rel = r1 * weighted - x_rel * (r1 * r1 * r1) * jnp.mean(
            weighted * x_rel, axis=1, keepdims=True
        )
        high = part_rel.astype(bf16)
        low = (part_rel - high.astype(f32)).astype(bf16)
        input_grad = dmid + restore(high, pick_attn) + restore(low, pick_attn)

        own_wide = own_qkv[:, :wide].astype(f32)
        first_gain_grad = jnp.sum(own_wide * qkv_grad, axis=1) / first_gain.astype(f32)
        second = jnp.sum(
            gate_weight.astype(f32) * gate_grad + up_weight.astype(f32) * up_grad, axis=1
        )
        second = lax.psum(second, "tensor")
        second = lax.dynamic_slice(second, (t_i * shard,), (shard,))
        second_gain_grad = second / second_gain.astype(f32)

        return (
            layer_out.reshape(tokens.shape),
            input_grad.reshape(tokens.shape),
            first_gain_grad,
            qkv_grad[:, :qw],
            qkv_grad[:, qw : qw + kw],
            qkv_grad[:, qw + kw :],
            output_grad,
            second_gain_grad,
            gate_grad,
            up_grad,
            down_grad,
        )

    return per_device


def solution(mesh):
    rows = P(None, AXES, None)
    split = P(AXES, None)
    placed = (
        rows,
        rows,
        P(AXES),
        split,
        split,
        split,
        split,
        P(AXES),
        P("dp", "tensor"),
        P("dp", "tensor"),
        P("tensor", "dp"),
        rows,
    )
    return jax.shard_map(
        program(dict(mesh.shape)),
        mesh=mesh,
        in_specs=placed,
        out_specs=(
            rows,
            rows,
            P(AXES),
            split,
            split,
            split,
            split,
            P(AXES),
            P("dp", "tensor"),
            P("dp", "tensor"),
            P("tensor", "dp"),
        ),
        check_vma=False,
    )
```

time: 1710 us -> 816 us (0.48)
  waiting for transfers between devices: 1330 us -> 386 us
  local copies, waits for them, and re-layouts: 32.3 us -> 103 us
  starting transfers between devices: 3.12 us -> 59.7 us
  blocking collectives: 82.1 us -> 29.6 us
  matrix products: 200 us -> 181 us
    reduce_scatter x13 -> x0, waiting for transfers between devices: 882 us -> none  [the longest x1 142 us: reduce_attention(): lax.psum_scatter(new_parts[1], ('dp', 'tensor'), scatter_dimension=0, til...]
    all_gather x13 -> x0, waiting for transfers between devices: 440 us -> none  [the longest x1 62.7 us: fetch_mlp(): lax.all_gather(down_weight, 'dp', axis=1, tiled=True)]
    ppermute x0 -> x65, waiting for transfers between devices: none -> 386 us  [swap(): return lax.ppermute(array, AXES, [(i, i ^ mask) for i in range(world)])]
    unnamed x2 -> x0, blocking collectives: 82.1 us -> none
    ppermute x0 -> x65, starting transfers between devices: none -> 59.7 us  [swap(): return lax.ppermute(array, AXES, [(i, i ^ mask) for i in range(world)])]
    psum x0 -> x1, blocking collectives: none -> 29.6 us  [per_device(): second = lax.psum(second, 'tensor')]
    unnamed x394 -> x201, local copies, waits for them, and re-layouts: 16.5 us -> 42.8 us
    dot_general x21 -> x14, matrix products: 58.2 us -> 36.2 us  [across(): lax.dot_general(left_side, right_side, (((0,), (0,)), ((), ())), preferre...]
  transfers between devices with their start and end apart: 26 -> 65, of which waited for: 24 -> 26; matrix products, arithmetic and copies ran while one was open for 13% -> 35% of each run, Pallas kernels for 0% -> 0%
where the time goes in v1:
time: 816 us; the launch traced here: 806 us
  waiting for transfers between devices  386 us (47%)
  matrix products  181 us (22%)
  local copies, waits for them, and re-layouts  103 us (13%)
  starting transfers between devices  59.7 us (7%)
  other arithmetic  43.3 us (5%)
  blocking collectives  29.6 us (4%)
    ppermute x65, waiting for transfers between devices, swap(): return lax.ppermute(array, AXES, [(i, i ^ mask) for i in range(world)])  386 us
    dot_general x16, matrix products, against(): lax.dot_general(left_side, right_side, (((1,), (1,)), ((), ())), preferre...  67.3 us
    dot_general x14, matrix products, product(): return jnp.dot(left_side, right_side, preferred_element_type=f32)  66.5 us
    ppermute x65, starting transfers between devices, swap(): return lax.ppermute(array, AXES, [(i, i ^ mask) for i in range(world)])  59.7 us
    unnamed x201, local copies, waits for them, and re-layouts  42.8 us
    dot_general x14, matrix products, across(): lax.dot_general(left_side, right_side, (((0,), (0,)), ((), ())), preferre...  36.2 us
    psum x1, blocking collectives, per_device(): second = lax.psum(second, 'tensor')  29.6 us
  transfers between devices with their start and end apart: 65, of which 26 were waited for; matrix products, arithmetic and copies ran while one was open for 35% of the time, Pallas kernels for 0%

profile of v1, /device:TPU:0, one launch (start us, length us, event | category | flops | bytes accessed | tf_op | source)
XLA Modules:
  0.0 805.8 jit_solution(15397457779507763800)
XLA Ops:
  29.8 8.6 %collective-permute-done.4 = bf16[96,3200]{1,0:T(8,128)(2,1)S(1)} collective-permute-done((bf16[96,3200]{1,0:T(8,128)(2,1)S(1)}, bf16[96,3200]{1,0:T(8,128)(2,1)S(1)}, u32[]{:S(2)}, u32[]{:S(2)}) %collective-permute-start.4) | collective-permute-done | bytes 614432 | tf_op jit(solution)/shard_map/ppermute | solution.py:109
  39.7 27.5 %collective-permute-done.1 = bf16[96,3200]{1,0:T(8,128)(2,1)S(1)} collective-permute-done((bf16[96,3200]{1,0:T(8,128)(2,1)S(1)}, bf16[96,3200]{1,0:T(8,128)(2,1)S(1)}, u32[]{:S(2)}, u32[]{:S(2)}) %collective-permute-start.1) | collective-permute-done | bytes 614432 | tf_op jit(solution)/shard_map/ppermute | solution.py:109
  76.1 8.4 %collective-permute-done.3 = bf16[96,3200]{1,0:T(8,128)(2,1)S(1)} collective-permute-done((bf16[96,3200]{1,0:T(8,128)(2,1)S(1)}, bf16[96,3200]{1,0:T(8,128)(2,1)S(1)}, u32[]{:S(2)}, u32[]{:S(2)}) %collective-permute-start.3) | collective-permute-done | bytes 614432 | tf_op jit(solution)/shard_map/ppermute | solution.py:109
  88.3 13.0 %collective-permute-done.6 = bf16[96,3200]{1,0:T(8,128)(2,1)S(1)} collective-permute-done((bf16[96,3200]{1,0:T(8,128)(2,1)S(1)}, bf16[96,3200]{1,0:T(8,128)(2,1)S(1)}, u32[]{:S(2)}, u32[]{:S(2)}) %collective-permute-start.6) | collective-permute-done | bytes 614432 | tf_op jit(solution)/shard_map/ppermute | solution.py:109
  102.2 9.9 %collective-permute-done.7 = bf16[96,3200]{1,0:T(8,128)(2,1)S(1)} collective-permute-done((bf16[96,3200]{1,0:T(8,128)(2,1)S(1)}, bf16[96,3200]{1,0:T(8,128)(2,1)S(1)}, u32[]{:S(2)}, u32[]{:S(2)}) %collective-permute-start.7) | collective-permute-done | bytes 614432 | tf_op jit(solution)/shard_map/ppermute | solution.py:109
  141.3 7.3 collective-permute-done.34
  149.2 23.1 %collective-permute-done.23 = bf16[192,2048]{1,0:T(8,128)(2,1)S(1)} collective-permute-done((bf16[192,2048]{1,0:T(8,128)(2,1)}, bf16[192,2048]{1,0:T(8,128)(2,1)S(1)}, u32[]{:S(2)}, u32[]{:S(2)}) %collective-permute-start.23) | collective-permute-done | bytes 786464 | tf_op jit(solution)/shard_map/ppermute | solution.py:109
  253.8 18.8 %collective-permute-done.36 = bf16[192,1024]{1,0:T(8,128)(2,1)S(1)} collective-permute-done((bf16[192,1024]{1,0:T(8,128)(2,1)S(1)}, bf16[192,1024]{1,0:T(8,128)(2,1)S(1)}, u32[]{:S(2)}, u32[]{:S(2)}) %collective-permute-start.36) | collective-permute-done | bytes 393248 | tf_op jit(solution)/shard_map/ppermute | solution.py:109
  279.9 13.4 %collective-permute-done.28 = bf16[192,2048]{1,0:T(8,128)(2,1)S(1)} collective-permute-done((bf16[192,2048]{1,0:T(8,128)(2,1)}, bf16[192,2048]{1,0:T(8,128)(2,1)S(1)}, u32[]{:S(2)}, u32[]{:S(2)}) %collective-permute-start.28) | collective-permute-done | bytes 786464 | tf_op jit(solution)/shard_map/ppermute | solution.py:109
  294.8 13.2 %collective-permute-done.29 = bf16[192,2048]{1,0:T(8,128)(2,1)S(1)} collective-permute-done((bf16[192,2048]{1,0:T(8,128)(2,1)S(1)}, bf16[192,2048]{1,0:T(8,128)(2,1)S(1)}, u32[]{:S(2)}, u32[]{:S(2)}) %collective-permute-start.29) | collective-permute-done | bytes 786464 | tf_op jit(solution)/shard_map/ppermute | solution.py:109
  313.7 17.0 %fusion.176 = f32[1536,2048]{1,0:T(8,128)} fusion(bf16[1536,2048]{1,0:T(8,128)(2,1)S(1)} %copy-done.68, bf16[384,1536]{1,0:T(8,128)(2,1)S(1)} %collective-permute-done.22, bf16[384,1536]{1,0:T(8,128)(2,1)S(1)} %collective-permute-done.21, bf16[384,1536]{1,0:T(8,128)(2,1)S(1)} %collective-permute-done.20, bf16[384,1536]{1,0:T(8,128)(2,1)S(1)} %fusion.47), kind=kOutput, calls=%fused_computation.319 | convolution fusion | flops 9682550784 | bytes 23592960 | tf_op jit(solution)/shard_map/dot_general | solution.py:57
  330.8 15.0 %multiply_convert_fusion.1 = (bf16[1536,1024]{1,0:T(8,128)(2,1)S(1)}, bf16[1536,1024]{1,0:T(8,128)(2,1)}, bf16[1536,1024]{1,0:T(8,128)(2,1)}) fusion(f32[1536,2048]{1,0:T(8,128)} %fusion.176, bf16[1536,1024]{1,0:T(8,128)(2,1)} %constant_dynamic-update-slice_fusion.31, bf16[384,1536]{1,0:T(8,128)(2,1)} %copy-done.42, bf16[384,1536]{1,0:T(8,128)(2,1)} %copy-done.41, ...), kind=kOutput, calls=%fused_computation.19 | convolution fusion | flops 4875878400 | bytes 29884416 | tf_op jit(solution)/shard_map/dot_general | solution.py:57
  345.7 6.8 fusion.92
  359.8 14.9 %convolution_convert_fusion.1 = bf16[1536,1536]{1,0:T(8,128)(2,1)} fusion(bf16[1536,2048]{1,0:T(8,128)(2,1)} %constant_dynamic-update-slice_fusion.22, bf16[1536,1024]{1,0:T(8,128)(2,1)} %get-tuple-element.19, bf16[1536,1024]{1,0:T(8,128)(2,1)S(1)} %get-tuple-element.18), kind=kOutput, calls=%fused_computation.14 | convolution fusion | flops 9678618624 | bytes 17301504 | tf_op jit(solution)/shard_map/dot_general | solution.py:67
  379.0 7.4 convolution_convert_fusion
  395.9 28.0 %collective-permute-done.59 = bf16[768,1024]{1,0:T(8,128)(2,1)} collective-permute-done((bf16[768,1024]{1,0:T(8,128)(2,1)}, bf16[768,1024]{1,0:T(8,128)(2,1)}, u32[]{:S(2)}, u32[]{:S(2)}) %collective-permute-start.59) | collective-permute-done | bytes 1572896 | tf_op jit(solution)/shard_map/ppermute | solution.py:109
  429.6 24.8 %collective-permute-done.56 = bf16[768,1024]{1,0:T(8,128)(2,1)S(1)} collective-permute-done((bf16[768,1024]{1,0:T(8,128)(2,1)}, bf16[768,1024]{1,0:T(8,128)(2,1)S(1)}, u32[]{:S(2)}, u32[]{:S(2)}) %collective-permute-start.56) | collective-permute-done | bytes 1572896 | tf_op jit(solution)/shard_map/ppermute | solution.py:109
  463.5 22.9 %collective-permute-done.57 = bf16[384,1024]{1,0:T(8,128)(2,1)S(1)} collective-permute-done((bf16[384,1024]{1,0:T(8,128)(2,1)S(1)}, bf16[384,1024]{1,0:T(8,128)(2,1)S(1)}, u32[]{:S(2)}, u32[]{:S(2)}) %collective-permute-start.57) | collective-permute-done | bytes 786464 | tf_op jit(solution)/shard_map/ppermute | solution.py:109
  496.7 9.9 %collective-permute-done.61 = bf16[192,1024]{1,0:T(8,128)(2,1)S(1)} collective-permute-done((bf16[192,1024]{1,0:T(8,128)(2,1)S(1)}, bf16[192,1024]{1,0:T(8,128)(2,1)S(1)}, u32[]{:S(2)}, u32[]{:S(2)}) %collective-permute-start.61) | collective-permute-done | bytes 393248 | tf_op jit(solution)/shard_map/ppermute | solution.py:109
  512.8 29.6 %psum.7 = f32[192]{0:T(256)} all-reduce(f32[192]{0:T(256)} %get-tuple-element.11), channel_id=1, replica_groups=mesh['dp'=8,'tensor'=4] {'tensor'}, use_global_device_ids=true, to_apply=%region_12.13 | all-reduce | flops 192 | bytes 1536 | tf_op jit(solution)/shard_map/psum | solution.py:327
  649.7 69.6 %collective-permute-done.52 = bf16[384,1536]{1,0:T(8,128)(2,1)S(1)} collective-permute-done((bf16[384,1536]{1,0:T(8,128)(2,1)S(1)}, bf16[384,1536]{1,0:T(8,128)(2,1)S(1)}, u32[]{:S(2)}, u32[]{:S(2)}) %collective-permute-start.52) | collective-permute-done | bytes 1179680 | tf_op jit(solution)/shard_map/ppermute | solution.py:109
  739.0 27.2 %collective-permute-done.47 = bf16[192,3072]{1,0:T(8,128)(2,1)S(1)} collective-permute-done((bf16[192,3072]{1,0:T(8,128)(2,1)S(1)}, bf16[192,3072]{1,0:T(8,128)(2,1)S(1)}, u32[]{:S(2)}, u32[]{:S(2)}) %collective-permute-start.47) | collective-permute-done | bytes 1179680 | tf_op jit(solution)/shard_map/ppermute | solution.py:109
  773.4 20.6 %collective-permute-done.48 = bf16[96,3072]{1,0:T(8,128)(2,1)S(1)} collective-permute-done((bf16[96,3072]{1,0:T(8,128)(2,1)S(1)}, bf16[96,3072]{1,0:T(8,128)(2,1)S(1)}, u32[]{:S(2)}, u32[]{:S(2)}) %collective-permute-start.48) | collective-permute-done | bytes 589856 | tf_op jit(solution)/shard_map/ppermute | solution.py:109
  796.5 6.6 collective-permute-done.49
  (471 shorter events, 359.5 us)
Async XLA Ops:
  0.7 112.3 %collective-permute-start.30 = (bf16[192,1024]{1,0:T(8,128)(2,1)}, bf16[192,1024]{1,0:T(8,128)(2,1)}, u32[]{:S(2)}, u32[]{:S(2)}) collective-permute-start(bf16[192,1024]{1,0:T(8,128)(2,1)} %bitcast.152), channel_id=1, source_target_pairs={{0,16},{1,17},{2,18},{3,19},{4,20},{5,21},{6,22},{7,23},{8,24},{9,... | collective-permute-start | bytes 1179656 | tf_op jit(solution)/shard_map/ppermute | solution.py:109
  4.8 109.7 %collective-permute-start.31 = (bf16[192,1024]{1,0:T(8,128)(2,1)}, bf16[192,1024]{1,0:T(8,128)(2,1)}, u32[]{:S(2)}, u32[]{:S(2)}) collective-permute-start(bf16[192,1024]{1,0:T(8,128)(2,1)} %bitcast.153), channel_id=1, source_target_pairs={{0,8},{1,9},{2,10},{3,11},{4,12},{5,13},{6,14},{7,15},{8,0},{9,1},... | collective-permute-start | bytes 1179656 | tf_op jit(solution)/shard_map/ppermute | solution.py:109
  26.1 90.0 %collective-permute-start.11 = (bf16[96,1536]{1,0:T(8,128)(2,1)}, bf16[96,1536]{1,0:T(8,128)(2,1)S(1)}, u32[]{:S(2)}, u32[]{:S(2)}) collective-permute-start(bf16[96,1536]{1,0:T(8,128)(2,1)} %get-tuple-element.42), channel_id=1, source_target_pairs={{0,16},{1,17},{2,18},{3,19},{4,20},{5,21},{6,22},{7,23},{8,24},{9,... | collective-permute-start | bytes 884744 | tf_op jit(solution)/shard_map/ppermute | solution.py:109
  112.1 65.9 %collective-permute-start.8 = (bf16[384,3200]{1,0:T(8,128)(2,1)}, bf16[384,3200]{1,0:T(8,128)(2,1)}, u32[]{:S(2)}, u32[]{:S(2)}) collective-permute-start(bf16[384,3200]{1,0:T(8,128)(2,1)} %constant_dynamic-update-slice_fusion), channel_id=1, source_target_pairs={{0,1},{1,0},{2,3},{3,2},{4,5},{5,4},{6,7},{7,6},{8,9},{9,8},{10,11... | collective-permute-start | bytes 7372808 | tf_op jit(solution)/shard_map/ppermute | solution.py:109
  112.9 66.1 %collective-permute-start.9 = (bf16[384,3200]{1,0:T(8,128)(2,1)}, bf16[384,3200]{1,0:T(8,128)(2,1)}, u32[]{:S(2)}, u32[]{:S(2)}) collective-permute-start(bf16[384,3200]{1,0:T(8,128)(2,1)} %constant_dynamic-update-slice_fusion.5), channel_id=1, source_target_pairs={{0,1},{1,0},{2,3},{3,2},{4,5},{5,4},{6,7},{7,6},{8,9},{9,8},{10,11... | collective-permute-start | bytes 7372808 | tf_op jit(solution)/shard_map/ppermute | solution.py:109
  141.3 103.7 %collective-permute-start.24 = (bf16[192,2048]{1,0:T(8,128)(2,1)}, bf16[192,2048]{1,0:T(8,128)(2,1)}, u32[]{:S(2)}, u32[]{:S(2)}) collective-permute-start(bf16[192,2048]{1,0:T(8,128)(2,1)} %get-tuple-element.35), channel_id=1, source_target_pairs={{0,8},{1,9},{2,10},{3,11},{4,12},{5,13},{6,14},{7,15},{8,0},{9,1},... | collective-permute-start | bytes 2359304 | tf_op jit(solution)/shard_map/ppermute | solution.py:109
  172.3 74.3 %collective-permute-start.26 = (bf16[192,2048]{1,0:T(8,128)(2,1)}, bf16[192,2048]{1,0:T(8,128)(2,1)}, u32[]{:S(2)}, u32[]{:S(2)}) collective-permute-start(bf16[192,2048]{1,0:T(8,128)(2,1)} %get-tuple-element.35), channel_id=1, source_target_pairs={{0,4},{1,5},{2,6},{3,7},{4,0},{5,1},{6,2},{7,3},{8,12},{9,13},{10,... | collective-permute-start | bytes 2359304 | tf_op jit(solution)/shard_map/ppermute | solution.py:109
  174.7 100.2 %collective-permute-start.39 = (bf16[384,1536]{1,0:T(8,128)(2,1)}, bf16[384,1536]{1,0:T(8,128)(2,1)}, u32[]{:S(2)}, u32[]{:S(2)}) collective-permute-start(bf16[384,1536]{1,0:T(8,128)(2,1)} %fusion.57), channel_id=1, source_target_pairs={{0,2},{1,3},{2,0},{3,1},{4,6},{5,7},{6,4},{7,5},{8,10},{9,11},{10,... | collective-permute-start | bytes 3538952 | tf_op jit(solution)/shard_map/ppermute | solution.py:109
  178.0 58.0 %collective-permute-start.18 = (bf16[384,1536]{1,0:T(8,128)(2,1)}, bf16[384,1536]{1,0:T(8,128)(2,1)}, u32[]{:S(2)}, u32[]{:S(2)}) collective-permute-start(bf16[384,1536]{1,0:T(8,128)(2,1)} %constant_dynamic-update-slice_fusion.11), channel_id=1, source_target_pairs={{0,1},{1,0},{2,3},{3,2},{4,5},{5,4},{6,7},{7,6},{8,9},{9,8},{10,11... | collective-permute-start | bytes 3538952 | tf_op jit(solution)/shard_map/ppermute | solution.py:109
  179.1 59.5 %collective-permute-start.19 = (bf16[384,1536]{1,0:T(8,128)(2,1)}, bf16[384,1536]{1,0:T(8,128)(2,1)}, u32[]{:S(2)}, u32[]{:S(2)}) collective-permute-start(bf16[384,1536]{1,0:T(8,128)(2,1)} %constant_dynamic-update-slice_fusion.16), channel_id=1, source_target_pairs={{0,1},{1,0},{2,3},{3,2},{4,5},{5,4},{6,7},{7,6},{8,9},{9,8},{10,11... | collective-permute-start | bytes 3538952 | tf_op jit(solution)/shard_map/ppermute | solution.py:109
  249.3 44.0 %collective-permute-start.20 = (bf16[384,1536]{1,0:T(8,128)(2,1)S(1)}, bf16[384,1536]{1,0:T(8,128)(2,1)S(1)}, u32[]{:S(2)}, u32[]{:S(2)}) collective-permute-start(bf16[384,1536]{1,0:T(8,128)(2,1)S(1)} %fusion.47), channel_id=1, source_target_pairs={{0,2},{1,3},{2,0},{3,1},{4,6},{5,7},{6,4},{7,5},{8,10},{9,11},{10,... | collective-permute-start | bytes 3538952 | tf_op jit(solution)/shard_map/ppermute | solution.py:109
  358.3 65.6 %collective-permute-start.59 = (bf16[768,1024]{1,0:T(8,128)(2,1)}, bf16[768,1024]{1,0:T(8,128)(2,1)}, u32[]{:S(2)}, u32[]{:S(2)}) collective-permute-start(bf16[768,1024]{1,0:T(8,128)(2,1)} %fusion.89), channel_id=1, source_target_pairs={{0,4},{1,5},{2,6},{3,7},{4,0},{5,1},{6,2},{7,3},{8,12},{9,13},{10,... | collective-permute-start | bytes 4718600 | tf_op jit(solution)/shard_map/ppermute | solution.py:109
  378.4 76.0 %collective-permute-start.56 = (bf16[768,1024]{1,0:T(8,128)(2,1)}, bf16[768,1024]{1,0:T(8,128)(2,1)S(1)}, u32[]{:S(2)}, u32[]{:S(2)}) collective-permute-start(bf16[768,1024]{1,0:T(8,128)(2,1)} %fusion.86), channel_id=1, source_target_pairs={{0,4},{1,5},{2,6},{3,7},{4,0},{5,1},{6,2},{7,3},{8,12},{9,13},{10,... | collective-permute-start | bytes 4718600 | tf_op jit(solution)/shard_map/ppermute | solution.py:109
  386.6 100.5 %collective-permute-start.42 = (bf16[768,1536]{1,0:T(8,128)(2,1)S(1)}, bf16[768,1536]{1,0:T(8,128)(2,1)}, u32[]{:S(2)}, u32[]{:S(2)}) collective-permute-start(bf16[768,1536]{1,0:T(8,128)(2,1)S(1)} %slice.327), channel_id=1, source_target_pairs={{0,1},{1,0},{2,3},{3,2},{4,5},{5,4},{6,7},{7,6},{8,9},{9,8},{10,11... | collective-permute-start | bytes 7077896 | tf_op jit(solution)/shard_map/ppermute | solution.py:109
  386.8 104.9 %collective-permute-start.37 = (bf16[768,1536]{1,0:T(8,128)(2,1)S(1)}, bf16[768,1536]{1,0:T(8,128)(2,1)}, u32[]{:S(2)}, u32[]{:S(2)}) collective-permute-start(bf16[768,1536]{1,0:T(8,128)(2,1)S(1)} %slice.323), channel_id=1, source_target_pairs={{0,1},{1,0},{2,3},{3,2},{4,5},{5,4},{6,7},{7,6},{8,9},{9,8},{10,11... | collective-permute-start | bytes 7077896 | tf_op jit(solution)/shard_map/ppermute | solution.py:109
  394.5 64.5 %collective-permute-start.63 = (bf16[384,1024]{1,0:T(8,128)(2,1)S(1)}, bf16[384,1024]{1,0:T(8,128)(2,1)S(1)}, u32[]{:S(2)}, u32[]{:S(2)}) collective-permute-start(bf16[384,1024]{1,0:T(8,128)(2,1)S(1)} %slice.497), channel_id=1, source_target_pairs={{0,8},{1,9},{2,10},{3,11},{4,12},{5,13},{6,14},{7,15},{8,0},{9,1},... | collective-permute-start | bytes 2359304 | tf_op jit(solution)/shard_map/ppermute | solution.py:109
  460.1 83.6 %collective-permute-start.64 = (bf16[192,1024]{1,0:T(8,128)(2,1)}, bf16[192,1024]{1,0:T(8,128)(2,1)}, u32[]{:S(2)}, u32[]{:S(2)}) collective-permute-start(bf16[192,1024]{1,0:T(8,128)(2,1)} %slice.503), channel_id=1, source_target_pairs={{0,16},{1,17},{2,18},{3,19},{4,20},{5,21},{6,22},{7,23},{8,24},{9,... | collective-permute-start | bytes 1179656 | tf_op jit(solution)/shard_map/ppermute | solution.py:109
  460.9 45.7 %collective-permute-start.61 = (bf16[192,1024]{1,0:T(8,128)(2,1)S(1)}, bf16[192,1024]{1,0:T(8,128)(2,1)S(1)}, u32[]{:S(2)}, u32[]{:S(2)}) collective-permute-start(bf16[192,1024]{1,0:T(8,128)(2,1)S(1)} %slice.504), channel_id=1, source_target_pairs={{0,16},{1,17},{2,18},{3,19},{4,20},{5,21},{6,22},{7,23},{8,24},{9,... | collective-permute-start | bytes 1179656 | tf_op jit(solution)/shard_map/ppermute | solution.py:109
  489.6 56.4 %collective-permute-start.43 = (bf16[384,1536]{1,0:T(8,128)(2,1)S(1)}, bf16[384,1536]{1,0:T(8,128)(2,1)}, u32[]{:S(2)}, u32[]{:S(2)}) collective-permute-start(bf16[384,1536]{1,0:T(8,128)(2,1)S(1)} %slice.495), channel_id=1, source_target_pairs={{0,2},{1,3},{2,0},{3,1},{4,6},{5,7},{6,4},{7,5},{8,10},{9,11},{10,... | collective-permute-start | bytes 3538952 | tf_op jit(solution)/shard_map/ppermute | solution.py:109
  495.3 271.8 %collective-permute-start.38 = (bf16[384,1536]{1,0:T(8,128)(2,1)}, bf16[384,1536]{1,0:T(8,128)(2,1)}, u32[]{:S(2)}, u32[]{:S(2)}) collective-permute-start(bf16[384,1536]{1,0:T(8,128)(2,1)} %slice.496), channel_id=1, source_target_pairs={{0,2},{1,3},{2,0},{3,1},{4,6},{5,7},{6,4},{7,5},{8,10},{9,11},{10,... | collective-permute-start | bytes 3538952 | tf_op jit(solution)/shard_map/ppermute | solution.py:109
  625.7 95.8 %collective-permute-start.44 = (bf16[384,3072]{1,0:T(8,128)(2,1)S(1)}, bf16[384,3072]{1,0:T(8,128)(2,1)S(1)}, u32[]{:S(2)}, u32[]{:S(2)}) collective-permute-start(bf16[384,3072]{1,0:T(8,128)(2,1)S(1)} %convolution_convert_fusion.3), channel_id=1, source_target_pairs={{0,1},{1,0},{2,3},{3,2},{4,5},{5,4},{6,7},{7,6},{8,9},{9,8},{10,11... | collective-permute-start | bytes 7077896 | tf_op jit(solution)/shard_map/ppermute | solution.py:109
  640.5 80.9 %collective-permute-start.46 = (bf16[384,3072]{1,0:T(8,128)(2,1)S(1)}, bf16[384,3072]{1,0:T(8,128)(2,1)S(1)}, u32[]{:S(2)}, u32[]{:S(2)}) collective-permute-start(bf16[384,3072]{1,0:T(8,128)(2,1)S(1)} %add_convert_fusion), channel_id=1, source_target_pairs={{0,2},{1,3},{2,0},{3,1},{4,6},{5,7},{6,4},{7,5},{8,10},{9,11},{10,... | collective-permute-start | bytes 7077896 | tf_op jit(solution)/shard_map/ppermute | solution.py:109
  642.2 77.1 %collective-permute-start.52 = (bf16[384,1536]{1,0:T(8,128)(2,1)S(1)}, bf16[384,1536]{1,0:T(8,128)(2,1)S(1)}, u32[]{:S(2)}, u32[]{:S(2)}) collective-permute-start(bf16[384,1536]{1,0:T(8,128)(2,1)S(1)} %add_convert_fusion.3), channel_id=1, source_target_pairs={{0,2},{1,3},{2,0},{3,1},{4,6},{5,7},{6,4},{7,5},{8,10},{9,11},{10,... | collective-permute-start | bytes 3538952 | tf_op jit(solution)/shard_map/ppermute | solution.py:109
  722.8 43.4 %collective-permute-start.47 = (bf16[192,3072]{1,0:T(8,128)(2,1)S(1)}, bf16[192,3072]{1,0:T(8,128)(2,1)S(1)}, u32[]{:S(2)}, u32[]{:S(2)}) collective-permute-start(bf16[192,3072]{1,0:T(8,128)(2,1)S(1)} %slice.494), channel_id=1, source_target_pairs={{0,8},{1,9},{2,10},{3,11},{4,12},{5,13},{6,14},{7,15},{8,0},{9,1},... | collective-permute-start | bytes 3538952 | tf_op jit(solution)/shard_map/ppermute | solution.py:109
  (124 other events, 2424.5 us)

commit v2 on v1

v2 whole, which is shorter than its diff:
```python
import functools
import math

import jax
import jax.numpy as jnp
from jax import lax
from jax.experimental import pallas as pl
from jax.experimental.pallas import tpu as pltpu
from jax.sharding import PartitionSpec as P

HEADS = 16
KV_HEADS = 8
HEAD = 96
SLOTS = 6
GROUP = HEADS // KV_HEADS
LANES = 128

EPSILON = 1e-05
ROPE_BASE = 100000.0
NEG_LARGE = -1e30
AXES = ("dp", "tensor")
bf16 = jnp.bfloat16
f32 = jnp.float32


def pack_layout(seq_lengths, row_count):
    seq_ends = jnp.cumsum(seq_lengths)
    seq_starts = seq_ends - seq_lengths
    row_index = jnp.arange(row_count, dtype=jnp.int32)
    segment = jnp.sum((row_index[:, None] >= seq_ends[None, :]).astype(jnp.int32), axis=1)
    owner_hot = segment[:, None] == jnp.arange(seq_lengths.shape[0], dtype=jnp.int32)[None, :]
    position = row_index - jnp.sum(jnp.where(owner_hot, seq_starts[None, :], 0), axis=1)
    return (segment, position)


def rotary_tables(position, head_size):
    half_size = head_size // 2
    freq_index = jnp.arange(half_size, dtype=f32)
    inverse = jnp.exp(freq_index * (-2.0 / head_size) * math.log(ROPE_BASE))
    angles = position.astype(f32)[..., None] * inverse
    return (jnp.cos(angles), jnp.sin(angles))


def product(left_side, right_side):
    return jnp.dot(left_side, right_side, preferred_element_type=f32)


def across(left_side, right_side):
    return lax.dot_general(
        left_side, right_side, (((0,), (0,)), ((), ())), preferred_element_type=f32
    )


def against(left_side, right_side):
    return lax.dot_general(
        left_side, right_side, (((1,), (1,)), ((), ())), preferred_element_type=f32
    )


def bits_of(size):
    return [1 << k for k in range(size.bit_length() - 1)]


def rel_source(me, masks, block, count):
    place = jnp.arange(count, dtype=jnp.int32)
    step = place // block
    delta = jnp.zeros_like(step)
    for k, mask in enumerate(masks):
        delta = delta + ((step >> k) & 1) * mask
    return (me ^ delta) * block + place % block


def one_hot(source):
    count = source.shape[0]
    rows = lax.broadcasted_iota(jnp.int32, (count, count), 0)
    return (rows == source[None, :]).astype(bf16)


def join(parts):
    return parts[0] if len(parts) == 1 else jnp.concatenate(parts, axis=0)


BAND = 4 * HEAD


def turn(array, cosine, sine_part):
    lane = lax.broadcasted_iota(jnp.int32, array.shape, 1)
    swapped = jnp.where(
        lane % HEAD < HEAD // 2,
        pltpu.roll(array, BAND - HEAD // 2, 1),
        pltpu.roll(array, HEAD // 2, 1),
    )
    return array * cosine + swapped * sine_part


def head_masks():
    lane = lax.broadcasted_iota(jnp.int32, (1, BAND), 1)
    return [jnp.where(lane // HEAD == h, 1.0, 0.0) for h in range(4)]


def stack_heads(bands, masks):
    return jnp.concatenate([band * mask.astype(bf16) for band in bands for mask in masks], axis=0)


def unstack_heads(stacked, masks, per_pack):
    found = []
    for g in range(GROUP):
        total = 0.0
        for h in range(4):
            first = (g * 4 + h) * per_pack
            total = total + stacked[first : first + per_pack] * masks[h]
        found.append(total)
    return found


def pack_probs(stacked, keys, allowed):
    per_pack = keys.shape[0]
    scores = against(stacked, keys) * (1.0 / math.sqrt(HEAD))
    scores = scores.reshape(-1, per_pack, per_pack)
    peak = jnp.max(jnp.where(allowed, scores, NEG_LARGE), axis=-1, keepdims=True)
    raised = jnp.where(allowed, jnp.exp(jnp.where(allowed, scores - peak, 0.0)), 0.0)
    totals = jnp.sum(raised, axis=-1, keepdims=True)
    return raised / jnp.where(totals > 0, totals, 1.0)


def columns(band):
    return pl.ds(band * BAND, BAND)


def piece_rows(pieces, place, mixed):
    if not mixed:
        return jnp.concatenate([piece[:, place] for piece in pieces], axis=0)
    n = pieces[0].shape[0] // 2
    found = []
    for a, b in (pieces[:2], pieces[2:]):
        for k in (slice(0, n), slice(n, 2 * n)):
            found += [a[k, place], b[k, place]]
    return jnp.concatenate(found, axis=0)


def forward_kernel(micro, per_pack, kv_bands, *refs):
    x_ref, cos_ref, sin_ref, mask_ref, *piece_refs = refs[:-4]
    qkv_ref, att_ref, n1_ref, gains_ref = refs[-4:]
    q_bands = GROUP * kv_bands
    q_refs, kv_refs = piece_refs[:4], piece_refs[4:]
    tail = pl.ds(2 * kv_bands * BAND, LANES)
    gains = jnp.transpose(piece_rows(kv_refs, tail, False).astype(f32))
    gains_ref[...] = gains[: gains_ref.shape[0]]
    inputs = x_ref[...].astype(f32)
    scale = lax.rsqrt(jnp.mean(inputs * inputs, axis=1, keepdims=True) + EPSILON)
    n1_ref[...] = (inputs * scale * gains[:1]).astype(bf16)
    for band in range(q_bands + 2 * kv_bands):
        in_q = band < q_bands
        place = columns(band if in_q else band - q_bands)
        total = product(n1_ref[...], piece_rows(q_refs if in_q else kv_refs, place, in_q))
        if band < q_bands + kv_bands:
            total = turn(total, cos_ref[...], sin_ref[...])
        qkv_ref[:, columns(band)] = total.astype(bf16)

    masks = head_masks()

    def one_pack(pack, carry):
        rows = pl.ds(pl.multiple_of(pack * per_pack, per_pack), per_pack)
        allowed = (mask_ref[pl.ds(pack, 1)] > 0.0)
        for j in range(kv_bands):
            bands = [g * kv_bands + j for g in range(GROUP)]
            stacked = stack_heads([qkv_ref[rows, columns(b)] for b in bands], masks)
            keys = qkv_ref[rows, columns(q_bands + j)]
            values = qkv_ref[rows, columns(q_bands + kv_bands + j)]
            probs = pack_probs(stacked, keys, allowed)
            mixed = product(probs.astype(bf16).reshape(-1, per_pack), values)
            for b, band in zip(bands, unstack_heads(mixed, masks, per_pack)):
                att_ref[rows, columns(b)] = band.astype(bf16)
        return carry

    lax.fori_loop(0, micro, one_pack, 0)


def pack_kernel(q_ref, k_ref, v_ref, gains_ref, o_ref, out_ref):
    heads = [
        q_ref[:, (k * GROUP + g) * HEAD : (k * GROUP + g + 1) * HEAD]
        for g in range(GROUP)
        for k in range(KV_HEADS)
    ]
    first = 0
    for piece in (
        jnp.concatenate(heads, axis=1), k_ref[...], v_ref[...], gains_ref[...], o_ref[...]
    ):
        out_ref[:, first : first + piece.shape[1]] = piece
        first += piece.shape[1]


def backward_kernel(micro, per_pack, kv_bands, *refs):
    dmb_ref, qkv_ref, cos_ref, sin_ref, mask_ref, pick_ref, *out_refs = refs[:8]
    dqkv_ref, datt_ref = refs[-2:]
    half = pick_ref.shape[1] // 2
    datt = 0.0
    for k, piece in enumerate(out_refs):
        part = against(dmb_ref[...], piece[...]).astype(bf16)
        datt = datt + against(part, pick_ref[:, k * half : (k + 1) * half])
    datt_ref[...] = datt.astype(bf16)
    q_bands = GROUP * kv_bands
    factor = 1.0 / math.sqrt(HEAD)
    masks = head_masks()

    def one_pack(pack, carry):
        rows = pl.ds(pl.multiple_of(pack * per_pack, per_pack), per_pack)
        allowed = (mask_ref[pl.ds(pack, 1)] > 0.0)
        cosine, sine_part = cos_ref[rows, :], -sin_ref[rows, :]
        for j in range(kv_bands):
            bands = [g * kv_bands + j for g in range(GROUP)]
            stacked = stack_heads([qkv_ref[rows, columns(b)] for b in bands], masks)
            keys = qkv_ref[rows, columns(q_bands + j)]
            values = qkv_ref[rows, columns(q_bands + kv_bands + j)]
            grads = stack_heads([datt_ref[rows, columns(b)] for b in bands], masks)
            probs = pack_probs(stacked, keys, allowed)
            dprob = against(grads, values).reshape(probs.shape)
            delta = jnp.sum(probs * dprob, axis=-1, keepdims=True)
            dscore = (probs * (dprob - delta)).astype(bf16).reshape(-1, per_pack)
            dvalue = across(probs.astype(bf16).reshape(-1, per_pack), grads)
            dkey = turn(across(dscore, stacked) * factor, cosine, sine_part)
            dquery = product(dscore, keys) * factor
            for b, band in zip(bands, unstack_heads(dquery, masks, per_pack)):
                dqkv_ref[rows, columns(b)] = turn(band, cosine, sine_part).astype(bf16)
            dqkv_ref[rows, columns(q_bands + j)] = dkey.astype(bf16)
            dqkv_ref[rows, columns(q_bands + kv_bands + j)] = dvalue.astype(bf16)
        return carry

    lax.fori_loop(0, micro, one_pack, 0)


def mlp_kernel(ff, *refs):
    n2_ref, dy_ref, gu_ref, down_ref = refs[:4]
    hidden_ref, dgu_ref, *dn2_refs = refs[-4:]
    both = product(n2_ref[...], gu_ref[...])
    gate, up = both[:, :ff], both[:, ff:]
    dhid = product(dy_ref[...], down_ref[...])
    sig = jax.nn.sigmoid(gate)
    passed = gate * sig
    hidden_ref[...] = (passed * up).astype(bf16)
    dgu_ref[:, :ff] = (dhid * up * sig * (1.0 + gate * (1.0 - sig))).astype(bf16)
    dgu_ref[:, ff:] = (dhid * passed).astype(bf16)
    dn2 = against(dgu_ref[...], gu_ref[...]).astype(bf16)
    put_by_step(dn2_refs, [dn2] * 2)


def put_by_step(refs, values):
    for k, (ref, value) in enumerate(zip(refs, values)):

        @pl.when(pl.program_id(0) == k)
        def _(ref=ref, value=value):
            ref[...] = value.astype(ref.dtype)


def shape_of(rows, columns, kind):
    return jax.ShapeDtypeStruct((rows, columns), kind)


def estimate(flops):
    return pl.CostEstimate(flops=100000000000, bytes_accessed=0, transcendentals=0)


LIMIT = pltpu.CompilerParams(vmem_limit_bytes=56 * 1024 * 1024)
ANYWHERE = pl.BlockSpec(memory_space=pl.ANY)


def fixed(rows, columns, row=0, column=0):
    return pl.BlockSpec((rows, columns), lambda i: (row, column))


def mlp_call(first, n2, dy, gu, down, *earlier):
    rows, width = n2.shape
    ff = down.shape[1]
    block = rows // 4

    def band(columns):
        return pl.BlockSpec((block, columns), lambda i: (first + i, 0))

    return pl.pallas_call(
        functools.partial(mlp_kernel, ff),
        grid=(2,),
        in_specs=[band(width), band(width), fixed(*gu.shape), fixed(*down.shape)]
        + [ANYWHERE] * len(earlier),
        out_specs=[band(ff), band(2 * ff), fixed(block, width), fixed(block, width)],
        out_shape=[shape_of(rows, ff, bf16), shape_of(rows, 2 * ff, bf16)]
        + [shape_of(block, width, bf16)] * 2,
        input_output_aliases={4 + k: k for k in range(len(earlier) - 1)},
        compiler_params=LIMIT,
        cost_estimate=estimate(10 * 2 * block * width * ff),
    )(n2, dy, gu, down, *earlier)


def sent_kernel(left_ref, right_ref, token_ref, out_ref):
    out_ref[...] = across(left_ref[...], right_ref[...]).astype(bf16)


def sent_call(left, right, at, columns, token):
    count, width = left.shape
    block = width // 4
    return pl.pallas_call(
        sent_kernel,
        grid=(2,),
        in_specs=[
            pl.BlockSpec((count, block), lambda i: (0, 2 + i)),
            fixed(count, columns, 0, at // columns),
            ANYWHERE,
        ],
        out_specs=pl.BlockSpec((block, columns), lambda i: (i, 0)),
        out_shape=shape_of(2 * block, columns, bf16),
        compiler_params=LIMIT,
        cost_estimate=estimate(4 * count * block * columns),
    )(left, right, token)


def kept_kernel(left_ref, right_ref, got_ref, token_ref, keep_ref, send_ref):
    total = across(left_ref[...], right_ref[...]) + got_ref[...].astype(f32)
    put_by_step((keep_ref, send_ref), (total, total))


def kept_call(left, right, at, columns, got, token):
    count, width = left.shape
    block = width // 4
    return pl.pallas_call(
        kept_kernel,
        grid=(2,),
        in_specs=[
            pl.BlockSpec((count, block), lambda i: (0, i)),
            fixed(count, columns, 0, at // columns),
            pl.BlockSpec((block, columns), lambda i: (i, 0)),
            ANYWHERE,
        ],
        out_specs=[fixed(block, columns)] * 2,
        out_shape=[shape_of(block, columns, f32), shape_of(block, columns, bf16)],
        compiler_params=LIMIT,
        cost_estimate=estimate(4 * count * block * columns),
    )(left, right, got, token)


def sum_kernel(count, *refs):
    total = 0.0
    for ref in refs[:count]:
        total = total + ref[...].astype(f32)
    outs = refs[count + 1 :]
    rows = total.shape[0] // len(outs)
    for k, out in enumerate(outs):
        out[...] = total[k * rows : (k + 1) * rows].astype(out.dtype)


def sum_call(arrays, kinds, token):
    rows, columns = arrays[0].shape
    block = columns // 2 if columns % 256 == 0 else columns
    part = rows // len(kinds)
    return pl.pallas_call(
        functools.partial(sum_kernel, len(arrays)),
        grid=(columns // block,),
        in_specs=[pl.BlockSpec((rows, block), lambda i: (0, i))] * len(arrays) + [ANYWHERE],
        out_specs=[pl.BlockSpec((part, block), lambda i: (0, i))] * len(kinds),
        out_shape=[shape_of(part, columns, kind) for kind in kinds],
        compiler_params=LIMIT,
        cost_estimate=estimate(rows * columns),
    )(*arrays, token)


def norm_back(upstream, signal, gain):
    inverse = lax.rsqrt(jnp.mean(signal * signal, axis=1, keepdims=True) + EPSILON)
    weighted = upstream * gain
    mixed = jnp.mean(weighted * signal, axis=1, keepdims=True)
    return inverse * weighted - signal * (inverse * inverse * inverse) * mixed


def second_norm_kernel(*refs):
    near_ref, core_ref, x_ref, pick_ref, dy_ref, middle_ref, gain_ref, _ = refs[:8]
    dmid_ref, dmb_ref = refs[8:]
    dn2 = near_ref[...].astype(f32) + core_ref[...].astype(f32) + x_ref[...].astype(f32)
    dn2 = against(dn2.astype(bf16), pick_ref[...])
    dmid = dy_ref[...].astype(f32) + norm_back(dn2, middle_ref[...], gain_ref[...])
    dmid_ref[...] = dmid
    dmb_ref[...] = dmid.astype(bf16)


def first_norm_kernel(band, *refs):
    dqkv_ref, x_ref, gains_ref, pick_ref, dmid_ref, *piece_refs = refs[:-2]
    out_ref = refs[-1]
    dn1 = 0.0
    bands = dqkv_ref.shape[1] // band
    for k in range(bands):
        in_q = k < bands // 2
        place = pl.ds((k if in_q else k - bands // 2) * band, band)
        found = piece_rows(piece_refs[:4] if in_q else piece_refs[4:], place, in_q)
        dn1 = dn1 + against(dqkv_ref[:, pl.ds(k * band, band)], found)
    part = norm_back(dn1, x_ref[...].astype(f32), gains_ref[:1])
    high = part.astype(bf16)
    low = (part - high.astype(f32)).astype(bf16)
    out_ref[...] = dmid_ref[...] + against(high, pick_ref[...]) + against(low, pick_ref[...])


def down_kernel(hidden_ref, down_ref, token_ref, *out_refs):
    rows = against(hidden_ref[...], down_ref[...])
    put_by_step(out_refs, [rows] * 4)


def down_call(hidden, down, token):
    rows, ff = hidden.shape
    width, block = down.shape[0], hidden.shape[0] // 4
    return pl.pallas_call(
        down_kernel,
        grid=(4,),
        in_specs=[pl.BlockSpec((block, ff), lambda i: (i, 0)), fixed(width, ff), ANYWHERE],
        out_specs=[fixed(block, width)] * 4,
        out_shape=[shape_of(block, width, bf16)] * 4,
        compiler_params=LIMIT,
        cost_estimate=estimate(2 * rows * width * ff),
    )(hidden, down, token)


def layer_kernel(own_ref, core_ref, x_ref, pick_ref, middle_ref, token_ref, out_ref):
    total = own_ref[...].astype(f32) + core_ref[...].astype(f32) + x_ref[...].astype(f32)
    total = middle_ref[...] + against(total.astype(bf16), pick_ref[...])
    out_ref[...] = total.astype(bf16)


def kernel_call(body, outs, cost, *args, token=None, scratch=()):
    tokens = () if token is None else (token,)
    return pl.pallas_call(
        body,
        out_shape=outs,
        in_specs=[pl.BlockSpec(memory_space=pltpu.VMEM)] * len(args) + [ANYWHERE] * len(tokens),
        out_specs=[pl.BlockSpec(memory_space=pltpu.VMEM)] * len(outs),
        scratch_shapes=list(scratch),
        compiler_params=LIMIT,
        cost_estimate=cost,
    )(*args, *tokens)


def after(array, *others):
    return lax.optimization_barrier((array,) + others)[0]


def together(*arrays):
    return lax.optimization_barrier(arrays)


def program(sizes):
    dp_n, tp_n = sizes["dp"], sizes["tensor"]
    world = dp_n * tp_n

    def swap(array, mask):
        return lax.ppermute(array, AXES, [(i, i ^ mask) for i in range(world)])

    dp_bits = [m * tp_n for m in bits_of(dp_n)]
    y_mask, z_masks = dp_bits[0], dp_bits[:0:-1]
    t_masks = bits_of(tp_n)[::-1]
    x_mask, core_mask = t_masks
    attn_masks = z_masks + [y_mask, x_mask, core_mask]
    mlp_masks = z_masks + [y_mask]

    def gather_far(own):
        if len(z_masks) == 2:
            one, two = z_masks
            return [own, swap(own, one), swap(own, two), swap(own, one ^ two)]
        held = own
        for mask in z_masks:
            held = join([held, swap(held, mask)])
        return [held]

    def finish(pair, token):
        (total,) = sum_call(pair, [f32], token)
        for mask in z_masks[:-2][::-1]:
            n = total.shape[0] // 2
            total = total[:n] + swap(total[n:].astype(bf16), mask).astype(f32)
        return total

    def per_device(
        tokens,
        lengths,
        first_gain,
        query_weight,
        key_weight,
        value_weight,
        output_weight,
        second_gain,
        gate_weight,
        up_weight,
        down_weight,
        cotangent,
    ):
        micro, per_pack, width = tokens.shape
        rows = micro * per_pack
        qw, kw = query_weight.shape[1], key_weight.shape[1]
        ff = gate_weight.shape[1]
        wide = qw + 2 * kw
        shard = query_weight.shape[0]
        dp_i, t_i = lax.axis_index("dp"), lax.axis_index("tensor")
        me = dp_i * tp_n + t_i

        x_low = tokens.reshape(rows, width)
        dy_low = cotangent.reshape(rows, width)
        half, quarter = width // 2, width // 4

        gains = jnp.pad(
            jnp.stack([first_gain, second_gain], axis=1), ((0, 0), (0, LANES - 2))
        )
        (own_attn,) = kernel_call(
            pack_kernel,
            [jax.ShapeDtypeStruct((shard, 2 * qw + 2 * kw + LANES), bf16)],
            None,
            query_weight,
            key_weight,
            value_weight,
            gains,
            output_weight,
        )
        own_gu = jnp.concatenate([gate_weight, up_weight], axis=1)
        own_down = down_weight.T
        own_mlp = jnp.concatenate([own_gu, own_down], axis=1)

        attn_source = rel_source(me, attn_masks, shard, width)
        pick_attn = one_hot(attn_source)
        head, lane = attn_source // HEAD, attn_source % HEAD
        pick_out = one_hot((head % GROUP * KV_HEADS + head // GROUP) * HEAD + lane)
        pick_mlp = one_hot(
            rel_source(dp_i, [m // tp_n for m in mlp_masks], shard * tp_n, width)
        )

        def order(array, pick):
            return product(array, pick).astype(bf16)

        def restore(array, pick):
            return against(array, pick)

        def middle_swap(array):
            n = array.shape[0] // 4
            return join([array[:n], array[2 * n : 3 * n], array[n : 2 * n], array[3 * n :]])

        dy_rel = order(after(dy_low, own_attn), pick_mlp)
        *far, mlp_y, dy_x = together(
            *gather_far(own_attn), swap(own_mlp, y_mask), swap(dy_rel, x_mask)
        )
        cut_q, cut_kv = slice(0, qw), slice(qw, qw + 2 * kw + LANES)
        edge = cut_kv.stop + width // 2
        cut_left, cut_right = slice(cut_kv.stop, edge), slice(edge, None)
        q_four, kv_four, left_four, right_four = [
            join([piece[:, cut] for piece in far]) for cut in (cut_q, cut_kv, cut_left, cut_right)
        ]

        q_x, kv_y, left_x, right_y, down_z = together(
            swap(q_four, x_mask),
            swap(kv_four, y_mask),
            swap(left_four, x_mask),
            swap(right_four, y_mask),
            swap(after(own_down, q_four), z_masks[0]),
        )
        q_eight = join([q_four, q_x])
        kv_eight = join([kv_four, kv_y])

        q_y, kv_x, q_c, kv_c, gu_z = together(
            swap(q_eight, y_mask),
            swap(kv_eight, x_mask),
            swap(q_eight, core_mask),
            swap(kv_eight, core_mask),
            swap(after(own_gu, q_x), z_masks[0]),
        )

        left_eight = join([left_four, left_x])
        right_eight = join([right_four, right_y])
        left_y = swap(after(left_eight, q_y), y_mask)
        right_x = swap(after(right_eight, q_y), x_mask)
        q_yc, kv_xc = together(swap(q_y, core_mask), swap(kv_x, core_mask))
        q_pieces = [q_eight, q_y, q_c, q_yc]
        kv_pieces = [kv_eight, kv_x, kv_c, kv_xc]

        def next_far(own, first):
            held, came = join([own, first]), [first]
            for mask in z_masks[1:]:
                came.append(swap(held, mask))
                held = join([held, came[-1]])
            return held, came

        gu_near, gu_came = next_far(own_gu, gu_z)
        gu_y1 = swap(gu_z, y_mask)
        down_y1 = swap(down_z, y_mask)

        segment, position = jax.vmap(lambda own: pack_layout(own, per_pack))(lengths[:, 0])
        cosine, sine_part = rotary_tables(position, HEAD)
        row_index = jnp.arange(per_pack, dtype=jnp.int32)
        allowed = (
            (segment[:, :, None] == segment[:, None, :])
            & (row_index[None, None, :] <= row_index[None, :, None])
            & (segment < SLOTS - 1)[:, :, None]
        ).astype(f32)

        inputs = x_low.astype(f32)
        r1 = lax.rsqrt(jnp.mean(inputs * inputs, axis=1, keepdims=True) + EPSILON)
        x_rel = order(x_low, pick_attn)
        half_tables = (cosine.reshape(rows, -1), sine_part.reshape(rows, -1))
        cos_band = jnp.tile(half_tables[0], (1, BAND // half_tables[0].shape[1]))
        sin_band = jnp.tile(jnp.concatenate([-half_tables[1], half_tables[1]], axis=1), (1, 4))
        kv_bands = kw // BAND
        shapes = (micro, per_pack, kv_bands)
        cost = pl.CostEstimate(
            flops=100000000000, bytes_accessed=0, transcendentals=0
        )
        qkv, attended, n1_rel, gains_rel = kernel_call(
            functools.partial(forward_kernel, *shapes),
            [
                jax.ShapeDtypeStruct((rows, wide), bf16),
                jax.ShapeDtypeStruct((rows, qw), bf16),
                jax.ShapeDtypeStruct((rows, width), bf16),
                jax.ShapeDtypeStruct((8, width), f32),
            ],
            cost,
            x_rel,
            cos_band,
            sin_band,
            allowed,
            *q_pieces,
            *kv_pieces,
        )
        g1_rel = gains_rel[:1]
        g2 = restore(gains_rel[1:2].astype(bf16), pick_attn)
        n1_parts = [n1_rel[:, :half], n1_rel[:, half:]]

        left_16 = middle_swap(join([left_eight, left_y]))
        right_16 = join([right_eight, right_x])
        out_16 = jnp.concatenate([left_16, right_16], axis=1)
        out_pieces = [out_16, swap(out_16, core_mask)]
        dy_near = join([dy_rel, dy_x])
        dy_c = swap(after(dy_near, attended), core_mask)

        att_rel = order(attended, pick_out)
        att_parts = [att_rel[:, :half], att_rel[:, half:]]
        middle = inputs + sum(product(a, b) for a, b in zip(att_parts, out_pieces))
        r2 = lax.rsqrt(jnp.mean(middle * middle, axis=1, keepdims=True) + EPSILON)
        n2 = (middle * r2 * g2).astype(bf16)

        n2_rel = after(order(n2, pick_mlp), *gu_came, gu_y1, down_y1)
        n2_x = swap(n2_rel, x_mask)
        n2_c = swap(n2_rel, core_mask)
        down_near, down_came = next_far(own_down, after(down_z, n2_rel))
        gu_full = join(
            [gu_near, mlp_y[:, : 2 * ff], gu_y1] + [swap(a, y_mask) for a in gu_came[1:]]
        )
        down_full = join(
            [down_near, mlp_y[:, 2 * ff :], down_y1] + [swap(a, y_mask) for a in down_came[1:]]
        )
        n2_all = join([n2_rel, n2_c, n2_x, swap(n2_x, core_mask)])
        dy_all = join([dy_rel, dy_c[:rows], dy_x, dy_c[rows:]])

        *grown, far_own, far_send = mlp_call(2, n2_all, dy_all, gu_full, down_full, n2_all)
        far_c = swap(far_send, core_mask)
        (dn2_sum,) = sum_call([far_own, far_c], [bf16], far_own)
        dn2_x = swap(dn2_sum, x_mask)
        hidden, dgu, near_own, near_send = mlp_call(
            0, n2_all, dy_all, gu_full, down_full, *grown, dn2_sum
        )
        near_c = swap(near_send, core_mask)
        down_b = sent_call(dy_all, hidden, 0, ff, near_own)
        down_got = swap(down_b, y_mask)

        dmid, dmb = kernel_call(
            second_norm_kernel,
            [shape_of(rows, width, f32), shape_of(rows, width, bf16)],
            estimate(4 * rows * width * width),
            near_own,
            near_c,
            dn2_x,
            pick_mlp,
            dy_low,
            middle,
            g2,
            token=down_b,
        )
        og_b = sent_call(att_rel, dmb, 0, width, dmb)
        og_c = swap(og_b, core_mask)
        gate_b = sent_call(n2_all, dgu, 0, ff, og_b)
        gate_got = swap(gate_b, y_mask)
        og = kept_call(att_rel, dmb, 0, width, og_c, gate_b)
        og_x = swap(og[1], x_mask)
        (dqkv,) = kernel_call(
            functools.partial(backward_kernel, *shapes),
            [shape_of(rows, wide, bf16)],
            cost,
            dmb,
            qkv,
            cos_band,
            sin_band,
            allowed,
            pick_out,
            *out_pieces,
            token=og[0],
            scratch=[pltpu.VMEM((rows, qw), bf16)],
        )
        qkv_b = sent_call(n1_rel, dqkv, 0, wide, dqkv)
        qkv_c = swap(qkv_b, core_mask)
        far_mask, near_mask = z_masks[-1], z_masks[-2]
        step = [f32, bf16]

        def onward(pair, got, mask, token):
            pair = sum_call([pair[0], got], step, token)
            return pair, swap(pair[1], mask)

        down_k = kept_call(dy_all, hidden, 0, ff, down_got, qkv_b)
        down_got = swap(down_k[1], far_mask)
        qkv_k = kept_call(n1_rel, dqkv, 0, wide, qkv_c, down_k[0])
        qkv_got = swap(qkv_k[1], x_mask)
        og, og_got = onward(og, og_x, y_mask, qkv_k[0])
        (input_grad,) = kernel_call(
            functools.partial(first_norm_kernel, 2 * BAND),
            [shape_of(rows, width, f32)],
            estimate(2 * rows * width * (wide + 2 * width)),
            dqkv,
            x_rel,
            gains_rel,
            pick_attn,
            dmid,
            *q_pieces,
            *kv_pieces,
            token=og[0],
        )
        down_k, down_got = onward(down_k, down_got, near_mask, input_grad)
        up_b = sent_call(n2_all, dgu, ff, ff, down_k[0])
        up_got = swap(up_b, y_mask)
        gate_k = kept_call(n2_all, dgu, 0, ff, gate_got, up_b)
        gate_got = swap(gate_k[1], far_mask)
        og, og_got = onward(og, og_got, far_mask, gate_k[0])
        down_grad = finish([down_k[0], down_got], og[0])
        gate_k, gate_got = onward(gate_k, gate_got, near_mask, down_grad)
        qkv_k, qkv_got = onward(qkv_k, qkv_got, y_mask, gate_k[0])
        og, og_got = onward(og, og_got, near_mask, qkv_k[0])
        lay = down_call(hidden, down_full, og[0])
        lay_f = swap(lay[3], core_mask)
        output_grad = finish([og[0], og_got], lay[0])
        up_k = kept_call(n2_all, dgu, ff, ff, up_got, output_grad)
        up_got = swap(up_k[1], far_mask)
        gate_grad = finish([gate_k[0], gate_got], up_k[0])
        (lay_s,) = sum_call([lay[2], lay_f], [bf16], gate_grad)
        lay_x = swap(lay_s, x_mask)
        qkv_k, qkv_got = onward(qkv_k, qkv_got, far_mask, lay_s)
        lay_c = swap(after(lay[1], qkv_k[0]), core_mask)
        up_k, up_got = onward(up_k, up_got, near_mask, qkv_k[0])
        qkv_k, qkv_got = onward(qkv_k, qkv_got, near_mask, up_k[0])
        (layer_out,) = kernel_call(
            layer_kernel,
            [shape_of(rows, width, bf16)],
            estimate(2 * rows * width * width),
            lay[0],
            lay_c,
            lay_x,
            pick_mlp,
            middle,
            token=qkv_k[0],
        )
        up_grad = finish([up_k[0], up_got], layer_out)
        qkv_grad = finish([qkv_k[0], qkv_got], up_grad)
        q_grad, kv_grad = qkv_grad[:, :qw], qkv_grad[:, qw:]
        down_grad = down_grad.T

        first = jnp.sum(own_attn[:, :wide].astype(f32) * qkv_grad, axis=1)
        first_gain_grad = first / first_gain.astype(f32)
        second = jnp.sum(
            gate_weight.astype(f32) * gate_grad + up_weight.astype(f32) * up_grad, axis=1
        )
        for mask in t_masks:
            second = second + swap(second, mask)
        second = lax.dynamic_slice(second, (t_i * shard,), (shard,))
        second_gain_grad = second / second_gain.astype(f32)

        return (
            layer_out.reshape(tokens.shape),
            input_grad.reshape(tokens.shape),
            first_gain_grad,
            q_grad.reshape(shard, GROUP, KV_HEADS, HEAD).swapaxes(1, 2).reshape(shard, qw),
            kv_grad[:, :kw],
            kv_grad[:, kw:],
            output_grad,
            second_gain_grad,
            gate_grad,
            up_grad,
            down_grad,
        )

    return per_device


def solution(mesh):
    rows = P(None, AXES, None)
    split = P(AXES, None)
    placed = (
        rows,
        rows,
        P(AXES),
        split,
        split,
        split,
        split,
        P(AXES),
        P("dp", "tensor"),
        P("dp", "tensor"),
        P("tensor", "dp"),
        rows,
    )
    return jax.shard_map(
        program(dict(mesh.shape)),
        mesh=mesh,
        in_specs=placed,
        out_specs=(
            rows,
            rows,
            P(AXES),
            split,
            split,
            split,
            split,
            P(AXES),
            P("dp", "tensor"),
            P("dp", "tensor"),
            P("tensor", "dp"),
        ),
        check_vma=False,
    )
```

time: 816 us -> 571 us (0.70)
  Pallas kernels: 0 us -> 225 us
  waiting for transfers between devices: 386 us -> 193 us
  matrix products: 181 us -> 18.9 us
  local copies, waits for them, and re-layouts: 103 us -> 40.3 us
  blocking collectives: 29.6 us -> 0 us
  other arithmetic: 43.3 us -> 26.9 us
    pallas_call x0 -> x35, Pallas kernels: none -> 225 us  [the longest x6 70.9 us: kernel_call(): pl.pallas_call(body, out_shape=outs, in_specs=[pl.BlockSpec(memory_space=...]
    ppermute x65 -> x57, waiting for transfers between devices: 386 us -> 193 us  [swap(): return lax.ppermute(array, AXES, [(i, i ^ mask) for i in range(world)])]
    dot_general x16 -> x1, matrix products: 67.3 us -> 2.25 us  [against(): lax.dot_general(left_side, right_side, (((1,), (1,)), ((), ())), preferre...]
    dot_general x14 -> x6, matrix products: 66.5 us -> 16.6 us  [product(): return jnp.dot(left_side, right_side, preferred_element_type=f32)]
    dot_general x20 -> x0, matrix products: 47.4 us -> none  [the longest x14 36.2 us: across(): lax.dot_general(left_side, right_side, (((0,), (0,)), ((), ())), preferre...]
    psum x1 -> x0, blocking collectives: 29.6 us -> none  [per_device(): second = lax.psum(second, 'tensor')]
    reshape x7 -> x2, local copies, waits for them, and re-layouts: 18.6 us -> 1.38 us  [per_device(): q_grad.reshape(shard, GROUP, KV_HEADS, HEAD).swapaxes(1, 2)]
    slice x31 -> x4, local copies, waits for them, and re-layouts: 16.4 us -> 1.91 us  [the longest x1 1.76 us: per_device(): kv_grad[:, kw:]]
  transfers between devices with their start and end apart: 65 -> 57, of which waited for: 26 -> 19; matrix products, arithmetic and copies ran while one was open for 35% -> 12% of each run, Pallas kernels for 0% -> 35%
where the time goes in v2:
time: 571 us; the launch traced here: 561 us
  Pallas kernels  225 us (39%)
  waiting for transfers between devices  193 us (34%)
  starting transfers between devices  55.5 us (10%)
  local copies, waits for them, and re-layouts  40.3 us (7%)
  other arithmetic  26.9 us (5%)
  matrix products  18.9 us (3%)
    ppermute x57, waiting for transfers between devices, swap(): return lax.ppermute(array, AXES, [(i, i ^ mask) for i in range(world)])  193 us
    pallas_call x6, Pallas kernels, kernel_call(): pl.pallas_call(body, out_shape=outs, in_specs=[pl.BlockSpec(memory_space=...  70.9 us
    ppermute x57, starting transfers between devices, swap(): return lax.ppermute(array, AXES, [(i, i ^ mask) for i in range(world)])  55.5 us
    pallas_call x2, Pallas kernels, mlp_call(): pl.pallas_call(functools.partial(mlp_kernel, ff), grid=(2,), in_specs=[ba...  40.6 us
    pallas_call x16, Pallas kernels, sum_call(): pl.pallas_call(functools.partial(sum_kernel, len(arrays)), grid=(columns...  39.3 us
    pallas_call x5, Pallas kernels, kept_call(): pl.pallas_call(kept_kernel, grid=(2,), in_specs=[pl.BlockSpec((count, blo...  35.7 us
    unnamed x125, local copies, waits for them, and re-layouts  32.3 us
    pallas_call x5, Pallas kernels, sent_call(): pl.pallas_call(sent_kernel, grid=(2,), in_specs=[pl.BlockSpec((count, blo...  28 us
  transfers between devices with their start and end apart: 57, of which 19 were waited for; matrix products, arithmetic and copies ran while one was open for 12% of the time, Pallas kernels for 35%

profile of v2, /device:TPU:0, one launch (start us, length us, event | category | flops | bytes accessed | tf_op | source)
XLA Modules:
  0.0 561.5 jit_solution(3388283349559049353)
XLA Ops:
  30.3 9.1 %collective-permute-done.2 = bf16[48,4736]{1,0:T(8,128)(2,1)S(1)} collective-permute-done((bf16[48,4736]{1,0:T(8,128)(2,1)}, bf16[48,4736]{1,0:T(8,128)(2,1)S(1)}, u32[]{:S(2)}, u32[]{:S(2)}) %collective-permute-start.2) | collective-permute-done | bytes 454688 | tf_op jit(solution)/shard_map/ppermute | solution.py:448
  53.3 7.9 %collective-permute-start.9 = (bf16[192,1024]{1,0:T(8,128)(2,1)S(1)}, bf16[192,1024]{1,0:T(8,128)(2,1)S(1)}, u32[]{:S(2)}, u32[]{:S(2)}) collective-permute-start(bf16[192,1024]{1,0:T(8,128)(2,1)S(1)} %bitcast.33), channel_id=1, source_target_pairs={{0,16},{1,17},{2,18},{3,19},{4,20},{5,21},{6,22},{7,23},{8,24},{9,... | collective-permute-start | bytes 1179656 | tf_op jit(solution)/shard_map/ppermute | solution.py:448
  70.4 7.7 %collective-permute-done.9 = bf16[192,1024]{1,0:T(8,128)(2,1)S(1)} collective-permute-done((bf16[192,1024]{1,0:T(8,128)(2,1)S(1)}, bf16[192,1024]{1,0:T(8,128)(2,1)S(1)}, u32[]{:S(2)}, u32[]{:S(2)}) %collective-permute-start.9) | collective-permute-done | bytes 393248 | tf_op jit(solution)/shard_map/ppermute | solution.py:448
  87.8 30.2 %collective-permute-done.14 = bf16[192,2048]{1,0:T(8,128)(2,1)S(1)} collective-permute-done((bf16[192,2048]{1,0:T(8,128)(2,1)S(1)}, bf16[192,2048]{1,0:T(8,128)(2,1)S(1)}, u32[]{:S(2)}, u32[]{:S(2)}) %collective-permute-start.14) | collective-permute-done | bytes 786464 | tf_op jit(solution)/shard_map/ppermute | solution.py:448
  125.2 16.5 %collective-permute-done.17 = bf16[384,768]{1,0:T(8,128)(2,1)S(1)} collective-permute-done((bf16[384,768]{1,0:T(8,128)(2,1)S(1)}, bf16[384,768]{1,0:T(8,128)(2,1)S(1)}, u32[]{:S(2)}, u32[]{:S(2)}) %collective-permute-start.17) | collective-permute-done | bytes 589856 | tf_op jit(solution)/shard_map/ppermute | solution.py:448
  144.4 17.2 %shard_map.204 = (bf16[384,3072]{1,0:T(8,128)(2,1)}, bf16[384,1536]{1,0:T(8,128)(2,1)}, bf16[384,1536]{1,0:T(8,128)(2,1)}, f32[8,1536]{1,0:T(8,128)}) custom-call(bf16[384,1536]{1,0:T(8,128)(2,1)} %fusion.18.refs_0_.refs_1_, f32[384,384]{1,0:T(8,128)} %copy.50.refs_1_.refs_2_, f32[384,384]{1,0:T(8,128)} %copy.51.refs_2_.refs_3_, ...), custom_call_target="tpu_custom_call" | custom-call | flops 99999997952 | tf_op jit(solution)/shard_map/pallas_call | solution.py:424
  167.9 9.9 %collective-permute-done.20 = bf16[384,2048]{1,0:T(8,128)(2,1)} collective-permute-done((bf16[384,2048]{1,0:T(8,128)(2,1)}, bf16[384,2048]{1,0:T(8,128)(2,1)}, u32[]{:S(2)}, u32[]{:S(2)}) %collective-permute-start.20) | collective-permute-done | bytes 1572896 | tf_op jit(solution)/shard_map/ppermute | solution.py:448
  193.5 18.8 %collective-permute-done.27 = bf16[384,2048]{1,0:T(8,128)(2,1)S(1)} collective-permute-done((bf16[384,2048]{1,0:T(8,128)(2,1)}, bf16[384,2048]{1,0:T(8,128)(2,1)S(1)}, u32[]{:S(2)}, u32[]{:S(2)}) %collective-permute-start.27) | collective-permute-done | bytes 1572896 | tf_op jit(solution)/shard_map/ppermute | solution.py:448
  224.6 16.1 %collective-permute-done.29 = bf16[384,1024]{1,0:T(8,128)(2,1)S(1)} collective-permute-done((bf16[384,1024]{1,0:T(8,128)(2,1)S(1)}, bf16[384,1024]{1,0:T(8,128)(2,1)S(1)}, u32[]{:S(2)}, u32[]{:S(2)}) %collective-permute-start.29) | collective-permute-done | bytes 786464 | tf_op jit(solution)/shard_map/ppermute | solution.py:448
  243.5 20.3 %shard_map.205 = (bf16[1536,1024]{1,0:T(8,128)(2,1)}, bf16[1536,2048]{1,0:T(8,128)(2,1)}, bf16[384,1536]{1,0:T(8,128)(2,1)}, bf16[384,1536]{1,0:T(8,128)(2,1)}) custom-call(bf16[1536,1536]{1,0:T(8,128)(2,1)} %constant_dynamic-update-slice_fusion.33.refs_0_.refs_4_.left_ref, bf16[1536,1536]{1,0:T(8,128)(2,1)} %pad_maximum_fusion.refs_1_.left_ref, ...), custom_call_target="tpu_custom_call" | custom-call | flops 99999997952 | tf_op jit(solution)/shard_map/pallas_call | solution.py:279
  277.4 20.4 %shard_map.207 = (bf16[1536,1024]{1,0:T(8,128)(2,1)}, bf16[1536,2048]{1,0:T(8,128)(2,1)}, bf16[384,1536]{1,0:T(8,128)(2,1)}, bf16[384,1536]{1,0:T(8,128)(2,1)}) custom-call(bf16[1536,1536]{1,0:T(8,128)(2,1)} %constant_dynamic-update-slice_fusion.33.refs_0_.refs_4_.left_ref, ...), custom_call_target="tpu_custom_call", output_to_operand_aliasing={{0}: (4, {}), {1}: (5, {})} | custom-call | flops 99999997952 | tf_op jit(solution)/shard_map/pallas_call | solution.py:279
  305.7 8.7 %shard_map.209 = (f32[384,1536]{1,0:T(8,128)}, bf16[384,1536]{1,0:T(8,128)(2,1)}) custom-call(bf16[384,1536]{1,0:T(8,128)(2,1)} %get-tuple-element.117.token_ref.refs_0_, bf16[384,1536]{1,0:T(8,128)(2,1)} %copy-done.39, bf16[384,1536]{1,0:T(8,128)(2,1)} %collective-permute-done.32.refs_2_, bf16[1536,1536]{1,0:T(8,128)(2,1)} %fusion.2.refs_3_.pick_ref, ...), custom_call_target="tpu_custom_call" | custom-call | flops 99999997952 | tf_op jit(solution)/shard_map/pallas_call | solution.py:424
  333.9 19.8 %shard_map.213.right_ref.token_ref.refs_0_ = bf16[384,3072]{1,0:T(8,128)(2,1)} custom-call(bf16[384,1536]{1,0:T(8,128)(2,1)} %get-tuple-element.119.right_ref.token_ref.refs_0_, bf16[384,3072]{1,0:T(8,128)(2,1)} %get-tuple-element.124.refs_1_, f32[384,384]{1,0:T(8,128)} %copy.50.refs_1_.refs_2_, f32[384,384]{1,0:T(8,128)} %copy.51.refs_2_.refs_3_, ...), custom_call_target="tpu_custom_call" | custom-call | flops 99999997952 | tf_op jit(solution)/shard_map/pallas_call | solution.py:424
  359.7 6.9 %shard_map.215 = (f32[384,1024]{1,0:T(8,128)}, bf16[384,1024]{1,0:T(8,128)(2,1)}) custom-call(bf16[1536,1536]{1,0:T(8,128)(2,1)} %pad_maximum_fusion.refs_1_.left_ref, bf16[1536,1024]{1,0:T(8,128)(2,1)} %get-tuple-element.116.right_ref.hidden_ref, bf16[768,1024]{1,0:T(8,128)(2,1)} %collective-permute-done.36.got_ref, bf16[768,3072]{1,0:T(8,128)(2,1)} %shard_map.214.token_ref), custom_call_target="tpu_custom_call" | custom-call | flops 99999997952 | tf_op jit(solution)/shard_map/pallas_call | solution.py:323
  370.0 8.8 %shard_map.216 = (f32[384,3072]{1,0:T(8,128)}, bf16[384,3072]{1,0:T(8,128)(2,1)}) custom-call(bf16[384,1536]{1,0:T(8,128)(2,1)} %get-tuple-element.123.left_ref, bf16[384,3072]{1,0:T(8,128)(2,1)} %shard_map.213.right_ref.token_ref.refs_0_, bf16[768,3072]{1,0:T(8,128)(2,1)} %copy-done.29, f32[384,1024]{1,0:T(8,128)} %get-tuple-element.125.token_ref.refs_0_), custom_call_target="tpu_custom_call" | custom-call | flops 99999997952 | tf_op jit(solution)/shard_map/pallas_call | solution.py:323
  382.5 16.1 %shard_map.218.refs_2_ = f32[384,1536]{1,0:T(8,128)} custom-call(bf16[384,3072]{1,0:T(8,128)(2,1)} %shard_map.213.right_ref.token_ref.refs_0_, bf16[384,1536]{1,0:T(8,128)(2,1)} %fusion.18.refs_0_.refs_1_, f32[8,1536]{1,0:T(8,128)} %get-tuple-element.104.refs_2_, bf16[1536,1536]{1,0:T(8,128)(2,1)} %fusion.5.refs_3_, f32[384,1536]{1,0:T(8,128)} %get-tuple-element.130.refs_4_, ...), custom_call_target="tpu_custom_call" | custom-call | flops 99999997952 | tf_op jit(solution)/shard_map/pallas_call | solution.py:424
  410.0 6.9 %shard_map.221 = (f32[384,1024]{1,0:T(8,128)}, bf16[384,1024]{1,0:T(8,128)(2,1)}) custom-call(bf16[1536,1536]{1,0:T(8,128)(2,1)} %constant_dynamic-update-slice_fusion.33.refs_0_.refs_4_.left_ref, bf16[1536,2048]{1,0:T(8,128)(2,1)} %get-tuple-element.120.right_ref, bf16[768,1024]{1,0:T(8,128)(2,1)} %collective-permute-done.38.got_ref, ...), custom_call_target="tpu_custom_call" | custom-call | flops 99999997952 | tf_op jit(solution)/shard_map/pallas_call | solution.py:323
  421.2 23.2 %collective-permute-done.43.refs_1_ = bf16[192,1024]{1,0:T(8,128)(2,1)S(1)} collective-permute-done((bf16[192,1024]{1,0:T(8,128)(2,1)S(1)}, bf16[192,1024]{1,0:T(8,128)(2,1)S(1)}, u32[]{:S(2)}, u32[]{:S(2)}) %collective-permute-start.43) | collective-permute-done | bytes 393248 | tf_op jit(solution)/shard_map/ppermute | solution.py:448
  453.0 7.4 %collective-permute-done.41.refs_1_ = bf16[384,3072]{1,0:T(8,128)(2,1)} collective-permute-done((bf16[384,3072]{1,0:T(8,128)(2,1)}, bf16[384,3072]{1,0:T(8,128)(2,1)}, u32[]{:S(2)}, u32[]{:S(2)}) %collective-permute-start.41) | collective-permute-done | bytes 2359328 | tf_op jit(solution)/shard_map/ppermute | solution.py:448
  467.4 10.5 %shard_map.227 = (bf16[384,1536]{1,0:T(8,128)(2,1)}, bf16[384,1536]{1,0:T(8,128)(2,1)}, bf16[384,1536]{1,0:T(8,128)(2,1)}, bf16[384,1536]{1,0:T(8,128)(2,1)}) custom-call(bf16[1536,1024]{1,0:T(8,128)(2,1)} %get-tuple-element.116.right_ref.hidden_ref, bf16[1536,1024]{1,0:T(8,128)(2,1)} %copy-done.18, f32[48,1536]{1,0:T(8,128)} %get-tuple-element.140.token_ref.refs_0_), custom_call_target="tpu_custom_call" | custom-call | flops 99999997952 | tf_op jit(solution)/shard_map/pallas_call | solution.py:405
  481.1 7.1 %shard_map.229 = (f32[384,1024]{1,0:T(8,128)}, bf16[384,1024]{1,0:T(8,128)(2,1)}) custom-call(bf16[1536,1536]{1,0:T(8,128)(2,1)} %constant_dynamic-update-slice_fusion.33.refs_0_.refs_4_.left_ref, bf16[1536,2048]{1,0:T(8,128)(2,1)} %get-tuple-element.120.right_ref, bf16[768,1024]{1,0:T(8,128)(2,1)} %collective-permute-done.47.got_ref, ...), custom_call_target="tpu_custom_call" | custom-call | flops 99999997952 | tf_op jit(solution)/shard_map/pallas_call | solution.py:323
  495.2 9.6 %collective-permute-done.44.refs_1_ = bf16[192,3072]{1,0:T(8,128)(2,1)} collective-permute-done((bf16[192,3072]{1,0:T(8,128)(2,1)}, bf16[192,3072]{1,0:T(8,128)(2,1)}, u32[]{:S(2)}, u32[]{:S(2)}) %collective-permute-start.44) | collective-permute-done | bytes 1179680 | tf_op jit(solution)/shard_map/ppermute | solution.py:448
  513.9 18.3 %collective-permute-done.51.refs_1_ = bf16[96,3072]{1,0:T(8,128)(2,1)S(1)} collective-permute-done((bf16[96,3072]{1,0:T(8,128)(2,1)}, bf16[96,3072]{1,0:T(8,128)(2,1)S(1)}, u32[]{:S(2)}, u32[]{:S(2)}) %collective-permute-start.51) | collective-permute-done | bytes 589856 | tf_op jit(solution)/shard_map/ppermute | solution.py:448
  536.0 7.1 %shard_map.235.refs_2_ = bf16[384,1536]{1,0:T(8,128)(2,1)} custom-call(bf16[384,1536]{1,0:T(8,128)(2,1)} %get-tuple-element.141.refs_2_.own_ref, bf16[384,1536]{1,0:T(8,128)(2,1)} %collective-permute-done.49.core_ref, bf16[384,1536]{1,0:T(8,128)(2,1)} %collective-permute-done.50.x_ref, bf16[1536,1536]{1,0:T(8,128)(2,1)} %fusion.2.refs_3_.pick_ref, ...), custom_call_target="tpu_custom_call" | custom-call | flops 99999997952 | tf_op jit(solution)/shard_map/pallas_call | solution.py:424
  (314 shorter events, 235.3 us)
Async XLA Ops:
  46.6 31.5 %collective-permute-start.5 = (bf16[192,1536]{1,0:T(8,128)(2,1)S(1)}, bf16[192,1536]{1,0:T(8,128)(2,1)S(1)}, u32[]{:S(2)}, u32[]{:S(2)}) collective-permute-start(bf16[192,1536]{1,0:T(8,128)(2,1)S(1)} %pad_maximum_fusion.7), channel_id=1, source_target_pairs={{0,2},{1,3},{2,0},{3,1},{4,6},{5,7},{6,4},{7,5},{8,10},{9,11},{10,... | collective-permute-start | bytes 1769480 | tf_op jit(solution)/shard_map/ppermute | solution.py:448
  78.1 40.3 %collective-permute-start.11 = (bf16[384,1664]{1,0:T(8,128)(2,1)S(1)}, bf16[384,1664]{1,0:T(8,128)(2,1)S(1)}, u32[]{:S(2)}, u32[]{:S(2)}) collective-permute-start(bf16[384,1664]{1,0:T(8,128)(2,1)S(1)} %constant_dynamic-update-slice_fusion.5.refs_8_.refs_9_), channel_id=1, source_target_pairs={{0,2},{1,3},{2,0},{3,1},{4,6},{5,7},{6,4},{7,5},{8,10},{9,11},{10,... | collective-permute-start | bytes 3833864 | tf_op jit(solution)/shard_map/ppermute | solution.py:448
  79.7 39.8 %collective-permute-start.13 = (bf16[384,1664]{1,0:T(8,128)(2,1)S(1)}, bf16[384,1664]{1,0:T(8,128)(2,1)S(1)}, u32[]{:S(2)}, u32[]{:S(2)}) collective-permute-start(bf16[384,1664]{1,0:T(8,128)(2,1)S(1)} %constant_dynamic-update-slice_fusion.5.refs_8_.refs_9_), channel_id=1, source_target_pairs={{0,1},{1,0},{2,3},{3,2},{4,5},{5,4},{6,7},{7,6},{8,9},{9,8},{10,11... | collective-permute-start | bytes 3833864 | tf_op jit(solution)/shard_map/ppermute | solution.py:448
  79.8 38.7 %collective-permute-start.10 = (bf16[384,1536]{1,0:T(8,128)(2,1)S(1)}, bf16[384,1536]{1,0:T(8,128)(2,1)S(1)}, u32[]{:S(2)}, u32[]{:S(2)}) collective-permute-start(bf16[384,1536]{1,0:T(8,128)(2,1)S(1)} %constant_dynamic-update-slice_fusion.refs_4_.refs_5_), channel_id=1, source_target_pairs={{0,4},{1,5},{2,6},{3,7},{4,0},{5,1},{6,2},{7,3},{8,12},{9,13},{10,... | collective-permute-start | bytes 3538952 | tf_op jit(solution)/shard_map/ppermute | solution.py:448
  80.3 38.1 %collective-permute-start.12 = (bf16[384,1536]{1,0:T(8,128)(2,1)S(1)}, bf16[384,1536]{1,0:T(8,128)(2,1)S(1)}, u32[]{:S(2)}, u32[]{:S(2)}) collective-permute-start(bf16[384,1536]{1,0:T(8,128)(2,1)S(1)} %constant_dynamic-update-slice_fusion.refs_4_.refs_5_), channel_id=1, source_target_pairs={{0,1},{1,0},{2,3},{3,2},{4,5},{5,4},{6,7},{7,6},{8,9},{9,8},{10,11... | collective-permute-start | bytes 3538952 | tf_op jit(solution)/shard_map/ppermute | solution.py:448
  81.4 36.5 %collective-permute-start.14 = (bf16[192,2048]{1,0:T(8,128)(2,1)S(1)}, bf16[192,2048]{1,0:T(8,128)(2,1)S(1)}, u32[]{:S(2)}, u32[]{:S(2)}) collective-permute-start(bf16[192,2048]{1,0:T(8,128)(2,1)S(1)} %get-tuple-element.92), channel_id=1, source_target_pairs={{0,16},{1,17},{2,18},{3,19},{4,20},{5,21},{6,22},{7,23},{8,24},{9,... | collective-permute-start | bytes 2359304 | tf_op jit(solution)/shard_map/ppermute | solution.py:448
  117.9 71.9 %collective-permute-start.22 = (bf16[192,1024]{1,0:T(8,128)(2,1)S(1)}, bf16[192,1024]{1,0:T(8,128)(2,1)S(1)}, u32[]{:S(2)}, u32[]{:S(2)}) collective-permute-start(bf16[192,1024]{1,0:T(8,128)(2,1)S(1)} %collective-permute-done.9), channel_id=1, source_target_pairs={{0,4},{1,5},{2,6},{3,7},{4,0},{5,1},{6,2},{7,3},{8,12},{9,13},{10,... | collective-permute-start | bytes 1179656 | tf_op jit(solution)/shard_map/ppermute | solution.py:448
  141.7 40.4 %collective-permute-start.21 = (bf16[192,2048]{1,0:T(8,128)(2,1)S(1)}, bf16[192,2048]{1,0:T(8,128)(2,1)}, u32[]{:S(2)}, u32[]{:S(2)}) collective-permute-start(bf16[192,2048]{1,0:T(8,128)(2,1)S(1)} %collective-permute-done.14), channel_id=1, source_target_pairs={{0,4},{1,5},{2,6},{3,7},{4,0},{5,1},{6,2},{7,3},{8,12},{9,13},{10,... | collective-permute-start | bytes 2359304 | tf_op jit(solution)/shard_map/ppermute | solution.py:448
  142.2 35.6 %collective-permute-start.20 = (bf16[384,2048]{1,0:T(8,128)(2,1)}, bf16[384,2048]{1,0:T(8,128)(2,1)}, u32[]{:S(2)}, u32[]{:S(2)}) collective-permute-start(bf16[384,2048]{1,0:T(8,128)(2,1)} %pad_maximum_fusion.3), channel_id=1, source_target_pairs={{0,8},{1,9},{2,10},{3,11},{4,12},{5,13},{6,14},{7,15},{8,0},{9,1},... | collective-permute-start | bytes 4718600 | tf_op jit(solution)/shard_map/ppermute | solution.py:448
  144.4 38.9 %collective-permute-start.19 = (bf16[768,1536]{1,0:T(8,128)(2,1)S(1)}, bf16[768,1536]{1,0:T(8,128)(2,1)}, u32[]{:S(2)}, u32[]{:S(2)}) collective-permute-start(bf16[768,1536]{1,0:T(8,128)(2,1)S(1)} %pad_maximum_fusion.1.refs_6_), channel_id=1, source_target_pairs={{0,1},{1,0},{2,3},{3,2},{4,5},{5,4},{6,7},{7,6},{8,9},{9,8},{10,11... | collective-permute-start | bytes 7077896 | tf_op jit(solution)/shard_map/ppermute | solution.py:448
  167.5 45.0 %collective-permute-start.26 = (bf16[768,1536]{1,0:T(8,128)(2,1)S(1)}, bf16[768,1536]{1,0:T(8,128)(2,1)S(1)}, u32[]{:S(2)}, u32[]{:S(2)}) collective-permute-start(bf16[768,1536]{1,0:T(8,128)(2,1)S(1)} %copy-done.8), channel_id=1, source_target_pairs={{0,1},{1,0},{2,3},{3,2},{4,5},{5,4},{6,7},{7,6},{8,9},{9,8},{10,11... | collective-permute-start | bytes 7077896 | tf_op jit(solution)/shard_map/ppermute | solution.py:448
  177.8 34.5 %collective-permute-start.27 = (bf16[384,2048]{1,0:T(8,128)(2,1)}, bf16[384,2048]{1,0:T(8,128)(2,1)S(1)}, u32[]{:S(2)}, u32[]{:S(2)}) collective-permute-start(bf16[384,2048]{1,0:T(8,128)(2,1)} %collective-permute-done.20), channel_id=1, source_target_pairs={{0,4},{1,5},{2,6},{3,7},{4,0},{5,1},{6,2},{7,3},{8,12},{9,13},{10,... | collective-permute-start | bytes 4718600 | tf_op jit(solution)/shard_map/ppermute | solution.py:448
  189.9 32.5 %collective-permute-start.23 = (bf16[384,1536]{1,0:T(8,128)(2,1)S(1)}, bf16[384,1536]{1,0:T(8,128)(2,1)S(1)}, u32[]{:S(2)}, u32[]{:S(2)}) collective-permute-start(bf16[384,1536]{1,0:T(8,128)(2,1)S(1)} %fusion.16), channel_id=1, source_target_pairs={{0,1},{1,0},{2,3},{3,2},{4,5},{5,4},{6,7},{7,6},{8,9},{9,8},{10,11... | collective-permute-start | bytes 3538952 | tf_op jit(solution)/shard_map/ppermute | solution.py:448
  304.1 55.7 %collective-permute-start.36 = (bf16[768,1024]{1,0:T(8,128)(2,1)}, bf16[768,1024]{1,0:T(8,128)(2,1)}, u32[]{:S(2)}, u32[]{:S(2)}) collective-permute-start(bf16[768,1024]{1,0:T(8,128)(2,1)} %shard_map.208.refs_7_), channel_id=1, source_target_pairs={{0,4},{1,5},{2,6},{3,7},{4,0},{5,1},{6,2},{7,3},{8,12},{9,13},{10,... | collective-permute-start | bytes 4718600 | tf_op jit(solution)/shard_map/ppermute | solution.py:448
  324.5 85.5 %collective-permute-start.38 = (bf16[768,1024]{1,0:T(8,128)(2,1)}, bf16[768,1024]{1,0:T(8,128)(2,1)}, u32[]{:S(2)}, u32[]{:S(2)}) collective-permute-start(bf16[768,1024]{1,0:T(8,128)(2,1)} %shard_map.211.token_ref), channel_id=1, source_target_pairs={{0,4},{1,5},{2,6},{3,7},{4,0},{5,1},{6,2},{7,3},{8,12},{9,13},{10,... | collective-permute-start | bytes 4718600 | tf_op jit(solution)/shard_map/ppermute | solution.py:448
  333.2 45.6 %collective-permute-start.34 = (bf16[384,1536]{1,0:T(8,128)(2,1)}, bf16[384,1536]{1,0:T(8,128)(2,1)}, u32[]{:S(2)}, u32[]{:S(2)}) collective-permute-start(bf16[384,1536]{1,0:T(8,128)(2,1)} %get-tuple-element.122), channel_id=1, source_target_pairs={{0,2},{1,3},{2,0},{3,1},{4,6},{5,7},{6,4},{7,5},{8,10},{9,11},{10,... | collective-permute-start | bytes 3538952 | tf_op jit(solution)/shard_map/ppermute | solution.py:448
  366.7 32.0 %collective-permute-start.39 = (bf16[384,1024]{1,0:T(8,128)(2,1)}, bf16[384,1024]{1,0:T(8,128)(2,1)}, u32[]{:S(2)}, u32[]{:S(2)}) collective-permute-start(bf16[384,1024]{1,0:T(8,128)(2,1)} %get-tuple-element.129), channel_id=1, source_target_pairs={{0,8},{1,9},{2,10},{3,11},{4,12},{5,13},{6,14},{7,15},{8,0},{9,1},... | collective-permute-start | bytes 2359304 | tf_op jit(solution)/shard_map/ppermute | solution.py:448
  381.9 35.9 %collective-permute-start.37 = (bf16[192,1536]{1,0:T(8,128)(2,1)}, bf16[192,1536]{1,0:T(8,128)(2,1)}, u32[]{:S(2)}, u32[]{:S(2)}) collective-permute-start(bf16[192,1536]{1,0:T(8,128)(2,1)} %get-tuple-element.128), channel_id=1, source_target_pairs={{0,4},{1,5},{2,6},{3,7},{4,0},{5,1},{6,2},{7,3},{8,12},{9,13},{10,... | collective-permute-start | bytes 1769480 | tf_op jit(solution)/shard_map/ppermute | solution.py:448
  407.1 53.3 %collective-permute-start.41 = (bf16[384,3072]{1,0:T(8,128)(2,1)}, bf16[384,3072]{1,0:T(8,128)(2,1)}, u32[]{:S(2)}, u32[]{:S(2)}) collective-permute-start(bf16[384,3072]{1,0:T(8,128)(2,1)} %get-tuple-element.135), channel_id=1, source_target_pairs={{0,2},{1,3},{2,0},{3,1},{4,6},{5,7},{6,4},{7,5},{8,10},{9,11},{10,... | collective-permute-start | bytes 7077896 | tf_op jit(solution)/shard_map/ppermute | solution.py:448
  408.6 72.5 %collective-permute-start.47 = (bf16[768,1024]{1,0:T(8,128)(2,1)}, bf16[768,1024]{1,0:T(8,128)(2,1)}, u32[]{:S(2)}, u32[]{:S(2)}) collective-permute-start(bf16[768,1024]{1,0:T(8,128)(2,1)} %shard_map.220.token_ref), channel_id=1, source_target_pairs={{0,4},{1,5},{2,6},{3,7},{4,0},{5,1},{6,2},{7,3},{8,12},{9,13},{10,... | collective-permute-start | bytes 4718600 | tf_op jit(solution)/shard_map/ppermute | solution.py:448
  420.0 44.8 %collective-permute-start.40 = (bf16[96,1536]{1,0:T(8,128)(2,1)}, bf16[96,1536]{1,0:T(8,128)(2,1)}, u32[]{:S(2)}, u32[]{:S(2)}) collective-permute-start(bf16[96,1536]{1,0:T(8,128)(2,1)} %get-tuple-element.134), channel_id=1, source_target_pairs={{0,8},{1,9},{2,10},{3,11},{4,12},{5,13},{6,14},{7,15},{8,0},{9,1},... | collective-permute-start | bytes 884744 | tf_op jit(solution)/shard_map/ppermute | solution.py:448
  449.7 39.5 %collective-permute-start.46 = (bf16[192,1024]{1,0:T(8,128)(2,1)}, bf16[192,1024]{1,0:T(8,128)(2,1)}, u32[]{:S(2)}, u32[]{:S(2)}) collective-permute-start(bf16[192,1024]{1,0:T(8,128)(2,1)} %get-tuple-element.146), channel_id=1, source_target_pairs={{0,16},{1,17},{2,18},{3,19},{4,20},{5,21},{6,22},{7,23},{8,24},{9,... | collective-permute-start | bytes 1179656 | tf_op jit(solution)/shard_map/ppermute | solution.py:448
  493.8 42.1 %collective-permute-start.50 = (bf16[384,1536]{1,0:T(8,128)(2,1)}, bf16[384,1536]{1,0:T(8,128)(2,1)}, u32[]{:S(2)}, u32[]{:S(2)}) collective-permute-start(bf16[384,1536]{1,0:T(8,128)(2,1)} %shard_map.231.refs_2_), channel_id=1, source_target_pairs={{0,2},{1,3},{2,0},{3,1},{4,6},{5,7},{6,4},{7,5},{8,10},{9,11},{10,... | collective-permute-start | bytes 3538952 | tf_op jit(solution)/shard_map/ppermute | solution.py:448
  511.3 31.8 %collective-permute-start.54 = (bf16[192,1024]{1,0:T(8,128)(2,1)}, bf16[192,1024]{1,0:T(8,128)(2,1)}, u32[]{:S(2)}, u32[]{:S(2)}) collective-permute-start(bf16[192,1024]{1,0:T(8,128)(2,1)} %get-tuple-element.156), channel_id=1, source_target_pairs={{0,16},{1,17},{2,18},{3,19},{4,20},{5,21},{6,22},{7,23},{8,24},{9,... | collective-permute-start | bytes 1179656 | tf_op jit(solution)/shard_map/ppermute | solution.py:448
  (82 other events, 994.0 us)

commit v3 on v2

--- a/solution.py
+++ b/solution.py
@@ -68,12 +68,6 @@
     for k, mask in enumerate(masks):
         delta = delta + ((step >> k) & 1) * mask
     return (me ^ delta) * block + place % block
-
-
-def one_hot(source):
-    count = source.shape[0]
-    rows = lax.broadcasted_iota(jnp.int32, (count, count), 0)
-    return (rows == source[None, :]).astype(bf16)
 
 
 def join(parts):
@@ -143,7 +137,8 @@
     qkv_ref, att_ref, n1_ref, gains_ref = refs[-4:]
     q_bands = GROUP * kv_bands
     q_refs, kv_refs = piece_refs[:4], piece_refs[4:]
-    tail = pl.ds(2 * kv_bands * BAND, LANES)
+    skip = q_bands // 2
+    tail = pl.ds((skip + 2 * kv_bands) * BAND, LANES)
     gains = jnp.transpose(piece_rows(kv_refs, tail, False).astype(f32))
     gains_ref[...] = gains[: gains_ref.shape[0]]
     inputs = x_ref[...].astype(f32)
@@ -151,7 +146,7 @@
     n1_ref[...] = (inputs * scale * gains[:1]).astype(bf16)
     for band in range(q_bands + 2 * kv_bands):
         in_q = band < q_bands
-        place = columns(band if in_q else band - q_bands)
+        place = columns(band if in_q else band - q_bands + skip)
         total = product(n1_ref[...], piece_rows(q_refs if in_q else kv_refs, place, in_q))
         if band < q_bands + kv_bands:
             total = turn(total, cos_ref[...], sin_ref[...])
@@ -184,21 +179,20 @@
     ]
     first = 0
     for piece in (
-        jnp.concatenate(heads, axis=1), k_ref[...], v_ref[...], gains_ref[...], o_ref[...]
+        jnp.concatenate(heads, axis=1), o_ref[...], k_ref[...], v_ref[...], gains_ref[...]
     ):
         out_ref[:, first : first + piece.shape[1]] = piece
         first += piece.shape[1]
 
 
 def backward_kernel(micro, per_pack, kv_bands, *refs):
-    dmb_ref, qkv_ref, cos_ref, sin_ref, mask_ref, pick_ref, *out_refs = refs[:8]
+    dmb_ref, qkv_ref, cos_ref, sin_ref, mask_ref, pick_ref, *piece_refs = refs[:14]
     dqkv_ref, datt_ref = refs[-2:]
     half = pick_ref.shape[1] // 2
-    datt = 0.0
-    for k, piece in enumerate(out_refs):
-        part = against(dmb_ref[...], piece[...]).astype(bf16)
-        datt = datt + against(part, pick_ref[:, k * half : (k + 1) * half])
-    datt_ref[...] = datt.astype(bf16)
+    everything = slice(None)
+    datt = against(dmb_ref[:, :half], piece_rows(piece_refs[:4], everything, True))
+    datt = datt + against(dmb_ref[:, half:], piece_rows(piece_refs[4:], everything, False))
+    datt_ref[...] = against(datt.astype(bf16), pick_ref[...]).astype(bf16)
     q_bands = GROUP * kv_bands
     factor = 1.0 / math.sqrt(HEAD)
     masks = head_masks()
@@ -230,17 +224,25 @@
 
 
 def mlp_kernel(ff, *refs):
-    n2_ref, dy_ref, gu_ref, down_ref = refs[:4]
+    weight_refs = refs[4:8]
+    gu_refs, down_refs = weight_refs[:2], weight_refs[2:]
+    first = pl.program_id(0) == 0
+    n2_ref = jnp.where(first, refs[0][...], refs[1][...])
+    dy_ref = jnp.where(first, refs[2][...], refs[3][...])
     hidden_ref, dgu_ref, *dn2_refs = refs[-4:]
-    both = product(n2_ref[...], gu_ref[...])
+    half = gu_refs[0].shape[0]
+    lower, upper = slice(0, half), slice(half, 2 * half)
+    both = product(n2_ref[:, lower], gu_refs[0][...]) + product(n2_ref[:, upper], gu_refs[1][...])
     gate, up = both[:, :ff], both[:, ff:]
-    dhid = product(dy_ref[...], down_ref[...])
+    dhid = product(dy_ref[:, lower], down_refs[0][...])
+    dhid = dhid + product(dy_ref[:, upper], down_refs[1][...])
     sig = jax.nn.sigmoid(gate)
     passed = gate * sig
     hidden_ref[...] = (passed * up).astype(bf16)
     dgu_ref[:, :ff] = (dhid * up * sig * (1.0 + gate * (1.0 - sig))).astype(bf16)
     dgu_ref[:, ff:] = (dhid * passed).astype(bf16)
-    dn2 = against(dgu_ref[...], gu_ref[...]).astype(bf16)
+    dgu = dgu_ref[...]
+    dn2 = jnp.concatenate([against(dgu, gu[...]).astype(bf16) for gu in gu_refs], axis=1)
     put_by_step(dn2_refs, [dn2] * 2)
 
 
@@ -260,6 +262,7 @@
     return pl.CostEstimate(flops=100000000000, bytes_accessed=0, transcendentals=0)
 
 
+SHORT = pl.CostEstimate(flops=10**9, bytes_accessed=0, transcendentals=0)
 LIMIT = pltpu.CompilerParams(vmem_limit_bytes=56 * 1024 * 1024)
 ANYWHERE = pl.BlockSpec(memory_space=pl.ANY)
 
@@ -268,64 +271,76 @@
     return pl.BlockSpec((rows, columns), lambda i: (row, column))
 
 
-def mlp_call(first, n2, dy, gu, down, *earlier):
-    rows, width = n2.shape
-    ff = down.shape[1]
-    block = rows // 4
+def mlp_call(first, n2, dy, weights, *earlier):
+    block, width = n2[0][0].shape[0], n2[0][0].shape[1]
+    rows = 4 * block
+    ff = weights[-1].shape[1]
 
     def band(columns):
-        return pl.BlockSpec((block, columns), lambda i: (first + i, 0))
+        return pl.BlockSpec((block, columns), lambda i: (first + 2 * i, 0))
 
     return pl.pallas_call(
         functools.partial(mlp_kernel, ff),
         grid=(2,),
-        in_specs=[band(width), band(width), fixed(*gu.shape), fixed(*down.shape)]
+        in_specs=[fixed(block, width, row) for _, row in n2 + dy]
+        + [fixed(*array.shape) for array in weights]
         + [ANYWHERE] * len(earlier),
         out_specs=[band(ff), band(2 * ff), fixed(block, width), fixed(block, width)],
         out_shape=[shape_of(rows, ff, bf16), shape_of(rows, 2 * ff, bf16)]
         + [shape_of(block, width, bf16)] * 2,
-        input_output_aliases={4 + k: k for k in range(len(earlier) - 1)},
+        input_output_aliases={8 + k: k for k in range(len(earlier) - 1)},
         compiler_params=LIMIT,
         cost_estimate=estimate(10 * 2 * block * width * ff),
-    )(n2, dy, gu, down, *earlier)
-
-
-def sent_kernel(left_ref, right_ref, token_ref, out_ref):
-    out_ref[...] = across(left_ref[...], right_ref[...]).astype(bf16)
+    )(*[array for array, _ in n2 + dy], *weights, *earlier)
+
+
+def left_rows(refs):
+    return refs[0][...] if len(refs) == 1 else jnp.concatenate([r[...] for r in refs], axis=0)
+
+
+def left_parts(left, right):
+    if not isinstance(left, list):
+        left = [(left, 0)]
+    return left, right.shape[0] // len(left), left[0][0].shape[1]
+
+
+def sent_kernel(*refs):
+    right_ref, _, out_ref = refs[-3:]
+    out_ref[...] = across(left_rows(refs[:-3]), right_ref[...]).astype(bf16)
 
 
 def sent_call(left, right, at, columns, token):
-    count, width = left.shape
+    left, count, width = left_parts(left, right)
     block = width // 4
     return pl.pallas_call(
         sent_kernel,
         grid=(2,),
         in_specs=[
-            pl.BlockSpec((count, block), lambda i: (0, 2 + i)),
-            fixed(count, columns, 0, at // columns),
-            ANYWHERE,
-        ],
+            pl.BlockSpec((count, block), lambda i, row=row: (row, 2 + i)) for _, row in left
+        ]
+        + [fixed(right.shape[0], columns, 0, at // columns), ANYWHERE],
         out_specs=pl.BlockSpec((block, columns), lambda i: (i, 0)),
         out_shape=shape_of(2 * block, columns, bf16),
         compiler_params=LIMIT,
         cost_estimate=estimate(4 * count * block * columns),
-    )(left, right, token)
-
-
-def kept_kernel(left_ref, right_ref, got_ref, token_ref, keep_ref, send_ref):
-    total = across(left_ref[...], right_ref[...]) + got_ref[...].astype(f32)
+    )(*[array for array, _ in left], right, token)
+
+
+def kept_kernel(*refs):
+    right_ref, got_ref, _, keep_ref, send_ref = refs[-5:]
+    total = across(left_rows(refs[:-5]), right_ref[...]) + got_ref[...].astype(f32)
     put_by_step((keep_ref, send_ref), (total, total))
 
 
 def kept_call(left, right, at, columns, got, token):
-    count, width = left.shape
+    left, count, width = left_parts(left, right)
     block = width // 4
     return pl.pallas_call(
         kept_kernel,
         grid=(2,),
-        in_specs=[
-            pl.BlockSpec((count, block), lambda i: (0, i)),
-            fixed(count, columns, 0, at // columns),
+        in_specs=[pl.BlockSpec((count, block), lambda i, row=row: (row, i)) for _, row in left]
+        + [
+            fixed(right.shape[0], columns, 0, at // columns),
             pl.BlockSpec((block, columns), lambda i: (i, 0)),
             ANYWHERE,
         ],
@@ -333,7 +348,7 @@
         out_shape=[shape_of(block, columns, f32), shape_of(block, columns, bf16)],
         compiler_params=LIMIT,
         cost_estimate=estimate(4 * count * block * columns),
-    )(left, right, got, token)
+    )(*[array for array, _ in left], right, got, token)
 
 
 def sum_kernel(count, *refs):
@@ -385,7 +400,7 @@
     bands = dqkv_ref.shape[1] // band
     for k in range(bands):
         in_q = k < bands // 2
-        place = pl.ds((k if in_q else k - bands // 2) * band, band)
+        place = pl.ds((k if in_q else k - bands // 2 + 1) * band, band)
         found = piece_rows(piece_refs[:4] if in_q else piece_refs[4:], place, in_q)
         dn1 = dn1 + against(dqkv_ref[:, pl.ds(k * band, band)], found)
     part = norm_back(dn1, x_ref[...].astype(f32), gains_ref[:1])
@@ -394,23 +409,25 @@
     out_ref[...] = dmid_ref[...] + against(high, pick_ref[...]) + against(low, pick_ref[...])
 
 
-def down_kernel(hidden_ref, down_ref, token_ref, *out_refs):
-    rows = against(hidden_ref[...], down_ref[...])
+def down_kernel(hidden_ref, near_ref, far_ref, token_ref, *out_refs):
+    parts = [against(hidden_ref[...], ref[...]) for ref in (near_ref, far_ref)]
+    rows = jnp.concatenate(parts, axis=1)
     put_by_step(out_refs, [rows] * 4)
 
 
-def down_call(hidden, down, token):
+def down_call(hidden, near, far, token):
     rows, ff = hidden.shape
-    width, block = down.shape[0], hidden.shape[0] // 4
+    width, block = 2 * near.shape[0], hidden.shape[0] // 4
     return pl.pallas_call(
         down_kernel,
         grid=(4,),
-        in_specs=[pl.BlockSpec((block, ff), lambda i: (i, 0)), fixed(width, ff), ANYWHERE],
+        in_specs=[pl.BlockSpec((block, ff), lambda i: (i, 0))]
+        + [fixed(*near.shape), fixed(*far.shape), ANYWHERE],
         out_specs=[fixed(block, width)] * 4,
         out_shape=[shape_of(block, width, bf16)] * 4,
         compiler_params=LIMIT,
         cost_estimate=estimate(2 * rows * width * ff),
-    )(hidden, down, token)
+    )(hidden, near, far, token)
 
 
 def layer_kernel(own_ref, core_ref, x_ref, pick_ref, middle_ref, token_ref, out_ref):
@@ -419,17 +436,86 @@
     out_ref[...] = total.astype(bf16)
 
 
-def kernel_call(body, outs, cost, *args, token=None, scratch=()):
-    tokens = () if token is None else (token,)
+def join_kernel(plan, *refs):
+    outs = refs[-len(plan) :]
+    for out, pieces in zip(outs, plan):
+        first, width = 0, out.shape[1]
+        for k, column in pieces:
+            rows = refs[k].shape[0]
+            out[first : first + rows, :] = refs[k][:, column : column + width]
+            first += rows
+
+
+def pick_kernel(*refs):
+    for source, out in zip(refs[:3], refs[-3:]):
+        rows = lax.broadcasted_iota(jnp.int32, out.shape, 0)
+        out[...] = jnp.where(rows == source[...], 1.0, 0.0).astype(bf16)
+
+
+def order_kernel(count, *refs):
+    pick_ref, out_ref = refs[count], refs[-1]
+    n = refs[0].shape[0]
+    for k, ref in enumerate(refs[:count]):
+        out_ref[k * n : (k + 1) * n, :] = product(ref[...], pick_ref[...]).astype(bf16)
+
+
+def two_kernel(*refs):
+    gu_z, down_z, xs_y, ys_x = refs[:4]
+    both_ref, xs_ref, ys_ref = refs[-3:]
+    columns = gu_z.shape[1]
+    both_ref[:, :columns], both_ref[:, columns:] = gu_z[...], down_z[...]
+    xs_ref[...] = xs_y[...]
+    ys_ref[...] = ys_x[...]
+
+
+def join_call(arrays, plan, widths, token):
+    outs = [
+        shape_of(sum(arrays[k].shape[0] for k, _ in pieces), width, bf16)
+        for pieces, width in zip(plan, widths)
+    ]
+    return kernel_call(
+        functools.partial(join_kernel, plan), outs, estimate(0), *arrays, token=token
+    )
+
+
+def output_kernel(*refs):
+    att_ref, pick_out_ref, x_ref, gain_ref, pick_mlp_ref, *piece_refs = refs[:13]
+    rel_ref, middle_ref, n2_ref = refs[-3:]
+    att = product(att_ref[...], pick_out_ref[...]).astype(bf16)
+    rel_ref[...] = att
+    everything = slice(None)
+    left = product(att, piece_rows(piece_refs[:4], everything, True))
+    right = product(att, piece_rows(piece_refs[4:], everything, False))
+    middle = x_ref[...].astype(f32) + jnp.concatenate([left, right], axis=1)
+    middle_ref[...] = middle
+    scale = lax.rsqrt(jnp.mean(middle * middle, axis=1, keepdims=True) + EPSILON)
+    n2 = (middle * scale * gain_ref[...]).astype(bf16)
+    n2_ref[...] = product(n2, pick_mlp_ref[...]).astype(bf16)
+
+
+def kernel_call(body, outs, cost, *args, token=(), scratch=()):
+    tokens = token if isinstance(token, tuple) else (token,)
+    arrays, specs = [], []
+
+    def alone(shape, place=None):
+        where = (0,) * len(shape) if place is None else (0, place)
+        return pl.BlockSpec(shape, lambda i: where, pipeline_mode=pl.Buffered(1))
+
+    for arg in args:
+        array, (columns, place) = arg if isinstance(arg, tuple) else (arg, (None, None))
+        arrays.append(array)
+        shape = array.shape if columns is None else (array.shape[0], columns)
+        specs.append(alone(shape, place))
     return pl.pallas_call(
         body,
+        grid=(1,),
         out_shape=outs,
-        in_specs=[pl.BlockSpec(memory_space=pltpu.VMEM)] * len(args) + [ANYWHERE] * len(tokens),
-        out_specs=[pl.BlockSpec(memory_space=pltpu.VMEM)] * len(outs),
+        in_specs=specs + [ANYWHERE] * len(tokens),
+        out_specs=[alone(out.shape) for out in outs],
         scratch_shapes=list(scratch),
         compiler_params=LIMIT,
         cost_estimate=cost,
-    )(*args, *tokens)
+    )(*arrays, *tokens)
 
 
 def after(array, *others):
@@ -515,70 +601,72 @@
         own_mlp = jnp.concatenate([own_gu, own_down], axis=1)
 
         attn_source = rel_source(me, attn_masks, shard, width)
-        pick_attn = one_hot(attn_source)
         head, lane = attn_source // HEAD, attn_source % HEAD
-        pick_out = one_hot((head % GROUP * KV_HEADS + head // GROUP) * HEAD + lane)
-        pick_mlp = one_hot(
-            rel_source(dp_i, [m // tp_n for m in mlp_masks], shard * tp_n, width)
-        )
-
-        def order(array, pick):
-            return product(array, pick).astype(bf16)
+        out_source = (head % GROUP * KV_HEADS + head // GROUP) * HEAD + lane
+        mlp_source = rel_source(dp_i, [m // tp_n for m in mlp_masks], shard * tp_n, width)
 
         def restore(array, pick):
             return against(array, pick)
 
-        def middle_swap(array):
-            n = array.shape[0] // 4
-            return join([array[:n], array[2 * n : 3 * n], array[n : 2 * n], array[3 * n :]])
-
-        dy_rel = order(after(dy_low, own_attn), pick_mlp)
-        *far, mlp_y, dy_x = together(
-            *gather_far(own_attn), swap(own_mlp, y_mask), swap(dy_rel, x_mask)
-        )
-        cut_q, cut_kv = slice(0, qw), slice(qw, qw + 2 * kw + LANES)
-        edge = cut_kv.stop + width // 2
-        cut_left, cut_right = slice(cut_kv.stop, edge), slice(edge, None)
-        q_four, kv_four, left_four, right_four = [
-            join([piece[:, cut] for piece in far]) for cut in (cut_q, cut_kv, cut_left, cut_right)
-        ]
-
-        q_x, kv_y, left_x, right_y, down_z = together(
-            swap(q_four, x_mask),
-            swap(kv_four, y_mask),
-            swap(left_four, x_mask),
-            swap(right_four, y_mask),
-            swap(after(own_down, q_four), z_masks[0]),
-        )
-        q_eight = join([q_four, q_x])
-        kv_eight = join([kv_four, kv_y])
-
-        q_y, kv_x, q_c, kv_c, gu_z = together(
-            swap(q_eight, y_mask),
-            swap(kv_eight, x_mask),
-            swap(q_eight, core_mask),
-            swap(kv_eight, core_mask),
-            swap(after(own_gu, q_x), z_masks[0]),
-        )
-
-        left_eight = join([left_four, left_x])
-        right_eight = join([right_four, right_y])
-        left_y = swap(after(left_eight, q_y), y_mask)
-        right_x = swap(after(right_eight, q_y), x_mask)
-        q_yc, kv_xc = together(swap(q_y, core_mask), swap(kv_x, core_mask))
-        q_pieces = [q_eight, q_y, q_c, q_yc]
-        kv_pieces = [kv_eight, kv_x, kv_c, kv_xc]
-
-        def next_far(own, first):
-            held, came = join([own, first]), [first]
-            for mask in z_masks[1:]:
-                came.append(swap(held, mask))
-                held = join([held, came[-1]])
-            return held, came
-
-        gu_near, gu_came = next_far(own_gu, gu_z)
-        gu_y1 = swap(gu_z, y_mask)
-        down_y1 = swap(down_z, y_mask)
+        far = gather_far(own_attn)
+        mlp_y = swap(own_mlp, y_mask)
+        dy_x = swap(dy_low, x_mask)
+        widths = (qw + half, half + 2 * kw + LANES)
+        at = (0, widths[0])
+        xs_four, ys_four = join_call(
+            far, [[(k, first) for k in range(len(far))] for first in at], widths, (dy_x, mlp_y)
+        )
+
+        xs_x = swap(xs_four, x_mask)
+        ys_y = swap(ys_four, y_mask)
+        down_z = swap(after(own_down, xs_four), z_masks[0])
+        pairs = (xs_four, xs_x, ys_four, ys_y)
+        xs_eight, ys_eight = join_call(
+            pairs, [[(2 * k, 0), (2 * k + 1, 0)] for k in range(2)], widths, down_z
+        )
+
+        xs_y = swap(xs_eight, y_mask)
+        ys_x = swap(ys_eight, x_mask)
+        gu_z = swap(after(own_gu, xs_eight), z_masks[0])
+        mlp_far = swap(after(own_mlp, xs_eight), z_masks[1])
+        xs_c = swap(xs_eight, core_mask)
+        mlp_z, xs_far, ys_far = kernel_call(
+            two_kernel,
+            [
+                shape_of(*own_mlp.shape, bf16),
+                shape_of(*xs_y.shape, bf16),
+                shape_of(*ys_x.shape, bf16),
+            ],
+            SHORT,
+            gu_z,
+            down_z,
+            xs_y,
+            ys_x,
+            token=(xs_c, mlp_far),
+        )
+        ys_c = swap(after(ys_eight, mlp_z), core_mask)
+        pick_attn, pick_out, pick_mlp = kernel_call(
+            pick_kernel,
+            [shape_of(width, width, bf16)] * 3,
+            SHORT,
+            *[source[None, :] for source in (attn_source, out_source, mlp_source)],
+            token=mlp_z,
+        )
+        (x_rel,) = kernel_call(
+            functools.partial(order_kernel, 1),
+            [shape_of(rows, width, bf16)],
+            SHORT,
+            x_low,
+            pick_attn,
+        )
+
+        x_pieces = [xs_eight, xs_y, xs_c, swap(xs_far, core_mask)]
+        y_pieces = [ys_eight, ys_x, ys_c, swap(ys_far, core_mask)]
+        q_pieces = [(piece, (qw, 0)) for piece in x_pieces]
+        left_pieces = [(piece, (half, qw // half)) for piece in x_pieces]
+        right_pieces = [(piece, (half, 0)) for piece in y_pieces]
+        mlp_y1 = swap(mlp_z, y_mask)
+        mlp_near = swap(mlp_z, z_masks[1])
 
         segment, position = jax.vmap(lambda own: pack_layout(own, per_pack))(lengths[:, 0])
         cosine, sine_part = rotary_tables(position, HEAD)
@@ -589,9 +677,6 @@
             & (segment < SLOTS - 1)[:, :, None]
         ).astype(f32)
 
-        inputs = x_low.astype(f32)
-        r1 = lax.rsqrt(jnp.mean(inputs * inputs, axis=1, keepdims=True) + EPSILON)
-        x_rel = order(x_low, pick_attn)
         half_tables = (cosine.reshape(rows, -1), sine_part.reshape(rows, -1))
         cos_band = jnp.tile(half_tables[0], (1, BAND // half_tables[0].shape[1]))
         sin_band = jnp.tile(jnp.concatenate([-half_tables[1], half_tables[1]], axis=1), (1, 4))
@@ -614,44 +699,64 @@
             sin_band,
             allowed,
             *q_pieces,
-            *kv_pieces,
-        )
-        g1_rel = gains_rel[:1]
+            *y_pieces,
+        )
         g2 = restore(gains_rel[1:2].astype(bf16), pick_attn)
-        n1_parts = [n1_rel[:, :half], n1_rel[:, half:]]
-
-        left_16 = middle_swap(join([left_eight, left_y]))
-        right_16 = join([right_eight, right_x])
-        out_16 = jnp.concatenate([left_16, right_16], axis=1)
-        out_pieces = [out_16, swap(out_16, core_mask)]
-        dy_near = join([dy_rel, dy_x])
-        dy_c = swap(after(dy_near, attended), core_mask)
-
-        att_rel = order(attended, pick_out)
-        att_parts = [att_rel[:, :half], att_rel[:, half:]]
-        middle = inputs + sum(product(a, b) for a, b in zip(att_parts, out_pieces))
-        r2 = lax.rsqrt(jnp.mean(middle * middle, axis=1, keepdims=True) + EPSILON)
-        n2 = (middle * r2 * g2).astype(bf16)
-
-        n2_rel = after(order(n2, pick_mlp), *gu_came, gu_y1, down_y1)
+        (mlp_last,) = join_call(
+            (mlp_far, mlp_near), [[(0, 0), (1, 0)]], [3 * ff], (attended, mlp_y1)
+        )
+        mlp_y2 = swap(mlp_last, y_mask)
+        att_rel, middle, n2_rel = kernel_call(
+            output_kernel,
+            [shape_of(rows, qw, bf16), shape_of(rows, width, f32), shape_of(rows, width, bf16)],
+            estimate(6 * rows * width * width),
+            attended,
+            pick_out,
+            x_low,
+            g2,
+            pick_mlp,
+            *left_pieces,
+            *right_pieces,
+            token=mlp_last,
+        )
+
         n2_x = swap(n2_rel, x_mask)
         n2_c = swap(n2_rel, core_mask)
-        down_near, down_came = next_far(own_down, after(down_z, n2_rel))
-        gu_full = join(
-            [gu_near, mlp_y[:, : 2 * ff], gu_y1] + [swap(a, y_mask) for a in gu_came[1:]]
-        )
-        down_full = join(
-            [down_near, mlp_y[:, 2 * ff :], down_y1] + [swap(a, y_mask) for a in down_came[1:]]
-        )
-        n2_all = join([n2_rel, n2_c, n2_x, swap(n2_x, core_mask)])
-        dy_all = join([dy_rel, dy_c[:rows], dy_x, dy_c[rows:]])
-
-        *grown, far_own, far_send = mlp_call(2, n2_all, dy_all, gu_full, down_full, n2_all)
+        (dy_near,) = kernel_call(
+            functools.partial(order_kernel, 2),
+            [shape_of(2 * rows, width, bf16)],
+            estimate(0),
+            dy_low,
+            dy_x,
+            pick_mlp,
+            token=n2_rel,
+        )
+        dy_c = swap(dy_near, core_mask)
+        near_parts, far_parts = (own_mlp, mlp_z, mlp_last), (mlp_y, mlp_y1, mlp_y2)
+        for mask in z_masks[2:]:
+            near_parts = near_parts + (swap(join(near_parts), mask),)
+            far_parts = far_parts + (swap(near_parts[-1], y_mask),)
+
+        def assemble(parts, token):
+            plan = [[(k, 0) for k in range(len(parts))], [(k, 2 * ff) for k in range(len(parts))]]
+            return join_call(parts, plan, (2 * ff, ff), token)
+
+        gu_near, down_near = assemble(near_parts, dy_near)
+        (n2_f,) = join_call((n2_x,), [[(0, 0)]], [width], (far_parts[-1], gu_near))
+        n2_xc = swap(n2_f, core_mask)
+        gu_far, down_far = assemble(far_parts, n2_f)
+        weights = (gu_near, gu_far, down_near, down_far)
+        n2_all = [(n2_rel, 0), (n2_x, 0), (n2_c, 0), (n2_xc, 0)]
+        dy_all = [(dy_near, 0), (dy_near, 1), (dy_c, 0), (dy_c, 1)]
+        weights = (gu_near, gu_far, down_near, down_far)
+        *grown, far_own, far_send = mlp_call(
+            1, n2_all[1::2], dy_all[1::2], weights, gu_far
+        )
         far_c = swap(far_send, core_mask)
         (dn2_sum,) = sum_call([far_own, far_c], [bf16], far_own)
         dn2_x = swap(dn2_sum, x_mask)
         hidden, dgu, near_own, near_send = mlp_call(
-            0, n2_all, dy_all, gu_full, down_full, *grown, dn2_sum
+            0, n2_all[::2], dy_all[::2], weights, *grown, dn2_sum
         )
         near_c = swap(near_send, core_mask)
         down_b = sent_call(dy_all, hidden, 0, ff, near_own)
@@ -670,12 +775,6 @@
             g2,
             token=down_b,
         )
-        og_b = sent_call(att_rel, dmb, 0, width, dmb)
-        og_c = swap(og_b, core_mask)
-        gate_b = sent_call(n2_all, dgu, 0, ff, og_b)
-        gate_got = swap(gate_b, y_mask)
-        og = kept_call(att_rel, dmb, 0, width, og_c, gate_b)
-        og_x = swap(og[1], x_mask)
         (dqkv,) = kernel_call(
             functools.partial(backward_kernel, *shapes),
             [shape_of(rows, wide, bf16)],
@@ -686,12 +785,14 @@
             sin_band,
             allowed,
             pick_out,
-            *out_pieces,
-            token=og[0],
+            *left_pieces,
+            *right_pieces,
             scratch=[pltpu.VMEM((rows, qw), bf16)],
         )
         qkv_b = sent_call(n1_rel, dqkv, 0, wide, dqkv)
         qkv_c = swap(qkv_b, core_mask)
+        gate_b = sent_call(n2_all, dgu, 0, ff, qkv_b)
+        gate_got = swap(gate_b, y_mask)
         far_mask, near_mask = z_masks[-1], z_masks[-2]
         step = [f32, bf16]
 
@@ -699,11 +800,14 @@
             pair = sum_call([pair[0], got], step, token)
             return pair, swap(pair[1], mask)
 
-        down_k = kept_call(dy_all, hidden, 0, ff, down_got, qkv_b)
+        qkv_k = kept_call(n1_rel, dqkv, 0, wide, qkv_c, gate_b)
+        qkv_got = swap(qkv_k[1], x_mask)
+        down_k = kept_call(dy_all, hidden, 0, ff, down_got, qkv_k[0])
         down_got = swap(down_k[1], far_mask)
-        qkv_k = kept_call(n1_rel, dqkv, 0, wide, qkv_c, down_k[0])
-        qkv_got = swap(qkv_k[1], x_mask)
-        og, og_got = onward(og, og_x, y_mask, qkv_k[0])
+        up_b = sent_call(n2_all, dgu, ff, ff, down_k[0])
+        up_got = swap(up_b, y_mask)
+        gate_k = kept_call(n2_all, dgu, 0, ff, gate_got, up_b)
+        gate_got = swap(gate_k[1], far_mask)
         (input_grad,) = kernel_call(
             functools.partial(first_norm_kernel, 2 * BAND),
             [shape_of(rows, width, f32)],
@@ -714,31 +818,32 @@
             pick_attn,
             dmid,
             *q_pieces,
-            *kv_pieces,
-            token=og[0],
+            *y_pieces,
+            token=gate_k[0],
         )
         down_k, down_got = onward(down_k, down_got, near_mask, input_grad)
-        up_b = sent_call(n2_all, dgu, ff, ff, down_k[0])
-        up_got = swap(up_b, y_mask)
-        gate_k = kept_call(n2_all, dgu, 0, ff, gate_got, up_b)
-        gate_got = swap(gate_k[1], far_mask)
-        og, og_got = onward(og, og_got, far_mask, gate_k[0])
-        down_grad = finish([down_k[0], down_got], og[0])
-        gate_k, gate_got = onward(gate_k, gate_got, near_mask, down_grad)
-        qkv_k, qkv_got = onward(qkv_k, qkv_got, y_mask, gate_k[0])
-        og, og_got = onward(og, og_got, near_mask, qkv_k[0])
-        lay = down_call(hidden, down_full, og[0])
+        gate_k, gate_got = onward(gate_k, gate_got, near_mask, down_k[0])
+        up_k = kept_call(n2_all, dgu, ff, ff, up_got, gate_k[0])
+        up_got = swap(up_k[1], far_mask)
+        og_b = sent_call(att_rel, dmb, 0, width, up_k[0])
+        og_c = swap(og_b, core_mask)
+        down_grad = finish([down_k[0], down_got], og_b)
+        qkv_k, qkv_got = onward(qkv_k, qkv_got, y_mask, down_grad)
+        og = kept_call(att_rel, dmb, 0, width, og_c, qkv_k[0])
+        og_got = swap(og[1], x_mask)
+        gate_grad = finish([gate_k[0], gate_got], og[0])
+        up_k, up_got = onward(up_k, up_got, near_mask, gate_grad)
+        lay = down_call(hidden, *weights[2:], up_k[0])
         lay_f = swap(lay[3], core_mask)
-        output_grad = finish([og[0], og_got], lay[0])
-        up_k = kept_call(n2_all, dgu, ff, ff, up_got, output_grad)
-        up_got = swap(up_k[1], far_mask)
-        gate_grad = finish([gate_k[0], gate_got], up_k[0])
-        (lay_s,) = sum_call([lay[2], lay_f], [bf16], gate_grad)
+        og, og_got = onward(og, og_got, y_mask, lay[0])
+        (lay_s,) = sum_call([lay[1], lay_f], [bf16], og[0])
         lay_x = swap(lay_s, x_mask)
         qkv_k, qkv_got = onward(qkv_k, qkv_got, far_mask, lay_s)
-        lay_c = swap(after(lay[1], qkv_k[0]), core_mask)
-        up_k, up_got = onward(up_k, up_got, near_mask, qkv_k[0])
-        qkv_k, qkv_got = onward(qkv_k, qkv_got, near_mask, up_k[0])
+        og, og_got = onward(og, og_got, far_mask, qkv_k[0])
+        lay_c = swap(after(lay[2], og[0]), core_mask)
+        up_grad = finish([up_k[0], up_got], og[0])
+        qkv_k, qkv_got = onward(qkv_k, qkv_got, near_mask, up_grad)
+        og, og_got = onward(og, og_got, near_mask, qkv_k[0])
         (layer_out,) = kernel_call(
             layer_kernel,
             [shape_of(rows, width, bf16)],
@@ -748,14 +853,16 @@
             lay_x,
             pick_mlp,
             middle,
-            token=qkv_k[0],
-        )
-        up_grad = finish([up_k[0], up_got], layer_out)
-        qkv_grad = finish([qkv_k[0], qkv_got], up_grad)
+            token=og[0],
+        )
+        qkv_grad = finish([qkv_k[0], qkv_got], layer_out)
+        output_grad = finish([og[0], og_got], qkv_grad)
         q_grad, kv_grad = qkv_grad[:, :qw], qkv_grad[:, qw:]
         down_grad = down_grad.T
 
-        first = jnp.sum(own_attn[:, :wide].astype(f32) * qkv_grad, axis=1)
+        first = jnp.sum(own_attn[:, :qw].astype(f32) * q_grad, axis=1)
+        own_kv = own_attn[:, qw + width : qw + width + 2 * kw].astype(f32)
+        first = first + jnp.sum(own_kv * kv_grad, axis=1)
         first_gain_grad = first / first_gain.astype(f32)
         second = jnp.sum(
             gate_weight.astype(f32) * gate_grad + up_weight.astype(f32) * up_grad, axis=1

time: 571 us -> 550 us (0.963)
  Pallas kernels: 225 us -> 288 us
  local copies, waits for them, and re-layouts: 40.3 us -> 20 us
  other arithmetic: 26.9 us -> 9.09 us
  starting transfers between devices: 55.5 us -> 39.1 us
  matrix products: 18.9 us -> 2.72 us
  waiting for transfers between devices: 193 us -> 180 us
    pallas_call x8 -> x19, Pallas kernels: 112 us -> 174 us  [the longest x17 132 us: kernel_call(): pl.pallas_call(body, grid=(1,), out_shape=outs, in_specs=specs + [ANYWHER...]
    unnamed x125 -> x75, local copies, waits for them, and re-layouts: 32.3 us -> 13.8 us
    dot_general x6 -> x0, matrix products: 16.6 us -> none  [product(): return jnp.dot(left_side, right_side, preferred_element_type=f32)]
    ppermute x57 -> x50, starting transfers between devices: 55.5 us -> 39.1 us  [swap(): return lax.ppermute(array, AXES, [(i, i ^ mask) for i in range(world)])]
    ppermute x57 -> x50, waiting for transfers between devices: 193 us -> 180 us  [swap(): return lax.ppermute(array, AXES, [(i, i ^ mask) for i in range(world)])]
    convert_element_type x3 -> x0, other arithmetic: 12.8 us -> none  [one_hot(): return (rows == source[None, :]).astype(bf16)]
  transfers between devices with their start and end apart: 57 -> 50, of which waited for: 19 -> 22; matrix products, arithmetic and copies ran while one was open for 12% -> 3% of each run, Pallas kernels for 35% -> 46%
where the time goes in v3:
time: 550 us; the launch traced here: 541 us
  Pallas kernels  288 us (52%)
  waiting for transfers between devices  180 us (33%)
  starting transfers between devices  39.1 us (7%)
  local copies, waits for them, and re-layouts  20 us (4%)
  other arithmetic  9.09 us (2%)
    ppermute x50, waiting for transfers between devices, swap(): return lax.ppermute(array, AXES, [(i, i ^ mask) for i in range(world)])  180 us
    pallas_call x17, Pallas kernels, kernel_call(): pl.pallas_call(body, grid=(1,), out_shape=outs, in_specs=specs + [ANYWHER...  132 us
    pallas_call x2, Pallas kernels, mlp_call(): pl.pallas_call(functools.partial(mlp_kernel, ff), grid=(2,), in_specs=[fi...  41.9 us
    pallas_call x16, Pallas kernels, sum_call(): pl.pallas_call(functools.partial(sum_kernel, len(arrays)), grid=(columns...  39.2 us
    ppermute x50, starting transfers between devices, swap(): return lax.ppermute(array, AXES, [(i, i ^ mask) for i in range(world)])  39.1 us
    pallas_call x5, Pallas kernels, kept_call(): pl.pallas_call(kept_kernel, grid=(2,), in_specs=[pl.BlockSpec((count, blo...  36.2 us
    pallas_call x5, Pallas kernels, sent_call(): pl.pallas_call(sent_kernel, grid=(2,), in_specs=[pl.BlockSpec((count, blo...  28.6 us
    unnamed x75, local copies, waits for them, and re-layouts  13.8 us
  transfers between devices with their start and end apart: 50, of which 22 were waited for; matrix products, arithmetic and copies ran while one was open for 3% of the time, Pallas kernels for 46%

profile of v3, /device:TPU:0, one launch (start us, length us, event | category | flops | bytes accessed | tf_op | source)
XLA Modules:
  0.0 540.7 jit_solution(2450208120518041858)
XLA Ops:
  13.7 11.0 %collective-permute-done.2.refs_3_ = bf16[48,4736]{1,0:T(8,128)(2,1)S(1)} collective-permute-done((bf16[48,4736]{1,0:T(8,128)(2,1)}, bf16[48,4736]{1,0:T(8,128)(2,1)S(1)}, u32[]{:S(2)}, u32[]{:S(2)}) %collective-permute-start.2) | collective-permute-done | bytes 454688 | tf_op jit(solution)/shard_map/ppermute | solution.py:534
  24.8 9.1 %collective-permute-done.1.refs_2_ = bf16[48,4736]{1,0:T(8,128)(2,1)S(1)} collective-permute-done((bf16[48,4736]{1,0:T(8,128)(2,1)}, bf16[48,4736]{1,0:T(8,128)(2,1)S(1)}, u32[]{:S(2)}, u32[]{:S(2)}) %collective-permute-start.1) | collective-permute-done | bytes 454688 | tf_op jit(solution)/shard_map/ppermute | solution.py:534
  33.9 17.5 %collective-permute-done.refs_1_ = bf16[48,4736]{1,0:T(8,128)(2,1)S(1)} collective-permute-done((bf16[48,4736]{1,0:T(8,128)(2,1)}, bf16[48,4736]{1,0:T(8,128)(2,1)S(1)}, u32[]{:S(2)}, u32[]{:S(2)}) %collective-permute-start) | collective-permute-done | bytes 454688 | tf_op jit(solution)/shard_map/ppermute | solution.py:534
  56.3 18.0 %collective-permute-done.7.refs_4_.refs_1_ = bf16[192,1024]{1,0:T(8,128)(2,1)S(1)} collective-permute-done((bf16[192,1024]{1,0:T(8,128)(2,1)S(1)}, bf16[192,1024]{1,0:T(8,128)(2,1)S(1)}, u32[]{:S(2)}, u32[]{:S(2)}) %collective-permute-start.7) | collective-permute-done | bytes 393248 | tf_op jit(solution)/shard_map/ppermute | solution.py:534
  87.9 39.3 %collective-permute-done.8.refs_0_ = bf16[192,2048]{1,0:T(8,128)(2,1)} collective-permute-done((bf16[192,2048]{1,0:T(8,128)(2,1)}, bf16[192,2048]{1,0:T(8,128)(2,1)}, u32[]{:S(2)}, u32[]{:S(2)}) %collective-permute-start.8) | collective-permute-done | bytes 786464 | tf_op jit(solution)/shard_map/ppermute | solution.py:534
  155.4 17.5 %shard_map.209 = (bf16[384,3072]{1,0:T(8,128)(2,1)}, bf16[384,1536]{1,0:T(8,128)(2,1)}, bf16[384,1536]{1,0:T(8,128)(2,1)}, f32[8,1536]{1,0:T(8,128)}) custom-call(bf16[384,1536]{1,0:T(8,128)(2,1)} %shard_map.208.refs_0_.refs_1_, f32[384,384]{1,0:T(8,128)} %copy.46.refs_1_.refs_2_, f32[384,384]{1,0:T(8,128)} %copy.47.refs_2_.refs_3_, ...), custom_call_target="tpu_custom_call" | custom-call | flops 99999997952 | tf_op jit(solution)/shard_map/pallas_call | solution.py:509
  180.5 12.6 %shard_map.211 = (bf16[384,1536]{1,0:T(8,128)(2,1)}, f32[384,1536]{1,0:T(8,128)}, bf16[384,1536]{1,0:T(8,128)(2,1)}) custom-call(bf16[384,1536]{1,0:T(8,128)(2,1)} %get-tuple-element.91.refs_2_.refs_0_, bf16[1536,1536]{1,0:T(8,128)(2,1)} %get-tuple-element.92.refs_1_.refs_5_, bf16[384,1536]{1,0:T(8,128)(2,1)} %bitcast.30, f32[1,1536]{1,0:T(1,128)} %fusion.8.refs_3_.refs_6_, ...), custom_call_target="tpu_custom_call" | custom-call | flops 99999997952 | tf_op jit(solution)/shard_map/pallas_call | solution.py:509
  194.6 8.3 %shard_map.212.refs_3_.refs_2_.refs_0_.refs_1_ = bf16[768,1536]{1,0:T(8,128)(2,1)} custom-call(bf16[384,1536]{1,0:T(8,128)(2,1)} %bitcast.36, bf16[384,1536]{1,0:T(8,128)(2,1)} %collective-permute-done.3.refs_4_.refs_1_, bf16[1536,1536]{1,0:T(8,128)(2,1)} %get-tuple-element.94.refs_4_.refs_2_.refs_3_.pick_ref, ...), custom_call_target="tpu_custom_call" | custom-call | flops 99999997952 | tf_op jit(solution)/shard_map/pallas_call | solution.py:509
  207.6 13.3 %collective-permute-done.21.refs_0_.refs_1_ = bf16[384,1536]{1,0:T(8,128)(2,1)} collective-permute-done((bf16[384,1536]{1,0:T(8,128)(2,1)}, bf16[384,1536]{1,0:T(8,128)(2,1)}, u32[]{:S(2)}, u32[]{:S(2)}) %collective-permute-start.21) | collective-permute-done | bytes 1179680 | tf_op jit(solution)/shard_map/ppermute | solution.py:534
  220.9 11.4 %collective-permute-done.20.refs_1_.refs_2_ = bf16[384,3072]{1,0:T(8,128)(2,1)} collective-permute-done((bf16[384,3072]{1,0:T(8,128)(2,1)}, bf16[384,3072]{1,0:T(8,128)(2,1)}, u32[]{:S(2)}, u32[]{:S(2)}) %collective-permute-start.20) | collective-permute-done | bytes 2359328 | tf_op jit(solution)/shard_map/ppermute | solution.py:534
  240.5 21.2 %shard_map.216 = (bf16[1536,1024]{1,0:T(8,128)(2,1)}, bf16[1536,2048]{1,0:T(8,128)(2,1)}, bf16[384,1536]{1,0:T(8,128)(2,1)}, bf16[384,1536]{1,0:T(8,128)(2,1)}) custom-call(bf16[384,1536]{1,0:T(8,128)(2,1)} %collective-permute-done.21.refs_0_.refs_1_, bf16[384,1536]{1,0:T(8,128)(2,1)} %copy-done.21, ...), custom_call_target="tpu_custom_call" | custom-call | flops 99999997952 | tf_op jit(solution)/shard_map/pallas_call | solution.py:282
  272.1 20.7 %shard_map.218 = (bf16[1536,1024]{1,0:T(8,128)(2,1)}, bf16[1536,2048]{1,0:T(8,128)(2,1)}, bf16[384,1536]{1,0:T(8,128)(2,1)}, bf16[384,1536]{1,0:T(8,128)(2,1)}) custom-call(bf16[384,1536]{1,0:T(8,128)(2,1)} %get-tuple-element.95.refs_3_.refs_0_, bf16[384,1536]{1,0:T(8,128)(2,1)} %copy-done.22, ...), custom_call_target="tpu_custom_call", output_to_operand_aliasing={{0}: (8, {}), {1}: (9, {})} | custom-call | flops 99999997952 | tf_op jit(solution)/shard_map/pallas_call | solution.py:282
  301.7 8.7 %shard_map.220 = (f32[384,1536]{1,0:T(8,128)}, bf16[384,1536]{1,0:T(8,128)(2,1)}) custom-call(bf16[384,1536]{1,0:T(8,128)(2,1)} %get-tuple-element.106.refs_5_.refs_0_, bf16[384,1536]{1,0:T(8,128)(2,1)} %copy-done.26, bf16[384,1536]{1,0:T(8,128)(2,1)} %collective-permute-done.26.refs_2_, ...), custom_call_target="tpu_custom_call" | custom-call | flops 99999997952 | tf_op jit(solution)/shard_map/pallas_call | solution.py:509
  310.5 19.8 %shard_map.221.refs_1_.refs_2_.refs_0_ = bf16[384,3072]{1,0:T(8,128)(2,1)} custom-call(bf16[384,1536]{1,0:T(8,128)(2,1)} %get-tuple-element.110.refs_0_.refs_1_, bf16[384,3072]{1,0:T(8,128)(2,1)} %get-tuple-element.111.refs_1_, f32[384,384]{1,0:T(8,128)} %copy.46.refs_1_.refs_2_, f32[384,384]{1,0:T(8,128)} %copy.47.refs_2_.refs_3_, ...), custom_call_target="tpu_custom_call" | custom-call | flops 99999997952 | tf_op jit(solution)/shard_map/pallas_call | solution.py:509
  346.7 9.0 %shard_map.224 = (f32[384,3072]{1,0:T(8,128)}, bf16[384,3072]{1,0:T(8,128)(2,1)}) custom-call(bf16[384,1536]{1,0:T(8,128)(2,1)} %get-tuple-element.107.refs_0_, bf16[384,3072]{1,0:T(8,128)(2,1)} %shard_map.221.refs_1_.refs_2_.refs_0_, bf16[768,3072]{1,0:T(8,128)(2,1)} %copy-done.16, bf16[768,1024]{1,0:T(8,128)(2,1)} %shard_map.223.refs_3_), custom_call_target="tpu_custom_call" | custom-call | flops 99999997952 | tf_op jit(solution)/shard_map/pallas_call | solution.py:338
  355.6 7.1 %shard_map.225 = (f32[384,1024]{1,0:T(8,128)}, bf16[384,1024]{1,0:T(8,128)(2,1)}) custom-call(bf16[768,1536]{1,0:T(8,128)(2,1)} %shard_map.212.refs_3_.refs_2_.refs_0_.refs_1_, bf16[768,1536]{1,0:T(8,128)(2,1)} %shard_map.212.refs_3_.refs_2_.refs_0_.refs_1_, bf16[768,1536]{1,0:T(8,128)(2,1)} %collective-permute-done.19.refs_3_.refs_2_, ...), custom_call_target="tpu_custom_call" | custom-call | flops 99999997952 | tf_op jit(solution)/shard_map/pallas_call | solution.py:338
  370.9 9.3 %collective-permute-done.29.refs_5_ = bf16[768,1024]{1,0:T(8,128)(2,1)} collective-permute-done((bf16[768,1024]{1,0:T(8,128)(2,1)}, bf16[768,1024]{1,0:T(8,128)(2,1)}, u32[]{:S(2)}, u32[]{:S(2)}) %collective-permute-start.29) | collective-permute-done | bytes 1572896 | tf_op jit(solution)/shard_map/ppermute | solution.py:534
  380.2 7.2 %shard_map.227 = (f32[384,1024]{1,0:T(8,128)}, bf16[384,1024]{1,0:T(8,128)(2,1)}) custom-call(bf16[384,1536]{1,0:T(8,128)(2,1)} %get-tuple-element.95.refs_3_.refs_0_, bf16[384,1536]{1,0:T(8,128)(2,1)} %collective-permute-done.21.refs_0_.refs_1_, bf16[384,1536]{1,0:T(8,128)(2,1)} %copy-done.22, bf16[384,1536]{1,0:T(8,128)(2,1)} %copy-done.21, ...), custom_call_target="tpu_custom_call" | custom-call | flops 99999997952 | tf_op jit(solution)/shard_map/pallas_call | solution.py:338
  389.4 16.8 %shard_map.228.refs_2_ = f32[384,1536]{1,0:T(8,128)} custom-call(bf16[384,3072]{1,0:T(8,128)(2,1)} %shard_map.221.refs_1_.refs_2_.refs_0_, bf16[384,1536]{1,0:T(8,128)(2,1)} %shard_map.208.refs_0_.refs_1_, f32[8,1536]{1,0:T(8,128)} %get-tuple-element.93.refs_2_, bf16[1536,1536]{1,0:T(8,128)(2,1)} %get-tuple-element.87.refs_1_.refs_3_, ...), custom_call_target="tpu_custom_call" | custom-call | flops 99999997952 | tf_op jit(solution)/shard_map/pallas_call | solution.py:509
  414.0 7.4 %shard_map.231 = (f32[384,1024]{1,0:T(8,128)}, bf16[384,1024]{1,0:T(8,128)(2,1)}) custom-call(bf16[384,1536]{1,0:T(8,128)(2,1)} %get-tuple-element.95.refs_3_.refs_0_, bf16[384,1536]{1,0:T(8,128)(2,1)} %collective-permute-done.21.refs_0_.refs_1_, bf16[384,1536]{1,0:T(8,128)(2,1)} %copy-done.22, bf16[384,1536]{1,0:T(8,128)(2,1)} %copy-done.21, ...), custom_call_target="tpu_custom_call" | custom-call | flops 99999997952 | tf_op jit(solution)/shard_map/pallas_call | solution.py:338
  426.2 10.1 %collective-permute-done.36.refs_1_ = bf16[192,1024]{1,0:T(8,128)(2,1)} collective-permute-done((bf16[192,1024]{1,0:T(8,128)(2,1)}, bf16[192,1024]{1,0:T(8,128)(2,1)}, u32[]{:S(2)}, u32[]{:S(2)}) %collective-permute-start.36) | collective-permute-done | bytes 393248 | tf_op jit(solution)/shard_map/ppermute | solution.py:534
  459.3 10.6 %shard_map.238 = (bf16[384,1536]{1,0:T(8,128)(2,1)}, bf16[384,1536]{1,0:T(8,128)(2,1)}, bf16[384,1536]{1,0:T(8,128)(2,1)}, bf16[384,1536]{1,0:T(8,128)(2,1)}) custom-call(bf16[1536,1024]{1,0:T(8,128)(2,1)} %get-tuple-element.104.refs_4_.hidden_ref, bf16[768,1024]{1,0:T(8,128)(2,1)} %get-tuple-element.98.refs_6_.near_ref, ...), custom_call_target="tpu_custom_call" | custom-call | flops 99999997952 | tf_op jit(solution)/shard_map/pallas_call | solution.py:421
  469.9 7.2 %collective-permute-done.37.refs_1_ = bf16[384,1536]{1,0:T(8,128)(2,1)} collective-permute-done((bf16[384,1536]{1,0:T(8,128)(2,1)}, bf16[384,1536]{1,0:T(8,128)(2,1)}, u32[]{:S(2)}, u32[]{:S(2)}) %collective-permute-start.37) | collective-permute-done | bytes 1179680 | tf_op jit(solution)/shard_map/ppermute | solution.py:534
  511.4 11.9 %collective-permute-done.42.x_ref = bf16[384,1536]{1,0:T(8,128)(2,1)} collective-permute-done((bf16[384,1536]{1,0:T(8,128)(2,1)}, bf16[384,1536]{1,0:T(8,128)(2,1)}, u32[]{:S(2)}, u32[]{:S(2)}) %collective-permute-start.42) | collective-permute-done | bytes 1179680 | tf_op jit(solution)/shard_map/ppermute | solution.py:534
  (231 shorter events, 214.1 us)
Async XLA Ops:
  2.1 49.3 %collective-permute-start.4 = (bf16[192,3072]{1,0:T(8,128)(2,1)S(1)}, bf16[192,3072]{1,0:T(8,128)(2,1)S(1)}, u32[]{:S(2)}, u32[]{:S(2)}) collective-permute-start(bf16[192,3072]{1,0:T(8,128)(2,1)S(1)} %pad_maximum_fusion.refs_0_), channel_id=1, source_target_pairs={{0,4},{1,5},{2,6},{3,7},{4,0},{5,1},{6,2},{7,3},{8,12},{9,13},{10,... | collective-permute-start | bytes 3538952 | tf_op jit(solution)/shard_map/ppermute | solution.py:534
  5.1 46.3 %collective-permute-start.3 = (bf16[384,1536]{1,0:T(8,128)(2,1)S(1)}, bf16[384,1536]{1,0:T(8,128)(2,1)}, u32[]{:S(2)}, u32[]{:S(2)}) collective-permute-start(bf16[384,1536]{1,0:T(8,128)(2,1)S(1)} %bitcast.38), channel_id=1, source_target_pairs={{0,2},{1,3},{2,0},{3,1},{4,6},{5,7},{6,4},{7,5},{8,10},{9,11},{10,... | collective-permute-start | bytes 3538952 | tf_op jit(solution)/shard_map/ppermute | solution.py:534
  12.9 38.5 %collective-permute-start = (bf16[48,4736]{1,0:T(8,128)(2,1)}, bf16[48,4736]{1,0:T(8,128)(2,1)S(1)}, u32[]{:S(2)}, u32[]{:S(2)}) collective-permute-start(bf16[48,4736]{1,0:T(8,128)(2,1)} %shard_map.203.refs_0_), channel_id=1, source_target_pairs={{0,16},{1,17},{2,18},{3,19},{4,20},{5,21},{6,22},{7,23},{8,24},{9,... | collective-permute-start | bytes 1363976 | tf_op jit(solution)/shard_map/ppermute | solution.py:534
  82.2 47.1 %collective-permute-start.10 = (bf16[384,2432]{1,0:T(8,128)(2,1)}, bf16[384,2432]{1,0:T(8,128)(2,1)S(1)}, u32[]{:S(2)}, u32[]{:S(2)}) collective-permute-start(bf16[384,2432]{1,0:T(8,128)(2,1)} %get-tuple-element.89.refs_8_.refs_9_.refs_10_), channel_id=1, source_target_pairs={{0,2},{1,3},{2,0},{3,1},{4,6},{5,7},{6,4},{7,5},{8,10},{9,11},{10,... | collective-permute-start | bytes 5603336 | tf_op jit(solution)/shard_map/ppermute | solution.py:534
  82.7 46.6 %collective-permute-start.11 = (bf16[384,2304]{1,0:T(8,128)(2,1)}, bf16[384,2304]{1,0:T(8,128)(2,1)}, u32[]{:S(2)}, u32[]{:S(2)}) collective-permute-start(bf16[384,2304]{1,0:T(8,128)(2,1)} %get-tuple-element.82.refs_4_.refs_5_.refs_6_), channel_id=1, source_target_pairs={{0,1},{1,0},{2,3},{3,2},{4,5},{5,4},{6,7},{7,6},{8,9},{9,8},{10,11... | collective-permute-start | bytes 5308424 | tf_op jit(solution)/shard_map/ppermute | solution.py:534
  82.8 46.6 %collective-permute-start.9 = (bf16[384,2304]{1,0:T(8,128)(2,1)}, bf16[384,2304]{1,0:T(8,128)(2,1)}, u32[]{:S(2)}, u32[]{:S(2)}) collective-permute-start(bf16[384,2304]{1,0:T(8,128)(2,1)} %get-tuple-element.82.refs_4_.refs_5_.refs_6_), channel_id=1, source_target_pairs={{0,4},{1,5},{2,6},{3,7},{4,0},{5,1},{6,2},{7,3},{8,12},{9,13},{10,... | collective-permute-start | bytes 5308424 | tf_op jit(solution)/shard_map/ppermute | solution.py:534
  84.3 45.1 %collective-permute-start.12 = (bf16[192,3072]{1,0:T(8,128)(2,1)S(1)}, bf16[192,3072]{1,0:T(8,128)(2,1)}, u32[]{:S(2)}, u32[]{:S(2)}) collective-permute-start(bf16[192,3072]{1,0:T(8,128)(2,1)S(1)} %copy-done.7), channel_id=1, source_target_pairs={{0,8},{1,9},{2,10},{3,11},{4,12},{5,13},{6,14},{7,15},{8,0},{9,1},... | collective-permute-start | bytes 3538952 | tf_op jit(solution)/shard_map/ppermute | solution.py:534
  85.2 41.9 %collective-permute-start.8 = (bf16[192,2048]{1,0:T(8,128)(2,1)}, bf16[192,2048]{1,0:T(8,128)(2,1)}, u32[]{:S(2)}, u32[]{:S(2)}) collective-permute-start(bf16[192,2048]{1,0:T(8,128)(2,1)} %pad_maximum_fusion.1), channel_id=1, source_target_pairs={{0,16},{1,17},{2,18},{3,19},{4,20},{5,21},{6,22},{7,23},{8,24},{9,... | collective-permute-start | bytes 2359304 | tf_op jit(solution)/shard_map/ppermute | solution.py:534
  140.8 34.9 %collective-permute-start.17 = (bf16[192,3072]{1,0:T(8,128)(2,1)}, bf16[192,3072]{1,0:T(8,128)(2,1)}, u32[]{:S(2)}, u32[]{:S(2)}) collective-permute-start(bf16[192,3072]{1,0:T(8,128)(2,1)} %get-tuple-element.86.refs_3_.refs_1_), channel_id=1, source_target_pairs={{0,4},{1,5},{2,6},{3,7},{4,0},{5,1},{6,2},{7,3},{8,12},{9,13},{10,... | collective-permute-start | bytes 3538952 | tf_op jit(solution)/shard_map/ppermute | solution.py:534
  141.3 34.4 %collective-permute-start.16 = (bf16[192,3072]{1,0:T(8,128)(2,1)}, bf16[192,3072]{1,0:T(8,128)(2,1)}, u32[]{:S(2)}, u32[]{:S(2)}) collective-permute-start(bf16[192,3072]{1,0:T(8,128)(2,1)} %get-tuple-element.86.refs_3_.refs_1_), channel_id=1, source_target_pairs={{0,8},{1,9},{2,10},{3,11},{4,12},{5,13},{6,14},{7,15},{8,0},{9,1},... | collective-permute-start | bytes 3538952 | tf_op jit(solution)/shard_map/ppermute | solution.py:534
  179.0 53.4 %collective-permute-start.20 = (bf16[384,3072]{1,0:T(8,128)(2,1)}, bf16[384,3072]{1,0:T(8,128)(2,1)}, u32[]{:S(2)}, u32[]{:S(2)}) collective-permute-start(bf16[384,3072]{1,0:T(8,128)(2,1)} %shard_map.210.refs_13_.refs_2_), channel_id=1, source_target_pairs={{0,4},{1,5},{2,6},{3,7},{4,0},{5,1},{6,2},{7,3},{8,12},{9,13},{10,... | collective-permute-start | bytes 7077896 | tf_op jit(solution)/shard_map/ppermute | solution.py:534
  193.1 27.8 %collective-permute-start.21 = (bf16[384,1536]{1,0:T(8,128)(2,1)}, bf16[384,1536]{1,0:T(8,128)(2,1)}, u32[]{:S(2)}, u32[]{:S(2)}) collective-permute-start(bf16[384,1536]{1,0:T(8,128)(2,1)} %get-tuple-element.95.refs_3_.refs_0_), channel_id=1, source_target_pairs={{0,2},{1,3},{2,0},{3,1},{4,6},{5,7},{6,4},{7,5},{8,10},{9,11},{10,... | collective-permute-start | bytes 3538952 | tf_op jit(solution)/shard_map/ppermute | solution.py:534
  207.6 31.9 %collective-permute-start.19 = (bf16[768,1536]{1,0:T(8,128)(2,1)}, bf16[768,1536]{1,0:T(8,128)(2,1)}, u32[]{:S(2)}, u32[]{:S(2)}) collective-permute-start(bf16[768,1536]{1,0:T(8,128)(2,1)} %shard_map.212.refs_3_.refs_2_.refs_0_.refs_1_), channel_id=1, source_target_pairs={{0,1},{1,0},{2,3},{3,2},{4,5},{5,4},{6,7},{7,6},{8,9},{9,8},{10,11... | collective-permute-start | bytes 7077896 | tf_op jit(solution)/shard_map/ppermute | solution.py:534
  269.5 31.2 %collective-permute-start.26 = (bf16[384,1536]{1,0:T(8,128)(2,1)}, bf16[384,1536]{1,0:T(8,128)(2,1)}, u32[]{:S(2)}, u32[]{:S(2)}) collective-permute-start(bf16[384,1536]{1,0:T(8,128)(2,1)} %shard_map.217.refs_10_), channel_id=1, source_target_pairs={{0,2},{1,3},{2,0},{3,1},{4,6},{5,7},{6,4},{7,5},{8,10},{9,11},{10,... | collective-permute-start | bytes 3538952 | tf_op jit(solution)/shard_map/ppermute | solution.py:534
  299.2 56.4 %collective-permute-start.24 = (bf16[768,1024]{1,0:T(8,128)(2,1)}, bf16[768,1024]{1,0:T(8,128)(2,1)}, u32[]{:S(2)}, u32[]{:S(2)}) collective-permute-start(bf16[768,1024]{1,0:T(8,128)(2,1)} %shard_map.219.refs_7_), channel_id=1, source_target_pairs={{0,4},{1,5},{2,6},{3,7},{4,0},{5,1},{6,2},{7,3},{8,12},{9,13},{10,... | collective-permute-start | bytes 4718600 | tf_op jit(solution)/shard_map/ppermute | solution.py:534
  342.6 37.5 %collective-permute-start.29 = (bf16[768,1024]{1,0:T(8,128)(2,1)}, bf16[768,1024]{1,0:T(8,128)(2,1)}, u32[]{:S(2)}, u32[]{:S(2)}) collective-permute-start(bf16[768,1024]{1,0:T(8,128)(2,1)} %shard_map.223.refs_3_), channel_id=1, source_target_pairs={{0,4},{1,5},{2,6},{3,7},{4,0},{5,1},{6,2},{7,3},{8,12},{9,13},{10,... | collective-permute-start | bytes 4718600 | tf_op jit(solution)/shard_map/ppermute | solution.py:534
  362.8 43.4 %collective-permute-start.31 = (bf16[384,1024]{1,0:T(8,128)(2,1)}, bf16[384,1024]{1,0:T(8,128)(2,1)}, u32[]{:S(2)}, u32[]{:S(2)}) collective-permute-start(bf16[384,1024]{1,0:T(8,128)(2,1)} %get-tuple-element.116), channel_id=1, source_target_pairs={{0,8},{1,9},{2,10},{3,11},{4,12},{5,13},{6,14},{7,15},{8,0},{9,1},... | collective-permute-start | bytes 2359304 | tf_op jit(solution)/shard_map/ppermute | solution.py:534
  370.4 43.7 %collective-permute-start.28 = (bf16[768,1024]{1,0:T(8,128)(2,1)}, bf16[768,1024]{1,0:T(8,128)(2,1)}, u32[]{:S(2)}, u32[]{:S(2)}) collective-permute-start(bf16[768,1024]{1,0:T(8,128)(2,1)} %shard_map.226.refs_6_), channel_id=1, source_target_pairs={{0,4},{1,5},{2,6},{3,7},{4,0},{5,1},{6,2},{7,3},{8,12},{9,13},{10,... | collective-permute-start | bytes 4718600 | tf_op jit(solution)/shard_map/ppermute | solution.py:534
  388.9 52.2 %collective-permute-start.35 = (bf16[384,3072]{1,0:T(8,128)(2,1)}, bf16[384,3072]{1,0:T(8,128)(2,1)}, u32[]{:S(2)}, u32[]{:S(2)}) collective-permute-start(bf16[384,3072]{1,0:T(8,128)(2,1)} %get-tuple-element.124), channel_id=1, source_target_pairs={{0,2},{1,3},{2,0},{3,1},{4,6},{5,7},{6,4},{7,5},{8,10},{9,11},{10,... | collective-permute-start | bytes 7077896 | tf_op jit(solution)/shard_map/ppermute | solution.py:534
  408.7 27.7 %collective-permute-start.36 = (bf16[192,1024]{1,0:T(8,128)(2,1)}, bf16[192,1024]{1,0:T(8,128)(2,1)}, u32[]{:S(2)}, u32[]{:S(2)}) collective-permute-start(bf16[192,1024]{1,0:T(8,128)(2,1)} %get-tuple-element.125), channel_id=1, source_target_pairs={{0,16},{1,17},{2,18},{3,19},{4,20},{5,21},{6,22},{7,23},{8,24},{9,... | collective-permute-start | bytes 1179656 | tf_op jit(solution)/shard_map/ppermute | solution.py:534
  412.3 39.7 %collective-permute-start.33 = (bf16[192,1024]{1,0:T(8,128)(2,1)}, bf16[192,1024]{1,0:T(8,128)(2,1)}, u32[]{:S(2)}, u32[]{:S(2)}) collective-permute-start(bf16[192,1024]{1,0:T(8,128)(2,1)} %get-tuple-element.122), channel_id=1, source_target_pairs={{0,16},{1,17},{2,18},{3,19},{4,20},{5,21},{6,22},{7,23},{8,24},{9,... | collective-permute-start | bytes 1179656 | tf_op jit(solution)/shard_map/ppermute | solution.py:534
  421.5 35.3 %collective-permute-start.32 = (bf16[384,1024]{1,0:T(8,128)(2,1)}, bf16[384,1024]{1,0:T(8,128)(2,1)}, u32[]{:S(2)}, u32[]{:S(2)}) collective-permute-start(bf16[384,1024]{1,0:T(8,128)(2,1)} %get-tuple-element.121), channel_id=1, source_target_pairs={{0,8},{1,9},{2,10},{3,11},{4,12},{5,13},{6,14},{7,15},{8,0},{9,1},... | collective-permute-start | bytes 2359304 | tf_op jit(solution)/shard_map/ppermute | solution.py:534
  445.4 39.7 %collective-permute-start.39 = (bf16[192,3072]{1,0:T(8,128)(2,1)}, bf16[192,3072]{1,0:T(8,128)(2,1)}, u32[]{:S(2)}, u32[]{:S(2)}) collective-permute-start(bf16[192,3072]{1,0:T(8,128)(2,1)} %get-tuple-element.134), channel_id=1, source_target_pairs={{0,4},{1,5},{2,6},{3,7},{4,0},{5,1},{6,2},{7,3},{8,12},{9,13},{10,... | collective-permute-start | bytes 3538952 | tf_op jit(solution)/shard_map/ppermute | solution.py:534
  509.4 29.1 %collective-permute-start.47 = (bf16[48,1536]{1,0:T(8,128)(2,1)}, bf16[48,1536]{1,0:T(8,128)(2,1)}, u32[]{:S(2)}, u32[]{:S(2)}) collective-permute-start(bf16[48,1536]{1,0:T(8,128)(2,1)} %get-tuple-element.146), channel_id=1, source_target_pairs={{0,16},{1,17},{2,18},{3,19},{4,20},{5,21},{6,22},{7,23},{8,24},{9,... | collective-permute-start | bytes 442376 | tf_op jit(solution)/shard_map/ppermute | solution.py:534
  (63 other events, 757.9 us)

commit v4 on v3

--- a/solution.py
+++ b/solution.py
@@ -667,6 +667,7 @@
         right_pieces = [(piece, (half, 0)) for piece in y_pieces]
         mlp_y1 = swap(mlp_z, y_mask)
         mlp_near = swap(mlp_z, z_masks[1])
+        mlp_y2 = swap(mlp_far, y_mask)
 
         segment, position = jax.vmap(lambda own: pack_layout(own, per_pack))(lengths[:, 0])
         cosine, sine_part = rotary_tables(position, HEAD)
@@ -702,10 +703,8 @@
             *y_pieces,
         )
         g2 = restore(gains_rel[1:2].astype(bf16), pick_attn)
-        (mlp_last,) = join_call(
-            (mlp_far, mlp_near), [[(0, 0), (1, 0)]], [3 * ff], (attended, mlp_y1)
-        )
-        mlp_y2 = swap(mlp_last, y_mask)
+        (mlp_last,) = join_call((mlp_near,), [[(0, 0)]], [3 * ff], attended)
+        mlp_y3 = swap(mlp_last, y_mask)
         att_rel, middle, n2_rel = kernel_call(
             output_kernel,
             [shape_of(rows, qw, bf16), shape_of(rows, width, f32), shape_of(rows, width, bf16)],
@@ -732,7 +731,8 @@
             token=n2_rel,
         )
         dy_c = swap(dy_near, core_mask)
-        near_parts, far_parts = (own_mlp, mlp_z, mlp_last), (mlp_y, mlp_y1, mlp_y2)
+        near_parts = (own_mlp, mlp_z, mlp_far, mlp_last)
+        far_parts = (mlp_y, mlp_y1, mlp_y2, mlp_y3)
         for mask in z_masks[2:]:
             near_parts = near_parts + (swap(join(near_parts), mask),)
             far_parts = far_parts + (swap(near_parts[-1], y_mask),)
@@ -742,7 +742,7 @@
             return join_call(parts, plan, (2 * ff, ff), token)
 
         gu_near, down_near = assemble(near_parts, dy_near)
-        (n2_f,) = join_call((n2_x,), [[(0, 0)]], [width], (far_parts[-1], gu_near))
+        (n2_f,) = join_call((n2_x,), [[(0, 0)]], [width], (mlp_y2,) + far_parts[-1:] + (gu_near,))
         n2_xc = swap(n2_f, core_mask)
         gu_far, down_far = assemble(far_parts, n2_f)
         weights = (gu_near, gu_far, down_near, down_far)

time: 550 us -> 542 us (0.985)
  waiting for transfers between devices: 180 us -> 170 us
    ppermute x50 -> x51, waiting for transfers between devices: 180 us -> 170 us  [swap(): return lax.ppermute(array, AXES, [(i, i ^ mask) for i in range(world)])]
    ppermute x50 -> x51, starting transfers between devices: 39.1 us -> 41 us  [swap(): return lax.ppermute(array, AXES, [(i, i ^ mask) for i in range(world)])]
  transfers between devices with their start and end apart: 50 -> 51, of which waited for: 22 -> 24; matrix products, arithmetic and copies ran while one was open for 3% -> 3% of each run, Pallas kernels for 46% -> 48%
where the time goes in v4:
time: 542 us; the launch traced here: 532 us
  Pallas kernels  288 us (53%)
  waiting for transfers between devices  170 us (31%)
  starting transfers between devices  41 us (8%)
  local copies, waits for them, and re-layouts  20 us (4%)
  other arithmetic  9.09 us (2%)
    ppermute x51, waiting for transfers between devices, swap(): return lax.ppermute(array, AXES, [(i, i ^ mask) for i in range(world)])  170 us
    pallas_call x17, Pallas kernels, kernel_call(): pl.pallas_call(body, grid=(1,), out_shape=outs, in_specs=specs + [ANYWHER...  131 us
    pallas_call x2, Pallas kernels, mlp_call(): pl.pallas_call(functools.partial(mlp_kernel, ff), grid=(2,), in_specs=[fi...  41.9 us
    ppermute x51, starting transfers between devices, swap(): return lax.ppermute(array, AXES, [(i, i ^ mask) for i in range(world)])  41 us
    pallas_call x16, Pallas kernels, sum_call(): pl.pallas_call(functools.partial(sum_kernel, len(arrays)), grid=(columns...  39.1 us
    pallas_call x5, Pallas kernels, kept_call(): pl.pallas_call(kept_kernel, grid=(2,), in_specs=[pl.BlockSpec((count, blo...  36.3 us
    pallas_call x5, Pallas kernels, sent_call(): pl.pallas_call(sent_kernel, grid=(2,), in_specs=[pl.BlockSpec((count, blo...  28.6 us
    unnamed x75, local copies, waits for them, and re-layouts  13.8 us
  transfers between devices with their start and end apart: 51, of which 24 were waited for; matrix products, arithmetic and copies ran while one was open for 3% of the time, Pallas kernels for 48%

profile of v4, /device:TPU:0, one launch (start us, length us, event | category | flops | bytes accessed | tf_op | source)
XLA Modules:
  0.0 532.3 jit_solution(12966886513886983070)
XLA Ops:
  13.7 11.0 %collective-permute-done.2.refs_3_ = bf16[48,4736]{1,0:T(8,128)(2,1)S(1)} collective-permute-done((bf16[48,4736]{1,0:T(8,128)(2,1)}, bf16[48,4736]{1,0:T(8,128)(2,1)S(1)}, u32[]{:S(2)}, u32[]{:S(2)}) %collective-permute-start.2) | collective-permute-done | bytes 454688 | tf_op jit(solution)/shard_map/ppermute | solution.py:534
  24.8 9.1 %collective-permute-done.1.refs_2_ = bf16[48,4736]{1,0:T(8,128)(2,1)S(1)} collective-permute-done((bf16[48,4736]{1,0:T(8,128)(2,1)}, bf16[48,4736]{1,0:T(8,128)(2,1)S(1)}, u32[]{:S(2)}, u32[]{:S(2)}) %collective-permute-start.1) | collective-permute-done | bytes 454688 | tf_op jit(solution)/shard_map/ppermute | solution.py:534
  33.9 17.5 %collective-permute-done.refs_1_ = bf16[48,4736]{1,0:T(8,128)(2,1)S(1)} collective-permute-done((bf16[48,4736]{1,0:T(8,128)(2,1)}, bf16[48,4736]{1,0:T(8,128)(2,1)S(1)}, u32[]{:S(2)}, u32[]{:S(2)}) %collective-permute-start) | collective-permute-done | bytes 454688 | tf_op jit(solution)/shard_map/ppermute | solution.py:534
  56.3 18.0 %collective-permute-done.7.refs_4_.refs_1_ = bf16[192,1024]{1,0:T(8,128)(2,1)S(1)} collective-permute-done((bf16[192,1024]{1,0:T(8,128)(2,1)S(1)}, bf16[192,1024]{1,0:T(8,128)(2,1)S(1)}, u32[]{:S(2)}, u32[]{:S(2)}) %collective-permute-start.7) | collective-permute-done | bytes 393248 | tf_op jit(solution)/shard_map/ppermute | solution.py:534
  87.9 39.3 %collective-permute-done.8.refs_0_ = bf16[192,2048]{1,0:T(8,128)(2,1)} collective-permute-done((bf16[192,2048]{1,0:T(8,128)(2,1)}, bf16[192,2048]{1,0:T(8,128)(2,1)}, u32[]{:S(2)}, u32[]{:S(2)}) %collective-permute-start.8) | collective-permute-done | bytes 786464 | tf_op jit(solution)/shard_map/ppermute | solution.py:534
  157.0 17.6 %shard_map.209 = (bf16[384,3072]{1,0:T(8,128)(2,1)}, bf16[384,1536]{1,0:T(8,128)(2,1)}, bf16[384,1536]{1,0:T(8,128)(2,1)}, f32[8,1536]{1,0:T(8,128)}) custom-call(bf16[384,1536]{1,0:T(8,128)(2,1)} %shard_map.208.refs_0_.refs_1_, f32[384,384]{1,0:T(8,128)} %copy.46.refs_1_.refs_2_, f32[384,384]{1,0:T(8,128)} %copy.47.refs_2_.refs_3_, ...), custom_call_target="tpu_custom_call" | custom-call | flops 99999997952 | tf_op jit(solution)/shard_map/pallas_call | solution.py:509
  186.2 12.8 %shard_map.211 = (bf16[384,1536]{1,0:T(8,128)(2,1)}, f32[384,1536]{1,0:T(8,128)}, bf16[384,1536]{1,0:T(8,128)(2,1)}) custom-call(bf16[384,1536]{1,0:T(8,128)(2,1)} %get-tuple-element.91.refs_1_.refs_0_, bf16[1536,1536]{1,0:T(8,128)(2,1)} %get-tuple-element.92.refs_1_.refs_5_, bf16[384,1536]{1,0:T(8,128)(2,1)} %bitcast.30, f32[1,1536]{1,0:T(1,128)} %fusion.8.refs_3_.refs_6_, ...), custom_call_target="tpu_custom_call" | custom-call | flops 99999997952 | tf_op jit(solution)/shard_map/pallas_call | solution.py:509
  200.4 8.3 %shard_map.212.refs_4_.refs_2_.refs_0_.refs_1_ = bf16[768,1536]{1,0:T(8,128)(2,1)} custom-call(bf16[384,1536]{1,0:T(8,128)(2,1)} %bitcast.36, bf16[384,1536]{1,0:T(8,128)(2,1)} %collective-permute-done.3.refs_4_.refs_1_, bf16[1536,1536]{1,0:T(8,128)(2,1)} %get-tuple-element.94.refs_4_.refs_2_.refs_3_.pick_ref, ...), custom_call_target="tpu_custom_call" | custom-call | flops 99999997952 | tf_op jit(solution)/shard_map/pallas_call | solution.py:509
  213.4 6.6 %collective-permute-done.21.refs_2_.refs_3_ = bf16[192,3072]{1,0:T(8,128)(2,1)} collective-permute-done((bf16[192,3072]{1,0:T(8,128)(2,1)}, bf16[192,3072]{1,0:T(8,128)(2,1)}, u32[]{:S(2)}, u32[]{:S(2)}) %collective-permute-start.21) | collective-permute-done | bytes 1179680 | tf_op jit(solution)/shard_map/ppermute | solution.py:534
  234.1 21.2 %shard_map.216 = (bf16[1536,1024]{1,0:T(8,128)(2,1)}, bf16[1536,2048]{1,0:T(8,128)(2,1)}, bf16[384,1536]{1,0:T(8,128)(2,1)}, bf16[384,1536]{1,0:T(8,128)(2,1)}) custom-call(bf16[384,1536]{1,0:T(8,128)(2,1)} %collective-permute-done.22.refs_0_.refs_1_, bf16[384,1536]{1,0:T(8,128)(2,1)} %copy-done.21, ...), custom_call_target="tpu_custom_call" | custom-call | flops 99999997952 | tf_op jit(solution)/shard_map/pallas_call | solution.py:282
  265.5 20.7 %shard_map.218 = (bf16[1536,1024]{1,0:T(8,128)(2,1)}, bf16[1536,2048]{1,0:T(8,128)(2,1)}, bf16[384,1536]{1,0:T(8,128)(2,1)}, bf16[384,1536]{1,0:T(8,128)(2,1)}) custom-call(bf16[384,1536]{1,0:T(8,128)(2,1)} %get-tuple-element.95.refs_3_.refs_0_, bf16[384,1536]{1,0:T(8,128)(2,1)} %copy-done.22, ...), custom_call_target="tpu_custom_call", output_to_operand_aliasing={{0}: (8, {}), {1}: (9, {})} | custom-call | flops 99999997952 | tf_op jit(solution)/shard_map/pallas_call | solution.py:282
  295.3 8.8 %shard_map.220 = (f32[384,1536]{1,0:T(8,128)}, bf16[384,1536]{1,0:T(8,128)(2,1)}) custom-call(bf16[384,1536]{1,0:T(8,128)(2,1)} %get-tuple-element.106.refs_5_.refs_0_, bf16[384,1536]{1,0:T(8,128)(2,1)} %copy-done.26, bf16[384,1536]{1,0:T(8,128)(2,1)} %collective-permute-done.27.refs_2_, ...), custom_call_target="tpu_custom_call" | custom-call | flops 99999997952 | tf_op jit(solution)/shard_map/pallas_call | solution.py:509
  304.0 19.9 %shard_map.221.refs_1_.refs_2_.refs_0_ = bf16[384,3072]{1,0:T(8,128)(2,1)} custom-call(bf16[384,1536]{1,0:T(8,128)(2,1)} %get-tuple-element.110.refs_0_.refs_1_, bf16[384,3072]{1,0:T(8,128)(2,1)} %get-tuple-element.111.refs_1_, f32[384,384]{1,0:T(8,128)} %copy.46.refs_1_.refs_2_, f32[384,384]{1,0:T(8,128)} %copy.47.refs_2_.refs_3_, ...), custom_call_target="tpu_custom_call" | custom-call | flops 99999997952 | tf_op jit(solution)/shard_map/pallas_call | solution.py:509
  340.3 9.0 %shard_map.224 = (f32[384,3072]{1,0:T(8,128)}, bf16[384,3072]{1,0:T(8,128)(2,1)}) custom-call(bf16[384,1536]{1,0:T(8,128)(2,1)} %get-tuple-element.107.refs_0_, bf16[384,3072]{1,0:T(8,128)(2,1)} %shard_map.221.refs_1_.refs_2_.refs_0_, bf16[768,3072]{1,0:T(8,128)(2,1)} %copy-done.16, bf16[768,1024]{1,0:T(8,128)(2,1)} %shard_map.223.refs_3_), custom_call_target="tpu_custom_call" | custom-call | flops 99999997952 | tf_op jit(solution)/shard_map/pallas_call | solution.py:338
  349.3 7.2 %shard_map.225 = (f32[384,1024]{1,0:T(8,128)}, bf16[384,1024]{1,0:T(8,128)(2,1)}) custom-call(bf16[768,1536]{1,0:T(8,128)(2,1)} %shard_map.212.refs_4_.refs_2_.refs_0_.refs_1_, bf16[768,1536]{1,0:T(8,128)(2,1)} %shard_map.212.refs_4_.refs_2_.refs_0_.refs_1_, bf16[768,1536]{1,0:T(8,128)(2,1)} %collective-permute-done.18.refs_3_.refs_2_, ...), custom_call_target="tpu_custom_call" | custom-call | flops 99999997952 | tf_op jit(solution)/shard_map/pallas_call | solution.py:338
  363.7 10.2 %collective-permute-done.30.refs_5_ = bf16[768,1024]{1,0:T(8,128)(2,1)} collective-permute-done((bf16[768,1024]{1,0:T(8,128)(2,1)}, bf16[768,1024]{1,0:T(8,128)(2,1)}, u32[]{:S(2)}, u32[]{:S(2)}) %collective-permute-start.30) | collective-permute-done | bytes 1572896 | tf_op jit(solution)/shard_map/ppermute | solution.py:534
  373.8 7.2 %shard_map.227 = (f32[384,1024]{1,0:T(8,128)}, bf16[384,1024]{1,0:T(8,128)(2,1)}) custom-call(bf16[384,1536]{1,0:T(8,128)(2,1)} %get-tuple-element.95.refs_3_.refs_0_, bf16[384,1536]{1,0:T(8,128)(2,1)} %collective-permute-done.22.refs_0_.refs_1_, bf16[384,1536]{1,0:T(8,128)(2,1)} %copy-done.22, bf16[384,1536]{1,0:T(8,128)(2,1)} %copy-done.21, ...), custom_call_target="tpu_custom_call" | custom-call | flops 99999997952 | tf_op jit(solution)/shard_map/pallas_call | solution.py:338
  382.2 16.8 %shard_map.228.refs_2_ = f32[384,1536]{1,0:T(8,128)} custom-call(bf16[384,3072]{1,0:T(8,128)(2,1)} %shard_map.221.refs_1_.refs_2_.refs_0_, bf16[384,1536]{1,0:T(8,128)(2,1)} %shard_map.208.refs_0_.refs_1_, f32[8,1536]{1,0:T(8,128)} %get-tuple-element.93.refs_2_, bf16[1536,1536]{1,0:T(8,128)(2,1)} %get-tuple-element.87.refs_1_.refs_3_, ...), custom_call_target="tpu_custom_call" | custom-call | flops 99999997952 | tf_op jit(solution)/shard_map/pallas_call | solution.py:509
  407.0 7.4 %shard_map.231 = (f32[384,1024]{1,0:T(8,128)}, bf16[384,1024]{1,0:T(8,128)(2,1)}) custom-call(bf16[384,1536]{1,0:T(8,128)(2,1)} %get-tuple-element.95.refs_3_.refs_0_, bf16[384,1536]{1,0:T(8,128)(2,1)} %collective-permute-done.22.refs_0_.refs_1_, bf16[384,1536]{1,0:T(8,128)(2,1)} %copy-done.22, bf16[384,1536]{1,0:T(8,128)(2,1)} %copy-done.21, ...), custom_call_target="tpu_custom_call" | custom-call | flops 99999997952 | tf_op jit(solution)/shard_map/pallas_call | solution.py:338
  419.7 10.3 %collective-permute-done.37.refs_1_ = bf16[192,1024]{1,0:T(8,128)(2,1)} collective-permute-done((bf16[192,1024]{1,0:T(8,128)(2,1)}, bf16[192,1024]{1,0:T(8,128)(2,1)}, u32[]{:S(2)}, u32[]{:S(2)}) %collective-permute-start.37) | collective-permute-done | bytes 393248 | tf_op jit(solution)/shard_map/ppermute | solution.py:534
  452.1 10.6 %shard_map.238 = (bf16[384,1536]{1,0:T(8,128)(2,1)}, bf16[384,1536]{1,0:T(8,128)(2,1)}, bf16[384,1536]{1,0:T(8,128)(2,1)}, bf16[384,1536]{1,0:T(8,128)(2,1)}) custom-call(bf16[1536,1024]{1,0:T(8,128)(2,1)} %get-tuple-element.104.refs_4_.hidden_ref, bf16[768,1024]{1,0:T(8,128)(2,1)} %get-tuple-element.98.refs_6_.near_ref, ...), custom_call_target="tpu_custom_call" | custom-call | flops 99999997952 | tf_op jit(solution)/shard_map/pallas_call | solution.py:421
  462.9 7.0 %collective-permute-done.38.refs_1_ = bf16[384,1536]{1,0:T(8,128)(2,1)} collective-permute-done((bf16[384,1536]{1,0:T(8,128)(2,1)}, bf16[384,1536]{1,0:T(8,128)(2,1)}, u32[]{:S(2)}, u32[]{:S(2)}) %collective-permute-start.38) | collective-permute-done | bytes 1179680 | tf_op jit(solution)/shard_map/ppermute | solution.py:534
  505.4 9.5 %collective-permute-done.43.x_ref = bf16[384,1536]{1,0:T(8,128)(2,1)} collective-permute-done((bf16[384,1536]{1,0:T(8,128)(2,1)}, bf16[384,1536]{1,0:T(8,128)(2,1)}, u32[]{:S(2)}, u32[]{:S(2)}) %collective-permute-start.43) | collective-permute-done | bytes 1179680 | tf_op jit(solution)/shard_map/ppermute | solution.py:534
  515.9 7.1 %shard_map.246.refs_2_ = bf16[384,1536]{1,0:T(8,128)(2,1)} custom-call(bf16[384,1536]{1,0:T(8,128)(2,1)} %get-tuple-element.129.refs_2_.own_ref, bf16[384,1536]{1,0:T(8,128)(2,1)} %copy-done.24, bf16[384,1536]{1,0:T(8,128)(2,1)} %collective-permute-done.43.x_ref, bf16[1536,1536]{1,0:T(8,128)(2,1)} %get-tuple-element.94.refs_4_.refs_2_.refs_3_.pick_ref, ...), custom_call_target="tpu_custom_call" | custom-call | flops 99999997952 | tf_op jit(solution)/shard_map/pallas_call | solution.py:509
  (233 shorter events, 217.8 us)
Async XLA Ops:
  2.1 49.3 %collective-permute-start.4 = (bf16[192,3072]{1,0:T(8,128)(2,1)S(1)}, bf16[192,3072]{1,0:T(8,128)(2,1)S(1)}, u32[]{:S(2)}, u32[]{:S(2)}) collective-permute-start(bf16[192,3072]{1,0:T(8,128)(2,1)S(1)} %pad_maximum_fusion.refs_0_), channel_id=1, source_target_pairs={{0,4},{1,5},{2,6},{3,7},{4,0},{5,1},{6,2},{7,3},{8,12},{9,13},{10,... | collective-permute-start | bytes 3538952 | tf_op jit(solution)/shard_map/ppermute | solution.py:534
  5.1 46.3 %collective-permute-start.3 = (bf16[384,1536]{1,0:T(8,128)(2,1)S(1)}, bf16[384,1536]{1,0:T(8,128)(2,1)}, u32[]{:S(2)}, u32[]{:S(2)}) collective-permute-start(bf16[384,1536]{1,0:T(8,128)(2,1)S(1)} %bitcast.38), channel_id=1, source_target_pairs={{0,2},{1,3},{2,0},{3,1},{4,6},{5,7},{6,4},{7,5},{8,10},{9,11},{10,... | collective-permute-start | bytes 3538952 | tf_op jit(solution)/shard_map/ppermute | solution.py:534
  12.9 38.5 %collective-permute-start = (bf16[48,4736]{1,0:T(8,128)(2,1)}, bf16[48,4736]{1,0:T(8,128)(2,1)S(1)}, u32[]{:S(2)}, u32[]{:S(2)}) collective-permute-start(bf16[48,4736]{1,0:T(8,128)(2,1)} %shard_map.203.refs_0_), channel_id=1, source_target_pairs={{0,16},{1,17},{2,18},{3,19},{4,20},{5,21},{6,22},{7,23},{8,24},{9,... | collective-permute-start | bytes 1363976 | tf_op jit(solution)/shard_map/ppermute | solution.py:534
  82.2 47.1 %collective-permute-start.10 = (bf16[384,2432]{1,0:T(8,128)(2,1)}, bf16[384,2432]{1,0:T(8,128)(2,1)S(1)}, u32[]{:S(2)}, u32[]{:S(2)}) collective-permute-start(bf16[384,2432]{1,0:T(8,128)(2,1)} %get-tuple-element.89.refs_8_.refs_9_.refs_10_), channel_id=1, source_target_pairs={{0,2},{1,3},{2,0},{3,1},{4,6},{5,7},{6,4},{7,5},{8,10},{9,11},{10,... | collective-permute-start | bytes 5603336 | tf_op jit(solution)/shard_map/ppermute | solution.py:534
  82.8 46.6 %collective-permute-start.11 = (bf16[384,2304]{1,0:T(8,128)(2,1)}, bf16[384,2304]{1,0:T(8,128)(2,1)}, u32[]{:S(2)}, u32[]{:S(2)}) collective-permute-start(bf16[384,2304]{1,0:T(8,128)(2,1)} %get-tuple-element.82.refs_4_.refs_5_.refs_6_), channel_id=1, source_target_pairs={{0,1},{1,0},{2,3},{3,2},{4,5},{5,4},{6,7},{7,6},{8,9},{9,8},{10,11... | collective-permute-start | bytes 5308424 | tf_op jit(solution)/shard_map/ppermute | solution.py:534
  82.8 46.6 %collective-permute-start.9 = (bf16[384,2304]{1,0:T(8,128)(2,1)}, bf16[384,2304]{1,0:T(8,128)(2,1)}, u32[]{:S(2)}, u32[]{:S(2)}) collective-permute-start(bf16[384,2304]{1,0:T(8,128)(2,1)} %get-tuple-element.82.refs_4_.refs_5_.refs_6_), channel_id=1, source_target_pairs={{0,4},{1,5},{2,6},{3,7},{4,0},{5,1},{6,2},{7,3},{8,12},{9,13},{10,... | collective-permute-start | bytes 5308424 | tf_op jit(solution)/shard_map/ppermute | solution.py:534
  84.3 45.1 %collective-permute-start.12 = (bf16[192,3072]{1,0:T(8,128)(2,1)S(1)}, bf16[192,3072]{1,0:T(8,128)(2,1)}, u32[]{:S(2)}, u32[]{:S(2)}) collective-permute-start(bf16[192,3072]{1,0:T(8,128)(2,1)S(1)} %copy-done.7), channel_id=1, source_target_pairs={{0,8},{1,9},{2,10},{3,11},{4,12},{5,13},{6,14},{7,15},{8,0},{9,1},... | collective-permute-start | bytes 3538952 | tf_op jit(solution)/shard_map/ppermute | solution.py:534
  85.3 41.9 %collective-permute-start.8 = (bf16[192,2048]{1,0:T(8,128)(2,1)}, bf16[192,2048]{1,0:T(8,128)(2,1)}, u32[]{:S(2)}, u32[]{:S(2)}) collective-permute-start(bf16[192,2048]{1,0:T(8,128)(2,1)} %pad_maximum_fusion.1), channel_id=1, source_target_pairs={{0,16},{1,17},{2,18},{3,19},{4,20},{5,21},{6,22},{7,23},{8,24},{9,... | collective-permute-start | bytes 2359304 | tf_op jit(solution)/shard_map/ppermute | solution.py:534
  140.8 72.6 %collective-permute-start.20 = (bf16[192,3072]{1,0:T(8,128)(2,1)}, bf16[192,3072]{1,0:T(8,128)(2,1)}, u32[]{:S(2)}, u32[]{:S(2)}) collective-permute-start(bf16[192,3072]{1,0:T(8,128)(2,1)} %collective-permute-done.12.refs_5_.refs_2_), channel_id=1, source_target_pairs={{0,4},{1,5},{2,6},{3,7},{4,0},{5,1},{6,2},{7,3},{8,12},{9,13},{10,... | collective-permute-start | bytes 3538952 | tf_op jit(solution)/shard_map/ppermute | solution.py:534
  141.3 87.0 %collective-permute-start.19 = (bf16[192,3072]{1,0:T(8,128)(2,1)}, bf16[192,3072]{1,0:T(8,128)(2,1)}, u32[]{:S(2)}, u32[]{:S(2)}) collective-permute-start(bf16[192,3072]{1,0:T(8,128)(2,1)} %get-tuple-element.86.refs_3_.refs_1_), channel_id=1, source_target_pairs={{0,4},{1,5},{2,6},{3,7},{4,0},{5,1},{6,2},{7,3},{8,12},{9,13},{10,... | collective-permute-start | bytes 3538952 | tf_op jit(solution)/shard_map/ppermute | solution.py:534
  155.1 28.1 %collective-permute-start.16 = (bf16[192,3072]{1,0:T(8,128)(2,1)}, bf16[192,3072]{1,0:T(8,128)(2,1)}, u32[]{:S(2)}, u32[]{:S(2)}) collective-permute-start(bf16[192,3072]{1,0:T(8,128)(2,1)} %get-tuple-element.86.refs_3_.refs_1_), channel_id=1, source_target_pairs={{0,8},{1,9},{2,10},{3,11},{4,12},{5,13},{6,14},{7,15},{8,0},{9,1},... | collective-permute-start | bytes 3538952 | tf_op jit(solution)/shard_map/ppermute | solution.py:534
  185.6 34.3 %collective-permute-start.21 = (bf16[192,3072]{1,0:T(8,128)(2,1)}, bf16[192,3072]{1,0:T(8,128)(2,1)}, u32[]{:S(2)}, u32[]{:S(2)}) collective-permute-start(bf16[192,3072]{1,0:T(8,128)(2,1)} %shard_map.210.refs_13_.refs_3_), channel_id=1, source_target_pairs={{0,4},{1,5},{2,6},{3,7},{4,0},{5,1},{6,2},{7,3},{8,12},{9,13},{10,... | collective-permute-start | bytes 3538952 | tf_op jit(solution)/shard_map/ppermute | solution.py:534
  198.9 26.9 %collective-permute-start.22 = (bf16[384,1536]{1,0:T(8,128)(2,1)}, bf16[384,1536]{1,0:T(8,128)(2,1)}, u32[]{:S(2)}, u32[]{:S(2)}) collective-permute-start(bf16[384,1536]{1,0:T(8,128)(2,1)} %get-tuple-element.95.refs_3_.refs_0_), channel_id=1, source_target_pairs={{0,2},{1,3},{2,0},{3,1},{4,6},{5,7},{6,4},{7,5},{8,10},{9,11},{10,... | collective-permute-start | bytes 3538952 | tf_op jit(solution)/shard_map/ppermute | solution.py:534
  263.0 31.2 %collective-permute-start.27 = (bf16[384,1536]{1,0:T(8,128)(2,1)}, bf16[384,1536]{1,0:T(8,128)(2,1)}, u32[]{:S(2)}, u32[]{:S(2)}) collective-permute-start(bf16[384,1536]{1,0:T(8,128)(2,1)} %shard_map.217.refs_10_), channel_id=1, source_target_pairs={{0,2},{1,3},{2,0},{3,1},{4,6},{5,7},{6,4},{7,5},{8,10},{9,11},{10,... | collective-permute-start | bytes 3538952 | tf_op jit(solution)/shard_map/ppermute | solution.py:534
  292.7 56.6 %collective-permute-start.25 = (bf16[768,1024]{1,0:T(8,128)(2,1)}, bf16[768,1024]{1,0:T(8,128)(2,1)}, u32[]{:S(2)}, u32[]{:S(2)}) collective-permute-start(bf16[768,1024]{1,0:T(8,128)(2,1)} %shard_map.219.refs_7_), channel_id=1, source_target_pairs={{0,4},{1,5},{2,6},{3,7},{4,0},{5,1},{6,2},{7,3},{8,12},{9,13},{10,... | collective-permute-start | bytes 4718600 | tf_op jit(solution)/shard_map/ppermute | solution.py:534
  336.3 37.5 %collective-permute-start.30 = (bf16[768,1024]{1,0:T(8,128)(2,1)}, bf16[768,1024]{1,0:T(8,128)(2,1)}, u32[]{:S(2)}, u32[]{:S(2)}) collective-permute-start(bf16[768,1024]{1,0:T(8,128)(2,1)} %shard_map.223.refs_3_), channel_id=1, source_target_pairs={{0,4},{1,5},{2,6},{3,7},{4,0},{5,1},{6,2},{7,3},{8,12},{9,13},{10,... | collective-permute-start | bytes 4718600 | tf_op jit(solution)/shard_map/ppermute | solution.py:534
  356.5 42.5 %collective-permute-start.32 = (bf16[384,1024]{1,0:T(8,128)(2,1)}, bf16[384,1024]{1,0:T(8,128)(2,1)}, u32[]{:S(2)}, u32[]{:S(2)}) collective-permute-start(bf16[384,1024]{1,0:T(8,128)(2,1)} %get-tuple-element.116), channel_id=1, source_target_pairs={{0,8},{1,9},{2,10},{3,11},{4,12},{5,13},{6,14},{7,15},{8,0},{9,1},... | collective-permute-start | bytes 2359304 | tf_op jit(solution)/shard_map/ppermute | solution.py:534
  363.2 43.8 %collective-permute-start.29 = (bf16[768,1024]{1,0:T(8,128)(2,1)}, bf16[768,1024]{1,0:T(8,128)(2,1)}, u32[]{:S(2)}, u32[]{:S(2)}) collective-permute-start(bf16[768,1024]{1,0:T(8,128)(2,1)} %shard_map.226.refs_6_), channel_id=1, source_target_pairs={{0,4},{1,5},{2,6},{3,7},{4,0},{5,1},{6,2},{7,3},{8,12},{9,13},{10,... | collective-permute-start | bytes 4718600 | tf_op jit(solution)/shard_map/ppermute | solution.py:534
  381.6 52.2 %collective-permute-start.36 = (bf16[384,3072]{1,0:T(8,128)(2,1)}, bf16[384,3072]{1,0:T(8,128)(2,1)}, u32[]{:S(2)}, u32[]{:S(2)}) collective-permute-start(bf16[384,3072]{1,0:T(8,128)(2,1)} %get-tuple-element.124), channel_id=1, source_target_pairs={{0,2},{1,3},{2,0},{3,1},{4,6},{5,7},{6,4},{7,5},{8,10},{9,11},{10,... | collective-permute-start | bytes 7077896 | tf_op jit(solution)/shard_map/ppermute | solution.py:534
  401.4 28.7 %collective-permute-start.37 = (bf16[192,1024]{1,0:T(8,128)(2,1)}, bf16[192,1024]{1,0:T(8,128)(2,1)}, u32[]{:S(2)}, u32[]{:S(2)}) collective-permute-start(bf16[192,1024]{1,0:T(8,128)(2,1)} %get-tuple-element.125), channel_id=1, source_target_pairs={{0,16},{1,17},{2,18},{3,19},{4,20},{5,21},{6,22},{7,23},{8,24},{9,... | collective-permute-start | bytes 1179656 | tf_op jit(solution)/shard_map/ppermute | solution.py:534
  405.6 39.1 %collective-permute-start.34 = (bf16[192,1024]{1,0:T(8,128)(2,1)}, bf16[192,1024]{1,0:T(8,128)(2,1)}, u32[]{:S(2)}, u32[]{:S(2)}) collective-permute-start(bf16[192,1024]{1,0:T(8,128)(2,1)} %get-tuple-element.122), channel_id=1, source_target_pairs={{0,16},{1,17},{2,18},{3,19},{4,20},{5,21},{6,22},{7,23},{8,24},{9,... | collective-permute-start | bytes 1179656 | tf_op jit(solution)/shard_map/ppermute | solution.py:534
  414.4 35.2 %collective-permute-start.33 = (bf16[384,1024]{1,0:T(8,128)(2,1)}, bf16[384,1024]{1,0:T(8,128)(2,1)}, u32[]{:S(2)}, u32[]{:S(2)}) collective-permute-start(bf16[384,1024]{1,0:T(8,128)(2,1)} %get-tuple-element.121), channel_id=1, source_target_pairs={{0,8},{1,9},{2,10},{3,11},{4,12},{5,13},{6,14},{7,15},{8,0},{9,1},... | collective-permute-start | bytes 2359304 | tf_op jit(solution)/shard_map/ppermute | solution.py:534
  438.2 39.8 %collective-permute-start.40 = (bf16[192,3072]{1,0:T(8,128)(2,1)}, bf16[192,3072]{1,0:T(8,128)(2,1)}, u32[]{:S(2)}, u32[]{:S(2)}) collective-permute-start(bf16[192,3072]{1,0:T(8,128)(2,1)} %get-tuple-element.134), channel_id=1, source_target_pairs={{0,4},{1,5},{2,6},{3,7},{4,0},{5,1},{6,2},{7,3},{8,12},{9,13},{10,... | collective-permute-start | bytes 3538952 | tf_op jit(solution)/shard_map/ppermute | solution.py:534
  502.7 27.4 %collective-permute-start.48 = (bf16[48,1536]{1,0:T(8,128)(2,1)}, bf16[48,1536]{1,0:T(8,128)(2,1)}, u32[]{:S(2)}, u32[]{:S(2)}) collective-permute-start(bf16[48,1536]{1,0:T(8,128)(2,1)} %get-tuple-element.146), channel_id=1, source_target_pairs={{0,16},{1,17},{2,18},{3,19},{4,20},{5,21},{6,22},{7,23},{8,24},{9,... | collective-permute-start | bytes 442376 | tf_op jit(solution)/shard_map/ppermute | solution.py:534
  (64 other events, 786.0 us)

commit v5 on v4

--- a/solution.py
+++ b/solution.py
@@ -827,23 +827,25 @@
         up_got = swap(up_k[1], far_mask)
         og_b = sent_call(att_rel, dmb, 0, width, up_k[0])
         og_c = swap(og_b, core_mask)
-        down_grad = finish([down_k[0], down_got], og_b)
+        lay = down_call(hidden, *weights[2:], og_b)
+        lay_f = swap(lay[3], core_mask)
+        down_grad = finish([down_k[0], down_got], lay[0])
         qkv_k, qkv_got = onward(qkv_k, qkv_got, y_mask, down_grad)
         og = kept_call(att_rel, dmb, 0, width, og_c, qkv_k[0])
         og_got = swap(og[1], x_mask)
         gate_grad = finish([gate_k[0], gate_got], og[0])
         up_k, up_got = onward(up_k, up_got, near_mask, gate_grad)
-        lay = down_call(hidden, *weights[2:], up_k[0])
-        lay_f = swap(lay[3], core_mask)
-        og, og_got = onward(og, og_got, y_mask, lay[0])
+        qkv_k, qkv_got = onward(qkv_k, qkv_got, far_mask, up_k[0])
+        og, og_got = onward(og, og_got, y_mask, qkv_k[0])
         (lay_s,) = sum_call([lay[1], lay_f], [bf16], og[0])
         lay_x = swap(lay_s, x_mask)
-        qkv_k, qkv_got = onward(qkv_k, qkv_got, far_mask, lay_s)
-        og, og_got = onward(og, og_got, far_mask, qkv_k[0])
+        og, og_got = onward(og, og_got, far_mask, lay_s)
         lay_c = swap(after(lay[2], og[0]), core_mask)
         up_grad = finish([up_k[0], up_got], og[0])
         qkv_k, qkv_got = onward(qkv_k, qkv_got, near_mask, up_grad)
         og, og_got = onward(og, og_got, near_mask, qkv_k[0])
+        qkv_grad = finish([qkv_k[0], qkv_got], og[0])
+        output_grad = finish([og[0], og_got], qkv_grad)
         (layer_out,) = kernel_call(
             layer_kernel,
             [shape_of(rows, width, bf16)],
@@ -853,10 +855,8 @@
             lay_x,
             pick_mlp,
             middle,
-            token=og[0],
-        )
-        qkv_grad = finish([qkv_k[0], qkv_got], layer_out)
-        output_grad = finish([og[0], og_got], qkv_grad)
+            token=output_grad,
+        )
         q_grad, kv_grad = qkv_grad[:, :qw], qkv_grad[:, qw:]
         down_grad = down_grad.T
 

time: 542 us -> 566 us (1.044)
  waiting for transfers between devices: 170 us -> 195 us
    ppermute x51, waiting for transfers between devices: 170 us -> 195 us  [swap(): return lax.ppermute(array, AXES, [(i, i ^ mask) for i in range(world)])]
    unnamed x75 -> x81, local copies, waits for them, and re-layouts: 13.8 us -> 15 us
  transfers between devices with their start and end apart: 51 -> 51, of which waited for: 24 -> 22; matrix products, arithmetic and copies ran while one was open for 3% -> 3% of each run, Pallas kernels for 48% -> 44%
where the time goes in v5:
time: 566 us; the launch traced here: 557 us
  Pallas kernels  287 us (51%)
  waiting for transfers between devices  195 us (34%)
  starting transfers between devices  40.2 us (7%)
  local copies, waits for them, and re-layouts  21.2 us (4%)
  other arithmetic  9.13 us (2%)
    ppermute x51, waiting for transfers between devices, swap(): return lax.ppermute(array, AXES, [(i, i ^ mask) for i in range(world)])  195 us
    pallas_call x17, Pallas kernels, kernel_call(): pl.pallas_call(body, grid=(1,), out_shape=outs, in_specs=specs + [ANYWHER...  131 us
    pallas_call x2, Pallas kernels, mlp_call(): pl.pallas_call(functools.partial(mlp_kernel, ff), grid=(2,), in_specs=[fi...  41.8 us
    ppermute x51, starting transfers between devices, swap(): return lax.ppermute(array, AXES, [(i, i ^ mask) for i in range(world)])  40.2 us
    pallas_call x16, Pallas kernels, sum_call(): pl.pallas_call(functools.partial(sum_kernel, len(arrays)), grid=(columns...  39.3 us
    pallas_call x5, Pallas kernels, kept_call(): pl.pallas_call(kept_kernel, grid=(2,), in_specs=[pl.BlockSpec((count, blo...  36.2 us
    pallas_call x5, Pallas kernels, sent_call(): pl.pallas_call(sent_kernel, grid=(2,), in_specs=[pl.BlockSpec((count, blo...  28.6 us
    unnamed x81, local copies, waits for them, and re-layouts  15 us
  transfers between devices with their start and end apart: 51, of which 22 were waited for; matrix products, arithmetic and copies ran while one was open for 3% of the time, Pallas kernels for 44%

profile of v5, /device:TPU:0, one launch (start us, length us, event | category | flops | bytes accessed | tf_op | source)
XLA Modules:
  0.0 556.9 jit_solution(12261242706804636573)
XLA Ops:
  13.7 11.0 %collective-permute-done.2.refs_3_ = bf16[48,4736]{1,0:T(8,128)(2,1)S(1)} collective-permute-done((bf16[48,4736]{1,0:T(8,128)(2,1)}, bf16[48,4736]{1,0:T(8,128)(2,1)S(1)}, u32[]{:S(2)}, u32[]{:S(2)}) %collective-permute-start.2) | collective-permute-done | bytes 454688 | tf_op jit(solution)/shard_map/ppermute | solution.py:534
  24.7 9.1 %collective-permute-done.1.refs_2_ = bf16[48,4736]{1,0:T(8,128)(2,1)S(1)} collective-permute-done((bf16[48,4736]{1,0:T(8,128)(2,1)}, bf16[48,4736]{1,0:T(8,128)(2,1)S(1)}, u32[]{:S(2)}, u32[]{:S(2)}) %collective-permute-start.1) | collective-permute-done | bytes 454688 | tf_op jit(solution)/shard_map/ppermute | solution.py:534
  33.9 17.5 %collective-permute-done.refs_1_ = bf16[48,4736]{1,0:T(8,128)(2,1)S(1)} collective-permute-done((bf16[48,4736]{1,0:T(8,128)(2,1)}, bf16[48,4736]{1,0:T(8,128)(2,1)S(1)}, u32[]{:S(2)}, u32[]{:S(2)}) %collective-permute-start) | collective-permute-done | bytes 454688 | tf_op jit(solution)/shard_map/ppermute | solution.py:534
  56.3 18.0 %collective-permute-done.7.refs_4_.refs_1_ = bf16[192,1024]{1,0:T(8,128)(2,1)S(1)} collective-permute-done((bf16[192,1024]{1,0:T(8,128)(2,1)S(1)}, bf16[192,1024]{1,0:T(8,128)(2,1)S(1)}, u32[]{:S(2)}, u32[]{:S(2)}) %collective-permute-start.7) | collective-permute-done | bytes 393248 | tf_op jit(solution)/shard_map/ppermute | solution.py:534
  87.8 39.3 %collective-permute-done.8.refs_0_ = bf16[192,2048]{1,0:T(8,128)(2,1)} collective-permute-done((bf16[192,2048]{1,0:T(8,128)(2,1)}, bf16[192,2048]{1,0:T(8,128)(2,1)}, u32[]{:S(2)}, u32[]{:S(2)}) %collective-permute-start.8) | collective-permute-done | bytes 786464 | tf_op jit(solution)/shard_map/ppermute | solution.py:534
  156.9 17.6 %shard_map.209 = (bf16[384,3072]{1,0:T(8,128)(2,1)}, bf16[384,1536]{1,0:T(8,128)(2,1)}, bf16[384,1536]{1,0:T(8,128)(2,1)}, f32[8,1536]{1,0:T(8,128)}) custom-call(bf16[384,1536]{1,0:T(8,128)(2,1)} %shard_map.208.refs_0_.refs_1_, f32[384,384]{1,0:T(8,128)} %copy.46.refs_1_.refs_2_, f32[384,384]{1,0:T(8,128)} %copy.47.refs_2_.refs_3_, ...), custom_call_target="tpu_custom_call" | custom-call | flops 99999997952 | tf_op jit(solution)/shard_map/pallas_call | solution.py:509
  186.1 12.6 %shard_map.211 = (bf16[384,1536]{1,0:T(8,128)(2,1)}, f32[384,1536]{1,0:T(8,128)}, bf16[384,1536]{1,0:T(8,128)(2,1)}) custom-call(bf16[384,1536]{1,0:T(8,128)(2,1)} %get-tuple-element.91.refs_1_.refs_0_, bf16[1536,1536]{1,0:T(8,128)(2,1)} %get-tuple-element.92.refs_1_.refs_5_, bf16[384,1536]{1,0:T(8,128)(2,1)} %bitcast.30, f32[1,1536]{1,0:T(1,128)} %fusion.8.refs_3_.refs_6_, ...), custom_call_target="tpu_custom_call" | custom-call | flops 99999997952 | tf_op jit(solution)/shard_map/pallas_call | solution.py:509
  200.2 8.3 %shard_map.212.refs_4_.refs_2_.refs_0_.refs_1_ = bf16[768,1536]{1,0:T(8,128)(2,1)} custom-call(bf16[384,1536]{1,0:T(8,128)(2,1)} %bitcast.36, bf16[384,1536]{1,0:T(8,128)(2,1)} %collective-permute-done.3.refs_4_.refs_1_, bf16[1536,1536]{1,0:T(8,128)(2,1)} %get-tuple-element.94.refs_4_.refs_2_.refs_3_.pick_ref, ...), custom_call_target="tpu_custom_call" | custom-call | flops 99999997952 | tf_op jit(solution)/shard_map/pallas_call | solution.py:509
  233.9 21.2 %shard_map.216 = (bf16[1536,1024]{1,0:T(8,128)(2,1)}, bf16[1536,2048]{1,0:T(8,128)(2,1)}, bf16[384,1536]{1,0:T(8,128)(2,1)}, bf16[384,1536]{1,0:T(8,128)(2,1)}) custom-call(bf16[384,1536]{1,0:T(8,128)(2,1)} %collective-permute-done.22.refs_0_.refs_1_, bf16[384,1536]{1,0:T(8,128)(2,1)} %copy-done.21, ...), custom_call_target="tpu_custom_call" | custom-call | flops 99999997952 | tf_op jit(solution)/shard_map/pallas_call | solution.py:282
  265.3 20.7 %shard_map.218 = (bf16[1536,1024]{1,0:T(8,128)(2,1)}, bf16[1536,2048]{1,0:T(8,128)(2,1)}, bf16[384,1536]{1,0:T(8,128)(2,1)}, bf16[384,1536]{1,0:T(8,128)(2,1)}) custom-call(bf16[384,1536]{1,0:T(8,128)(2,1)} %get-tuple-element.95.refs_3_.refs_0_, bf16[384,1536]{1,0:T(8,128)(2,1)} %copy-done.22, ...), custom_call_target="tpu_custom_call", output_to_operand_aliasing={{0}: (8, {}), {1}: (9, {})} | custom-call | flops 99999997952 | tf_op jit(solution)/shard_map/pallas_call | solution.py:282
  295.0 8.8 %shard_map.220 = (f32[384,1536]{1,0:T(8,128)}, bf16[384,1536]{1,0:T(8,128)(2,1)}) custom-call(bf16[384,1536]{1,0:T(8,128)(2,1)} %get-tuple-element.106.refs_5_.refs_0_, bf16[384,1536]{1,0:T(8,128)(2,1)} %copy-done.25, bf16[384,1536]{1,0:T(8,128)(2,1)} %collective-permute-done.26.refs_2_, ...), custom_call_target="tpu_custom_call" | custom-call | flops 99999997952 | tf_op jit(solution)/shard_map/pallas_call | solution.py:509
  303.7 19.7 %shard_map.221.refs_1_.refs_2_.refs_0_ = bf16[384,3072]{1,0:T(8,128)(2,1)} custom-call(bf16[384,1536]{1,0:T(8,128)(2,1)} %get-tuple-element.109.refs_0_.refs_1_, bf16[384,3072]{1,0:T(8,128)(2,1)} %get-tuple-element.112.refs_1_, f32[384,384]{1,0:T(8,128)} %copy.46.refs_1_.refs_2_, f32[384,384]{1,0:T(8,128)} %copy.47.refs_2_.refs_3_, ...), custom_call_target="tpu_custom_call" | custom-call | flops 99999997952 | tf_op jit(solution)/shard_map/pallas_call | solution.py:509
  339.8 8.9 %shard_map.224 = (f32[384,3072]{1,0:T(8,128)}, bf16[384,3072]{1,0:T(8,128)(2,1)}) custom-call(bf16[384,1536]{1,0:T(8,128)(2,1)} %get-tuple-element.111.refs_0_, bf16[384,3072]{1,0:T(8,128)(2,1)} %shard_map.221.refs_1_.refs_2_.refs_0_, bf16[768,3072]{1,0:T(8,128)(2,1)} %copy-done.16, bf16[768,1024]{1,0:T(8,128)(2,1)} %shard_map.223.refs_3_), custom_call_target="tpu_custom_call" | custom-call | flops 99999997952 | tf_op jit(solution)/shard_map/pallas_call | solution.py:338
  348.7 7.1 %shard_map.225 = (f32[384,1024]{1,0:T(8,128)}, bf16[384,1024]{1,0:T(8,128)(2,1)}) custom-call(bf16[768,1536]{1,0:T(8,128)(2,1)} %shard_map.212.refs_4_.refs_2_.refs_0_.refs_1_, bf16[768,1536]{1,0:T(8,128)(2,1)} %shard_map.212.refs_4_.refs_2_.refs_0_.refs_1_, bf16[768,1536]{1,0:T(8,128)(2,1)} %collective-permute-done.18.refs_3_.refs_2_, ...), custom_call_target="tpu_custom_call" | custom-call | flops 99999997952 | tf_op jit(solution)/shard_map/pallas_call | solution.py:338
  363.0 10.3 %collective-permute-done.30.refs_5_ = bf16[768,1024]{1,0:T(8,128)(2,1)} collective-permute-done((bf16[768,1024]{1,0:T(8,128)(2,1)}, bf16[768,1024]{1,0:T(8,128)(2,1)}, u32[]{:S(2)}, u32[]{:S(2)}) %collective-permute-start.30) | collective-permute-done | bytes 1572896 | tf_op jit(solution)/shard_map/ppermute | solution.py:534
  373.3 7.2 %shard_map.227 = (f32[384,1024]{1,0:T(8,128)}, bf16[384,1024]{1,0:T(8,128)(2,1)}) custom-call(bf16[384,1536]{1,0:T(8,128)(2,1)} %get-tuple-element.95.refs_3_.refs_0_, bf16[384,1536]{1,0:T(8,128)(2,1)} %collective-permute-done.22.refs_0_.refs_1_, bf16[384,1536]{1,0:T(8,128)(2,1)} %copy-done.22, bf16[384,1536]{1,0:T(8,128)(2,1)} %copy-done.21, ...), custom_call_target="tpu_custom_call" | custom-call | flops 99999997952 | tf_op jit(solution)/shard_map/pallas_call | solution.py:338
  381.6 16.8 %shard_map.228.refs_2_ = f32[384,1536]{1,0:T(8,128)} custom-call(bf16[384,3072]{1,0:T(8,128)(2,1)} %shard_map.221.refs_1_.refs_2_.refs_0_, bf16[384,1536]{1,0:T(8,128)(2,1)} %shard_map.208.refs_0_.refs_1_, f32[8,1536]{1,0:T(8,128)} %get-tuple-element.93.refs_2_, bf16[1536,1536]{1,0:T(8,128)(2,1)} %get-tuple-element.87.refs_1_.refs_3_, ...), custom_call_target="tpu_custom_call" | custom-call | flops 99999997952 | tf_op jit(solution)/shard_map/pallas_call | solution.py:509
  406.4 7.4 %shard_map.231 = (f32[384,1024]{1,0:T(8,128)}, bf16[384,1024]{1,0:T(8,128)(2,1)}) custom-call(bf16[384,1536]{1,0:T(8,128)(2,1)} %get-tuple-element.95.refs_3_.refs_0_, bf16[384,1536]{1,0:T(8,128)(2,1)} %collective-permute-done.22.refs_0_.refs_1_, bf16[384,1536]{1,0:T(8,128)(2,1)} %copy-done.22, bf16[384,1536]{1,0:T(8,128)(2,1)} %copy-done.21, ...), custom_call_target="tpu_custom_call" | custom-call | flops 99999997952 | tf_op jit(solution)/shard_map/pallas_call | solution.py:338
  417.8 10.6 %shard_map.233 = (bf16[384,1536]{1,0:T(8,128)(2,1)}, bf16[384,1536]{1,0:T(8,128)(2,1)}, bf16[384,1536]{1,0:T(8,128)(2,1)}, bf16[384,1536]{1,0:T(8,128)(2,1)}) custom-call(bf16[1536,1024]{1,0:T(8,128)(2,1)} %get-tuple-element.104.refs_4_.hidden_ref, bf16[768,1024]{1,0:T(8,128)(2,1)} %get-tuple-element.98.refs_6_.near_ref, ...), custom_call_target="tpu_custom_call" | custom-call | flops 99999997952 | tf_op jit(solution)/shard_map/pallas_call | solution.py:421
  445.7 7.9 %collective-permute-done.38.refs_1_ = bf16[384,1024]{1,0:T(8,128)(2,1)} collective-permute-done((bf16[384,1024]{1,0:T(8,128)(2,1)}, bf16[384,1024]{1,0:T(8,128)(2,1)}, u32[]{:S(2)}, u32[]{:S(2)}) %collective-permute-start.38) | collective-permute-done | bytes 786464 | tf_op jit(solution)/shard_map/ppermute | solution.py:534
  468.6 15.5 %collective-permute-done.36.refs_1_ = bf16[384,1536]{1,0:T(8,128)(2,1)S(1)} collective-permute-done((bf16[384,1536]{1,0:T(8,128)(2,1)S(1)}, bf16[384,1536]{1,0:T(8,128)(2,1)S(1)}, u32[]{:S(2)}, u32[]{:S(2)}) %collective-permute-start.36) | collective-permute-done | bytes 1179680 | tf_op jit(solution)/shard_map/ppermute | solution.py:534
  491.3 11.5 %collective-permute-done.40.refs_1_ = bf16[192,1536]{1,0:T(8,128)(2,1)S(1)} collective-permute-done((bf16[192,1536]{1,0:T(8,128)(2,1)}, bf16[192,1536]{1,0:T(8,128)(2,1)S(1)}, u32[]{:S(2)}, u32[]{:S(2)}) %collective-permute-start.40) | collective-permute-done | bytes 589856 | tf_op jit(solution)/shard_map/ppermute | solution.py:534
  521.1 11.6 %collective-permute-done.48.refs_1_ = bf16[48,3072]{1,0:T(8,128)(2,1)S(1)} collective-permute-done((bf16[48,3072]{1,0:T(8,128)(2,1)}, bf16[48,3072]{1,0:T(8,128)(2,1)S(1)}, u32[]{:S(2)}, u32[]{:S(2)}) %collective-permute-start.48) | collective-permute-done | bytes 294944 | tf_op jit(solution)/shard_map/ppermute | solution.py:534
  549.4 7.1 %shard_map.248 = bf16[384,1536]{1,0:T(8,128)(2,1)} custom-call(bf16[384,1536]{1,0:T(8,128)(2,1)} %get-tuple-element.122.refs_2_.own_ref, bf16[384,1536]{1,0:T(8,128)(2,1)} %collective-permute-done.42.core_ref, bf16[384,1536]{1,0:T(8,128)(2,1)} %collective-permute-done.43.x_ref, bf16[1536,1536]{1,0:T(8,128)(2,1)} %get-tuple-element.94.refs_4_.refs_2_.refs_3_.pick_ref, ...), custom_call_target="tpu_custom_call" | custom-call | flops 99999997952 | tf_op jit(solution)/shard_map/pallas_call | solution.py:509
  (239 shorter events, 229.9 us)
Async XLA Ops:
  2.1 49.3 %collective-permute-start.4 = (bf16[192,3072]{1,0:T(8,128)(2,1)S(1)}, bf16[192,3072]{1,0:T(8,128)(2,1)S(1)}, u32[]{:S(2)}, u32[]{:S(2)}) collective-permute-start(bf16[192,3072]{1,0:T(8,128)(2,1)S(1)} %pad_maximum_fusion.refs_0_), channel_id=1, source_target_pairs={{0,4},{1,5},{2,6},{3,7},{4,0},{5,1},{6,2},{7,3},{8,12},{9,13},{10,... | collective-permute-start | bytes 3538952 | tf_op jit(solution)/shard_map/ppermute | solution.py:534
  5.1 46.3 %collective-permute-start.3 = (bf16[384,1536]{1,0:T(8,128)(2,1)S(1)}, bf16[384,1536]{1,0:T(8,128)(2,1)}, u32[]{:S(2)}, u32[]{:S(2)}) collective-permute-start(bf16[384,1536]{1,0:T(8,128)(2,1)S(1)} %bitcast.38), channel_id=1, source_target_pairs={{0,2},{1,3},{2,0},{3,1},{4,6},{5,7},{6,4},{7,5},{8,10},{9,11},{10,... | collective-permute-start | bytes 3538952 | tf_op jit(solution)/shard_map/ppermute | solution.py:534
  12.9 38.5 %collective-permute-start = (bf16[48,4736]{1,0:T(8,128)(2,1)}, bf16[48,4736]{1,0:T(8,128)(2,1)S(1)}, u32[]{:S(2)}, u32[]{:S(2)}) collective-permute-start(bf16[48,4736]{1,0:T(8,128)(2,1)} %shard_map.203.refs_0_), channel_id=1, source_target_pairs={{0,16},{1,17},{2,18},{3,19},{4,20},{5,21},{6,22},{7,23},{8,24},{9,... | collective-permute-start | bytes 1363976 | tf_op jit(solution)/shard_map/ppermute | solution.py:534
  82.2 47.1 %collective-permute-start.10 = (bf16[384,2432]{1,0:T(8,128)(2,1)}, bf16[384,2432]{1,0:T(8,128)(2,1)S(1)}, u32[]{:S(2)}, u32[]{:S(2)}) collective-permute-start(bf16[384,2432]{1,0:T(8,128)(2,1)} %get-tuple-element.89.refs_8_.refs_9_.refs_10_), channel_id=1, source_target_pairs={{0,2},{1,3},{2,0},{3,1},{4,6},{5,7},{6,4},{7,5},{8,10},{9,11},{10,... | collective-permute-start | bytes 5603336 | tf_op jit(solution)/shard_map/ppermute | solution.py:534
  82.7 46.6 %collective-permute-start.11 = (bf16[384,2304]{1,0:T(8,128)(2,1)}, bf16[384,2304]{1,0:T(8,128)(2,1)}, u32[]{:S(2)}, u32[]{:S(2)}) collective-permute-start(bf16[384,2304]{1,0:T(8,128)(2,1)} %get-tuple-element.82.refs_4_.refs_5_.refs_6_), channel_id=1, source_target_pairs={{0,1},{1,0},{2,3},{3,2},{4,5},{5,4},{6,7},{7,6},{8,9},{9,8},{10,11... | collective-permute-start | bytes 5308424 | tf_op jit(solution)/shard_map/ppermute | solution.py:534
  82.7 46.6 %collective-permute-start.9 = (bf16[384,2304]{1,0:T(8,128)(2,1)}, bf16[384,2304]{1,0:T(8,128)(2,1)}, u32[]{:S(2)}, u32[]{:S(2)}) collective-permute-start(bf16[384,2304]{1,0:T(8,128)(2,1)} %get-tuple-element.82.refs_4_.refs_5_.refs_6_), channel_id=1, source_target_pairs={{0,4},{1,5},{2,6},{3,7},{4,0},{5,1},{6,2},{7,3},{8,12},{9,13},{10,... | collective-permute-start | bytes 5308424 | tf_op jit(solution)/shard_map/ppermute | solution.py:534
  84.2 45.1 %collective-permute-start.12 = (bf16[192,3072]{1,0:T(8,128)(2,1)S(1)}, bf16[192,3072]{1,0:T(8,128)(2,1)}, u32[]{:S(2)}, u32[]{:S(2)}) collective-permute-start(bf16[192,3072]{1,0:T(8,128)(2,1)S(1)} %copy-done.7), channel_id=1, source_target_pairs={{0,8},{1,9},{2,10},{3,11},{4,12},{5,13},{6,14},{7,15},{8,0},{9,1},... | collective-permute-start | bytes 3538952 | tf_op jit(solution)/shard_map/ppermute | solution.py:534
  85.2 41.9 %collective-permute-start.8 = (bf16[192,2048]{1,0:T(8,128)(2,1)}, bf16[192,2048]{1,0:T(8,128)(2,1)}, u32[]{:S(2)}, u32[]{:S(2)}) collective-permute-start(bf16[192,2048]{1,0:T(8,128)(2,1)} %pad_maximum_fusion.1), channel_id=1, source_target_pairs={{0,16},{1,17},{2,18},{3,19},{4,20},{5,21},{6,22},{7,23},{8,24},{9,... | collective-permute-start | bytes 2359304 | tf_op jit(solution)/shard_map/ppermute | solution.py:534
  140.7 72.5 %collective-permute-start.20 = (bf16[192,3072]{1,0:T(8,128)(2,1)}, bf16[192,3072]{1,0:T(8,128)(2,1)}, u32[]{:S(2)}, u32[]{:S(2)}) collective-permute-start(bf16[192,3072]{1,0:T(8,128)(2,1)} %collective-permute-done.12.refs_5_.refs_2_), channel_id=1, source_target_pairs={{0,4},{1,5},{2,6},{3,7},{4,0},{5,1},{6,2},{7,3},{8,12},{9,13},{10,... | collective-permute-start | bytes 3538952 | tf_op jit(solution)/shard_map/ppermute | solution.py:534
  141.2 86.8 %collective-permute-start.19 = (bf16[192,3072]{1,0:T(8,128)(2,1)}, bf16[192,3072]{1,0:T(8,128)(2,1)}, u32[]{:S(2)}, u32[]{:S(2)}) collective-permute-start(bf16[192,3072]{1,0:T(8,128)(2,1)} %get-tuple-element.86.refs_3_.refs_1_), channel_id=1, source_target_pairs={{0,4},{1,5},{2,6},{3,7},{4,0},{5,1},{6,2},{7,3},{8,12},{9,13},{10,... | collective-permute-start | bytes 3538952 | tf_op jit(solution)/shard_map/ppermute | solution.py:534
  185.6 34.3 %collective-permute-start.21 = (bf16[192,3072]{1,0:T(8,128)(2,1)}, bf16[192,3072]{1,0:T(8,128)(2,1)}, u32[]{:S(2)}, u32[]{:S(2)}) collective-permute-start(bf16[192,3072]{1,0:T(8,128)(2,1)} %shard_map.210.refs_13_.refs_3_), channel_id=1, source_target_pairs={{0,4},{1,5},{2,6},{3,7},{4,0},{5,1},{6,2},{7,3},{8,12},{9,13},{10,... | collective-permute-start | bytes 3538952 | tf_op jit(solution)/shard_map/ppermute | solution.py:534
  262.8 31.2 %collective-permute-start.26 = (bf16[384,1536]{1,0:T(8,128)(2,1)}, bf16[384,1536]{1,0:T(8,128)(2,1)}, u32[]{:S(2)}, u32[]{:S(2)}) collective-permute-start(bf16[384,1536]{1,0:T(8,128)(2,1)} %shard_map.217.refs_10_), channel_id=1, source_target_pairs={{0,2},{1,3},{2,0},{3,1},{4,6},{5,7},{6,4},{7,5},{8,10},{9,11},{10,... | collective-permute-start | bytes 3538952 | tf_op jit(solution)/shard_map/ppermute | solution.py:534
  292.4 56.3 %collective-permute-start.27 = (bf16[768,1024]{1,0:T(8,128)(2,1)}, bf16[768,1024]{1,0:T(8,128)(2,1)}, u32[]{:S(2)}, u32[]{:S(2)}) collective-permute-start(bf16[768,1024]{1,0:T(8,128)(2,1)} %shard_map.219.refs_7_), channel_id=1, source_target_pairs={{0,4},{1,5},{2,6},{3,7},{4,0},{5,1},{6,2},{7,3},{8,12},{9,13},{10,... | collective-permute-start | bytes 4718600 | tf_op jit(solution)/shard_map/ppermute | solution.py:534
  335.7 37.5 %collective-permute-start.30 = (bf16[768,1024]{1,0:T(8,128)(2,1)}, bf16[768,1024]{1,0:T(8,128)(2,1)}, u32[]{:S(2)}, u32[]{:S(2)}) collective-permute-start(bf16[768,1024]{1,0:T(8,128)(2,1)} %shard_map.223.refs_3_), channel_id=1, source_target_pairs={{0,4},{1,5},{2,6},{3,7},{4,0},{5,1},{6,2},{7,3},{8,12},{9,13},{10,... | collective-permute-start | bytes 4718600 | tf_op jit(solution)/shard_map/ppermute | solution.py:534
  355.8 42.6 %collective-permute-start.32 = (bf16[384,1024]{1,0:T(8,128)(2,1)}, bf16[384,1024]{1,0:T(8,128)(2,1)}, u32[]{:S(2)}, u32[]{:S(2)}) collective-permute-start(bf16[384,1024]{1,0:T(8,128)(2,1)} %get-tuple-element.117), channel_id=1, source_target_pairs={{0,8},{1,9},{2,10},{3,11},{4,12},{5,13},{6,14},{7,15},{8,0},{9,1},... | collective-permute-start | bytes 2359304 | tf_op jit(solution)/shard_map/ppermute | solution.py:534
  362.5 43.9 %collective-permute-start.29 = (bf16[768,1024]{1,0:T(8,128)(2,1)}, bf16[768,1024]{1,0:T(8,128)(2,1)}, u32[]{:S(2)}, u32[]{:S(2)}) collective-permute-start(bf16[768,1024]{1,0:T(8,128)(2,1)} %shard_map.226.refs_6_), channel_id=1, source_target_pairs={{0,4},{1,5},{2,6},{3,7},{4,0},{5,1},{6,2},{7,3},{8,12},{9,13},{10,... | collective-permute-start | bytes 4718600 | tf_op jit(solution)/shard_map/ppermute | solution.py:534
  381.1 52.2 %collective-permute-start.34 = (bf16[384,3072]{1,0:T(8,128)(2,1)}, bf16[384,3072]{1,0:T(8,128)(2,1)}, u32[]{:S(2)}, u32[]{:S(2)}) collective-permute-start(bf16[384,3072]{1,0:T(8,128)(2,1)} %get-tuple-element.124), channel_id=1, source_target_pairs={{0,2},{1,3},{2,0},{3,1},{4,6},{5,7},{6,4},{7,5},{8,10},{9,11},{10,... | collective-permute-start | bytes 7077896 | tf_op jit(solution)/shard_map/ppermute | solution.py:534
  400.8 28.9 %collective-permute-start.35 = (bf16[192,1024]{1,0:T(8,128)(2,1)}, bf16[192,1024]{1,0:T(8,128)(2,1)}, u32[]{:S(2)}, u32[]{:S(2)}) collective-permute-start(bf16[192,1024]{1,0:T(8,128)(2,1)} %get-tuple-element.125), channel_id=1, source_target_pairs={{0,16},{1,17},{2,18},{3,19},{4,20},{5,21},{6,22},{7,23},{8,24},{9,... | collective-permute-start | bytes 1179656 | tf_op jit(solution)/shard_map/ppermute | solution.py:534
  405.0 38.6 %collective-permute-start.39 = (bf16[192,1024]{1,0:T(8,128)(2,1)}, bf16[192,1024]{1,0:T(8,128)(2,1)}, u32[]{:S(2)}, u32[]{:S(2)}) collective-permute-start(bf16[192,1024]{1,0:T(8,128)(2,1)} %get-tuple-element.131), channel_id=1, source_target_pairs={{0,16},{1,17},{2,18},{3,19},{4,20},{5,21},{6,22},{7,23},{8,24},{9,... | collective-permute-start | bytes 1179656 | tf_op jit(solution)/shard_map/ppermute | solution.py:534
  429.7 59.0 %collective-permute-start.41 = (bf16[384,1536]{1,0:T(8,128)(2,1)}, bf16[384,1536]{1,0:T(8,128)(2,1)}, u32[]{:S(2)}, u32[]{:S(2)}) collective-permute-start(bf16[384,1536]{1,0:T(8,128)(2,1)} %get-tuple-element.137), channel_id=1, source_target_pairs={{0,1},{1,0},{2,3},{3,2},{4,5},{5,4},{6,7},{7,6},{8,9},{9,8},{10,11... | collective-permute-start | bytes 3538952 | tf_op jit(solution)/shard_map/ppermute | solution.py:534
  456.1 49.7 %collective-permute-start.46 = (bf16[192,1024]{1,0:T(8,128)(2,1)}, bf16[192,1024]{1,0:T(8,128)(2,1)}, u32[]{:S(2)}, u32[]{:S(2)}) collective-permute-start(bf16[192,1024]{1,0:T(8,128)(2,1)} %get-tuple-element.142), channel_id=1, source_target_pairs={{0,16},{1,17},{2,18},{3,19},{4,20},{5,21},{6,22},{7,23},{8,24},{9,... | collective-permute-start | bytes 1179656 | tf_op jit(solution)/shard_map/ppermute | solution.py:534
  467.9 45.8 %collective-permute-start.45 = (bf16[96,3072]{1,0:T(8,128)(2,1)}, bf16[96,3072]{1,0:T(8,128)(2,1)}, u32[]{:S(2)}, u32[]{:S(2)}) collective-permute-start(bf16[96,3072]{1,0:T(8,128)(2,1)} %get-tuple-element.141), channel_id=1, source_target_pairs={{0,8},{1,9},{2,10},{3,11},{4,12},{5,13},{6,14},{7,15},{8,0},{9,1},... | collective-permute-start | bytes 1769480 | tf_op jit(solution)/shard_map/ppermute | solution.py:534
  511.1 38.3 %collective-permute-start.43 = (bf16[384,1536]{1,0:T(8,128)(2,1)}, bf16[384,1536]{1,0:T(8,128)(2,1)}, u32[]{:S(2)}, u32[]{:S(2)}) collective-permute-start(bf16[384,1536]{1,0:T(8,128)(2,1)} %shard_map.241.refs_2_), channel_id=1, source_target_pairs={{0,2},{1,3},{2,0},{3,1},{4,6},{5,7},{6,4},{7,5},{8,10},{9,11},{10,... | collective-permute-start | bytes 3538952 | tf_op jit(solution)/shard_map/ppermute | solution.py:534
  517.7 31.7 %collective-permute-start.42 = (bf16[384,1536]{1,0:T(8,128)(2,1)}, bf16[384,1536]{1,0:T(8,128)(2,1)}, u32[]{:S(2)}, u32[]{:S(2)}) collective-permute-start(bf16[384,1536]{1,0:T(8,128)(2,1)} %get-tuple-element.139), channel_id=1, source_target_pairs={{0,1},{1,0},{2,3},{3,2},{4,5},{5,4},{6,7},{7,6},{8,9},{9,8},{10,11... | collective-permute-start | bytes 3538952 | tf_op jit(solution)/shard_map/ppermute | solution.py:534
  (67 other events, 807.8 us)
